TPU v7x, 512 devices: a whole 4x8x8 slice. The times are simulated.
512 devices in a mesh: row: 32 (over x, z), col: 16 (over y, core).
Axes of the slice: x: 4, y: 8, z: 8, core: 2. Of those that a mesh axis runs over, the one named last changes fastest.
Arguments:
- vectors: float32 [65536, 2048], P('row', 'col'), may hold values from -6 to 6
- reflectors: float32 [65536, 256], P('row'), may hold values from -0.09375 to 0.09375
- panel_factor: float32 [256, 256], replicated, as said below
- station_rows: int32 [512, 4], replicated, may hold values from 0 to 65535
- station_weights: float32 [512, 4], replicated, may hold values from -3 to 3
- event_rows: int32 [8, 4], replicated, may hold values from 0 to 65535
- event_weights: float32 [8, 4], replicated, may hold values from -3 to 3
- mode_freq: float32 [2048], P('col'), may hold values from 0.05 to 1.5
- mode_damp: float32 [2048], P('col'), may hold values from 0.0001 to 0.005
Outputs:
- rotated: float32 [65536, 2048], P('row', 'col')
- seismograms: float32 [8, 512, 1024], P(None, 'row', 'col')
Inputs may be any that keep to these rules, and one draw needn't show every extreme that they name: panel_factor is upper triangular with a positive diagonal.
All inputs are finite; a program needn't handle non-finite values.
Results may differ from a plain program's by a relative error of at most 0.0003.
Values sent between devices are 32-bit elements; how exact they have to be, the bound alone decides.
No kernel may reach another device: no remote copies, remote signals or barrier semaphores. Data moves between devices by JAX's collectives and lax.ppermute only.
A program may use at most 64 MiB of HBM per device.

v0:
```python
import jax
import jax.numpy as jnp
from jax import lax
from jax.sharding import PartitionSpec as P

NMODE = 2048
NT = 1024


def tap_sum(field, rows, weights, first, rows_here):
    local = rows - first
    inside = (local >= 0) & (local < rows_here)
    picked = jnp.take(field, jnp.clip(local, 0, rows_here - 1), axis=0)
    scaled = jnp.where(inside, weights, 0.0)
    return jnp.sum(picked * scaled[:, :, None], axis=1)


def mode_basis(freq, damp, times):
    return jnp.exp(-damp[:, None] * times[None, :]) * jnp.cos(freq[:, None] * times[None, :])


def shards(
    vectors,
    reflectors,
    panel_factor,
    station_rows,
    station_weights,
    event_rows,
    event_weights,
    mode_freq,
    mode_damp,
):
    high = lax.Precision.HIGHEST
    rows_here = vectors.shape[0]
    first = lax.axis_index("row") * rows_here
    comp_here = station_rows.shape[0] // lax.axis_size("row")
    events = event_rows.shape[0]
    partial_panel = jnp.dot(
        reflectors.T, vectors, precision=high, preferred_element_type=jnp.float32
    )
    panel = lax.psum(partial_panel, "row")
    folded = jnp.dot(panel_factor, panel, precision=high, preferred_element_type=jnp.float32)
    rotated = vectors - jnp.dot(
        reflectors, folded, precision=high, preferred_element_type=jnp.float32
    )
    receivers = lax.psum_scatter(
        tap_sum(rotated, station_rows, station_weights, first, rows_here),
        "row",
        scatter_dimension=0,
        tiled=True,
    )
    sources = lax.psum(tap_sum(rotated, event_rows, event_weights, first, rows_here), "row")
    factor = 1.0 / float(NMODE) ** 0.5
    times = jnp.arange(NT).astype(jnp.float32)
    basis = mode_basis(mode_freq, mode_damp, times)
    amplitude = (sources[:, None, :] * receivers[None, :, :]).reshape(events * comp_here, -1)
    partial_series = jnp.dot(
        amplitude, basis, precision=high, preferred_element_type=jnp.float32
    ).reshape(events, comp_here, NT)
    seismograms = lax.psum_scatter(partial_series, "col", scatter_dimension=2, tiled=True) * factor
    return (rotated, seismograms)


def solution(mesh):
    placed = (P("row", "col"), P("row", None), P(), P(), P(), P(), P(), P("col"), P("col"))
    return jax.shard_map(
        shards,
        mesh=mesh,
        in_specs=placed,
        out_specs=(P("row", "col"), P(None, "row", "col")),
        check_vma=False,
    )
```

profile of v0, /device:TPU:1, one launch (start us, length us, event | category | flops | bytes accessed | tf_op | source)
XLA Modules:
  0.0 481.5 jit_solution(2186342622419786504)
XLA Ops:
  7.3 1.5 copy-done
  8.8 5.3 %fusion.14 = f32[256,128]{1,0:T(8,128)} fusion(f32[2048,256]{1,0:T(8,128)S(1)} %copy-done, f32[2048,128]{1,0:T(8,128)} %param.9), kind=kOutput, calls=%fused_computation.29 | convolution fusion | flops 805306368 | bytes 3276800 | tf_op jit(solution)/shard_map/dot_general | solution.py:38
  14.1 1.3 copy.30
  15.6 0.2 copy.35
  15.8 0.1 copy.38
  16.0 0.9 copy.36
  16.8 1.1 reshape.40
  17.9 149.8 %all-reduce.2.cloned.1.call-done = f32[256,128]{1,0:T(8,128)} async-done(((f32[256,128]{1,0:T(8,128)}), f32[256,128]{1,0:T(8,128)}) %all-reduce.2.cloned.1.call-update) | async-done | bytes 131088 | tf_op jit(solution)/shard_map/psum | solution.py:41
  167.7 1.4 fusion.15
  169.1 3.2 fusion
  172.4 1.5 copy.39
  173.9 7.6 %gather_fusion.1 = f32[2048,128]{1,0:T(8,128)} fusion(f32[2048,128]{1,0:T(8,128)S(1)} %copy.39, s32[2048]{0:T(1024)S(1)} %broadcast_clamp_fusion), kind=kCustom, calls=%fused_computation.1 | custom fusion | bytes 2105344 | tf_op jit(solution)/shard_map/jit(_take)/gather | solution.py:13
  181.5 4.8 multiply_reduce_fusion
  186.4 0.1 copy.31
  186.6 0.6 gather_fusion
  187.3 58.7 %psum.15 = f32[8,128]{1,0:T(8,128)S(1)} all-reduce(f32[8,128]{1,0:T(8,128)S(1)} %multiply_reduce_fusion.1), channel_id=1, replica_groups=mesh['row'=32,'col'=16] {'row'}, use_global_device_ids=true, to_apply=%region_2.3 | all-reduce | flops 1024 | bytes 8192 | tf_op jit(solution)/shard_map/psum | solution.py:52
  246.0 157.3 %reduce-scatter.5.cloned.1.call-done = f32[16,128]{1,0:T(8,128)} async-done(((f32[512,128]{1,0:T(8,128)}), f32[16,128]{1,0:T(8,128)}) %reduce-scatter.5.cloned.1.call-update) | async-done | bytes 8208 | tf_op jit(solution)/shard_map/reduce_scatter | solution.py:46
  403.3 3.1 fusion.1
  406.4 2.6 copy.40
  409.0 3.9 reshape.51
  413.0 60.3 %reduce-scatter.7.cloned.1.call-done = f32[64,128]{1,0:T(8,128)} async-done(((f32[1024,128]{1,0:T(8,128)}), f32[64,128]{1,0:T(8,128)}) %reduce-scatter.7.cloned.1.call-update) | async-done | bytes 32784
  473.3 0.9 reshape.52
  474.2 0.1 copy.41
  474.3 0.7 broadcast_multiply_fusion
  (37 shorter events, 0.6 us)
Async XLA Ops:
  7.2 1.6 copy-start
  7.2 7.0 %copy-start.2 = (f32[2048,128]{1,0:T(8,128)S(1)}, f32[2048,128]{1,0:T(8,128)}, u32[]{:S(2)}) copy-start(f32[2048,128]{1,0:T(8,128)} %param.9) | copy-start | bytes 3145732
  7.2 8.3 %copy-start.8 = (f32[128]{0:T(128)S(1)}, f32[128]{0:T(128)}, u32[]{:S(2)}) copy-start(f32[128]{0:T(128)} %param.17) | copy-start | bytes 1540
  7.2 8.3 %copy-start.6 = (s32[8,4]{0,1:T(4,128)S(1)}, s32[8,4]{0,1:T(4,128)}, u32[]{:S(2)}) copy-start(s32[8,4]{0,1:T(4,128)} %param.14) | copy-start | bytes 388
  7.2 8.3 %copy-start.7 = (f32[8,4]{0,1:T(4,128)S(1)}, f32[8,4]{0,1:T(4,128)}, u32[]{:S(2)}) copy-start(f32[8,4]{0,1:T(4,128)} %param.15) | copy-start | bytes 388
  7.2 8.4 %copy-start.4 = (s32[512,4]{0,1:T(4,128)S(1)}, s32[512,4]{0,1:T(4,128)}, u32[]{:S(2)}) copy-start(s32[512,4]{0,1:T(4,128)} %param.12) | copy-start | bytes 24580
  7.2 8.4 %copy-start.5 = (f32[512,4]{0,1:T(4,128)S(1)}, f32[512,4]{0,1:T(4,128)}, u32[]{:S(2)}) copy-start(f32[512,4]{0,1:T(4,128)} %param.13) | copy-start | bytes 24580
  7.2 160.5 %all-reduce.2.cloned.1.call-start = ((), (), s32[]{:S(2)}) async-start(), calls=%async_computation.2 | async-start | bytes 262144 | tf_op jit(solution)/shard_map/psum | solution.py:41
  14.1 389.3 %reduce-scatter.5.cloned.1.call-start = ((), (), s32[]{:S(2)}) async-start(), calls=%async_computation.3 | async-start | bytes 270336 | tf_op jit(solution)/shard_map/reduce_scatter | solution.py:46
  15.5 153.7 %copy-start.3 = (f32[2048,128]{0,1:T(8,128)S(1)}, f32[2048,128]{0,1:T(8,128)}, u32[]{:S(2)}) copy-start(f32[2048,128]{0,1:T(8,128)} %copy.30) | copy-start | bytes 3145732
  173.9 12.7 %copy-start.1 = (f32[2048,128]{1,0:T(8,128)}, f32[2048,128]{1,0:T(8,128)S(1)}, u32[]{:S(2)}) copy-start(f32[2048,128]{1,0:T(8,128)S(1)} %copy.39) | copy-start | bytes 3145732
  181.5 221.8 %copy-start.9 = (f32[128]{0:T(128)S(1)}, f32[128]{0:T(128)}, u32[]{:S(2)}) copy-start(f32[128]{0:T(128)} %param.16) | copy-start | bytes 1540
  186.3 287.0 %reduce-scatter.7.cloned.1.call-start = ((), (), s32[]{:S(2)}) async-start(), calls=%async_computation.4 | async-start | bytes 557056
Sparse Core Ops, SparseCore 0:
  14.2 153.4 all-reduce.1
  186.4 216.8 reduce-scatter.4
  413.1 60.1 reduce-scatter.6
where the time goes:
time: 483 us; the launch traced here: 481 us
  waiting for transfers between devices  367 us (76%)
  blocking collectives  58.7 us (12%)
  local copies, waits for them, and re-layouts  22.7 us (5%)
  between operations  13.9 us (3%)
  matrix products  13 us (3%)
  other arithmetic  5.58 us (1%)
    reduce_scatter x1, waiting for transfers between devices, shards(): lax.psum_scatter(tap_sum(rotated, station_rows, station_weights, first, r...  157 us
    psum x1, waiting for transfers between devices, shards(): panel = lax.psum(partial_panel, 'row')  150 us
    unnamed x4, waiting for transfers between devices  60.4 us
    psum x1, blocking collectives, shards(): lax.psum(tap_sum(rotated, event_rows, event_weights, first, rows_here), '...  58.7 us
    unnamed x26, local copies, waits for them, and re-layouts  11.9 us
  transfers between devices with their start and end apart: 3, of which 3 were waited for; matrix products, arithmetic and copies ran while one was open for 1% of the time, Pallas kernels for 0%

commit v1 on v0

v1 whole, which is shorter than its diff:
```python
import jax
import jax.numpy as jnp
from jax import lax
from jax.sharding import PartitionSpec as P

NT = 1024

ROW_BITS = (1, 8, 2, 16, 4)
COL_BITS = (8, 4, 2, 1)


def rounds(bits, n):
    return [bit for bit in bits if bit < n]


def swap(x, axis, n, bit):
    return lax.ppermute(x, axis, [(i, i ^ bit) for i in range(n)])


def all_reduce(x, axis, n, bits):
    for bit in rounds(bits, n):
        x = x + swap(x, axis, n, bit)
    return x


def all_gather(xs, axis, n, bits, dim):
    me = lax.axis_index(axis)
    for bit in rounds(bits, n):
        low = (me & bit) == 0
        others = [swap(x, axis, n, bit) for x in xs]
        xs = [
            jnp.where(low, jnp.concatenate([x, o], dim), jnp.concatenate([o, x], dim))
            for x, o in zip(xs, others)
        ]
    return xs


def reduce_scatter(x, extra, axis, n, bits):
    me = lax.axis_index(axis)
    levels = n.bit_length() - 1
    blk = x.shape[0] // n
    rest = x.shape[1:]
    order = [1 << (levels - 1 - k) for k in range(levels)]
    x = x.reshape([2] * levels + [blk] + list(rest))
    width = rest[-1]
    for bit in rounds(bits, n):
        k = order.index(bit)
        lo = lax.index_in_dim(x, 0, k, keepdims=False)
        hi = lax.index_in_dim(x, 1, k, keepdims=False)
        high = (me & bit) != 0
        keep = jnp.where(high, hi, lo)
        send = jnp.where(high, lo, hi)
        packed = jnp.concatenate([send.reshape(-1, width), extra.reshape(-1, width)], 0)
        got = swap(packed, axis, n, bit)
        cut = send.size // width
        x = keep + got[:cut].reshape(send.shape)
        extra = extra + got[cut:].reshape(extra.shape)
        order.pop(k)
    return x.reshape([blk] + list(rest)), extra


def tap_sum(field, rows, weights, first, rows_here):
    local = rows - first
    inside = (local >= 0) & (local < rows_here)
    picked = jnp.take(field, jnp.clip(local, 0, rows_here - 1), axis=0)
    scaled = jnp.where(inside, weights, 0.0)
    return jnp.sum(picked * scaled[:, :, None], axis=1)


def mode_basis(freq, damp, times):
    return jnp.exp(-damp[:, None] * times[None, :]) * jnp.cos(freq[:, None] * times[None, :])


def shards(
    vectors,
    reflectors,
    panel_factor,
    station_rows,
    station_weights,
    event_rows,
    event_weights,
    mode_freq,
    mode_damp,
):
    high = lax.Precision.HIGHEST
    nrow = lax.axis_size("row")
    ncol = lax.axis_size("col")
    rows_here = vectors.shape[0]
    first = lax.axis_index("row") * rows_here
    comp_here = station_rows.shape[0] // nrow
    events = event_rows.shape[0]
    samples = NT // ncol

    freq, damp = all_gather([mode_freq, mode_damp], "col", ncol, COL_BITS, 0)
    times = (lax.axis_index("col") * samples + jnp.arange(samples)).astype(jnp.float32)
    basis = mode_basis(freq, damp, times)

    partial_panel = jnp.dot(
        reflectors.T, vectors, precision=high, preferred_element_type=jnp.float32
    )
    panel = all_reduce(partial_panel, "row", nrow, ROW_BITS)
    folded = jnp.dot(panel_factor, panel, precision=high, preferred_element_type=jnp.float32)
    rotated = vectors - jnp.dot(
        reflectors, folded, precision=high, preferred_element_type=jnp.float32
    )
    receivers, sources = reduce_scatter(
        tap_sum(rotated, station_rows, station_weights, first, rows_here),
        tap_sum(rotated, event_rows, event_weights, first, rows_here),
        "row",
        nrow,
        ROW_BITS,
    )
    receivers, sources = all_gather([receivers, sources], "col", ncol, COL_BITS, 1)
    factor = 1.0 / float(mode_freq.shape[0] * ncol) ** 0.5
    amplitude = (sources[:, None, :] * receivers[None, :, :]).reshape(events * comp_here, -1)
    series = jnp.dot(amplitude, basis, precision=high, preferred_element_type=jnp.float32)
    seismograms = series.reshape(events, comp_here, samples) * factor
    return (rotated, seismograms)


def solution(mesh):
    placed = (P("row", "col"), P("row", None), P(), P(), P(), P(), P(), P("col"), P("col"))
    return jax.shard_map(
        shards,
        mesh=mesh,
        in_specs=placed,
        out_specs=(P("row", "col"), P(None, "row", "col")),
        check_vma=False,
    )
```

time: 483 us -> 167 us (0.35)
  waiting for transfers between devices: 367 us -> 17.1 us
  starting transfers between devices: 0.12 us -> 103 us
  blocking collectives: 58.7 us -> 0 us
  between operations: 13.9 us -> 1.39 us
  other arithmetic: 5.58 us -> 13.6 us
  local copies, waits for them, and re-layouts: 22.7 us -> 17.8 us
    reduce_scatter x1 -> x0, waiting for transfers between devices: 157 us -> none  [shards(): lax.psum_scatter(tap_sum(rotated, station_rows, station_weights, first, r...]
    psum x1 -> x0, waiting for transfers between devices: 150 us -> none  [shards(): panel = lax.psum(partial_panel, 'row')]
    ppermute x0 -> x26, starting transfers between devices: none -> 103 us  [swap(): return lax.ppermute(x, axis, [(i, i ^ bit) for i in range(n)])]
    unnamed x4 -> x0, waiting for transfers between devices: 60.4 us -> none
    psum x1 -> x0, blocking collectives: 58.7 us -> none  [shards(): lax.psum(tap_sum(rotated, event_rows, event_weights, first, rows_here), '...]
    ppermute x0 -> x26, waiting for transfers between devices: none -> 17.1 us  [swap(): return lax.ppermute(x, axis, [(i, i ^ bit) for i in range(n)])]
    unnamed x26 -> x20, local copies, waits for them, and re-layouts: 11.9 us -> 4.48 us
  transfers between devices with their start and end apart: 3 -> 26, of which waited for: 3 -> 7; matrix products, arithmetic and copies ran while one was open for 1% -> 21% of each run, Pallas kernels for 0% -> 0%
where the time goes in v1:
time: 167 us; the launch traced here: 166 us
  starting transfers between devices  103 us (62%)
  local copies, waits for them, and re-layouts  17.8 us (11%)
  waiting for transfers between devices  17.1 us (10%)
  other arithmetic  13.6 us (8%)
  matrix products  12.7 us (8%)
    ppermute x26, starting transfers between devices, swap(): return lax.ppermute(x, axis, [(i, i ^ bit) for i in range(n)])  103 us
    ppermute x26, waiting for transfers between devices, swap(): return lax.ppermute(x, axis, [(i, i ^ bit) for i in range(n)])  17.1 us
    gather x2, local copies, waits for them, and re-layouts, tap_sum(): picked = jnp.take(field, jnp.clip(local, 0, rows_here - 1), axis=0)  8.13 us
    dot_general x1, matrix products, shards(): jnp.dot(reflectors.T, vectors, precision=high, preferred_element_type=jnp...  4.64 us
    unnamed x20, local copies, waits for them, and re-layouts  4.48 us
    reduce_sum x2, other arithmetic, tap_sum(): return jnp.sum(picked * scaled[:, :, None], axis=1)  4.18 us
    dot_general x1, matrix products, shards(): jnp.dot(amplitude, basis, precision=high, preferred_element_type=jnp.floa...  3.48 us
  transfers between devices with their start and end apart: 26, of which 7 were waited for; matrix products, arithmetic and copies ran while one was open for 21% of the time, Pallas kernels for 0%

profile of v1, /device:TPU:1, one launch (start us, length us, event | category | flops | bytes accessed | tf_op | source)
XLA Modules:
  0.0 165.7 jit_solution(16256910991490898434)
XLA Ops:
  2.2 4.6 %fusion.16 = f32[256,128]{1,0:T(8,128)S(1)} fusion(f32[2048,256]{1,0:T(8,128)S(1)} %copy-done, f32[2048,128]{1,0:T(8,128)} %param.9), kind=kOutput, calls=%fused_computation.67 | convolution fusion | flops 805306368 | bytes 3276800 | tf_op jit(solution)/shard_map/dot_general | solution.py:98
  6.9 4.8 %collective-permute-start = (f32[256,128]{1,0:T(8,128)S(1)}, f32[256,128]{1,0:T(8,128)}, u32[]{:S(2)}, u32[]{:S(2)}) collective-permute-start(f32[256,128]{1,0:T(8,128)S(1)} %fusion.16), channel_id=1, source_target_pairs={{0,16},{16,0},{32,48},{48,32},{64,80},{80,64},{96,112},{112,96},{1... | collective-permute-start | bytes 393224 | tf_op jit(solution)/shard_map/ppermute | solution.py:17
  11.7 7.5 %collective-permute-start.18 = (f32[128]{0:T(128)}, f32[128]{0:T(128)}, u32[]{:S(2)}, u32[]{:S(2)}) collective-permute-start(f32[128]{0:T(128)} %param.17), channel_id=1, source_target_pairs={{0,8},{1,9},{2,10},{3,11},{4,12},{5,13},{6,14},{7,15},{8,0},{9,1},... | collective-permute-start | bytes 1544 | tf_op jit(solution)/shard_map/ppermute | solution.py:17
  25.0 3.1 %collective-permute-start.1 = (f32[256,128]{1,0:T(8,128)S(1)}, f32[256,128]{1,0:T(8,128)S(1)}, u32[]{:S(2)}, u32[]{:S(2)}) collective-permute-start(f32[256,128]{1,0:T(8,128)S(1)} %add.71), channel_id=1, source_target_pairs={{0,128},{16,144},{32,160},{48,176},{64,192},{80,208},{96,224},{112... | collective-permute-start | bytes 393224 | tf_op jit(solution)/shard_map/ppermute | solution.py:17
  30.7 5.8 %collective-permute-start.2 = (f32[256,128]{1,0:T(8,128)S(1)}, f32[256,128]{1,0:T(8,128)S(1)}, u32[]{:S(2)}, u32[]{:S(2)}) collective-permute-start(f32[256,128]{1,0:T(8,128)S(1)} %add.72), channel_id=1, source_target_pairs={{0,32},{16,48},{32,0},{48,16},{64,96},{80,112},{96,64},{112,80},{1... | collective-permute-start | bytes 393224 | tf_op jit(solution)/shard_map/ppermute | solution.py:17
  40.0 6.6 %collective-permute-start.3 = (f32[256,128]{1,0:T(8,128)S(1)}, f32[256,128]{1,0:T(8,128)}, u32[]{:S(2)}, u32[]{:S(2)}) collective-permute-start(f32[256,128]{1,0:T(8,128)S(1)} %add.73), channel_id=1, source_target_pairs={{0,256},{16,272},{32,288},{48,304},{64,320},{80,336},{96,352},{112... | collective-permute-start | bytes 393224 | tf_op jit(solution)/shard_map/ppermute | solution.py:17
  54.4 6.5 %collective-permute-start.4 = (f32[256,128]{1,0:T(8,128)S(1)}, f32[256,128]{1,0:T(8,128)S(1)}, u32[]{:S(2)}, u32[]{:S(2)}) collective-permute-start(f32[256,128]{1,0:T(8,128)S(1)} %add.74), channel_id=1, source_target_pairs={{0,64},{16,80},{32,96},{48,112},{64,0},{80,16},{96,32},{112,48},{1... | collective-permute-start | bytes 393224 | tf_op jit(solution)/shard_map/ppermute | solution.py:17
  61.7 4.0 %collective-permute-start.19 = (f32[256]{0:T(256)S(1)}, f32[256]{0:T(256)S(1)}, u32[]{:S(2)}, u32[]{:S(2)}) collective-permute-start(f32[256]{0:T(256)S(1)} %maximum_select_fusion.14), channel_id=1, source_target_pairs={{0,4},{1,5},{2,6},{3,7},{4,0},{5,1},{6,2},{7,3},{8,12},{9,13},{10,... | collective-permute-start | bytes 3080 | tf_op jit(solution)/shard_map/ppermute | solution.py:17
  70.0 3.2 %fusion = f32[2048,128]{0,1:T(8,128)} fusion(f32[2048,128]{0,1:T(8,128)S(1)} %copy-done.3, f32[128,256]{1,0:T(8,128)S(1)} %fusion.13, f32[2048,256]{1,0:T(8,128)S(1)} %copy-done), kind=kOutput, calls=%fused_computation.3 | convolution fusion | flops 805568512 | bytes 4325376 | tf_op jit(solution)/shard_map/dot_general | solution.py:103
  74.8 7.6 %gather_fusion.1 = f32[2048,128]{1,0:T(8,128)} fusion(f32[2048,128]{1,0:T(8,128)S(1)} %copy.33, s32[2048]{0:T(1024)S(1)} %broadcast_clamp_fusion), kind=kCustom, calls=%fused_computation.1 | custom fusion | bytes 2105344 | tf_op jit(solution)/shard_map/jit(_take)/gather | solution.py:65
  83.0 4.1 %multiply_reduce_fusion = f32[512,128]{1,0:T(8,128)S(1)} fusion(f32[512,4,128]{2,1,0:T(4,128)} %bitcast.35, f32[512,4]{1,0:T(8,128)S(1)} %copy.32, pred[512,4]{1,0:T(8,128)(4,1)S(1)} %copy-done.4), kind=kLoop, calls=%fused_computation.6 | loop fusion | flops 720896 | bytes 1320960 | tf_op jit(solution)/shard_map/reduce_sum | solution.py:67
  89.2 3.0 %collective-permute-start.20 = (f32[512]{0:T(512)S(1)}, f32[512]{0:T(512)S(1)}, u32[]{:S(2)}, u32[]{:S(2)}) collective-permute-start(f32[512]{0:T(512)S(1)} %maximum_select_fusion.12), channel_id=1, source_target_pairs={{0,2},{1,3},{2,0},{3,1},{4,6},{5,7},{6,4},{7,5},{8,10},{9,11},{10,... | collective-permute-start | bytes 6152 | tf_op jit(solution)/shard_map/ppermute | solution.py:17
  96.9 7.5 %collective-permute-start.21 = (f32[1024]{0:T(1024)S(1)}, f32[1024]{0:T(1024)S(1)}, u32[]{:S(2)}, u32[]{:S(2)}) collective-permute-start(f32[1024]{0:T(1024)S(1)} %maximum_select_fusion.10), channel_id=1, source_target_pairs={{0,1},{1,0},{2,3},{3,2},{4,5},{5,4},{6,7},{7,6},{8,9},{9,8},{10,11... | collective-permute-start | bytes 12296 | tf_op jit(solution)/shard_map/ppermute | solution.py:17
  104.5 4.6 %collective-permute-start.7 = (f32[72,128]{1,0:T(8,128)S(1)}, f32[72,128]{1,0:T(8,128)S(1)}, u32[]{:S(2)}, u32[]{:S(2)}) collective-permute-start(f32[72,128]{1,0:T(8,128)S(1)} %pad_maximum_fusion.2), channel_id=1, source_target_pairs={{0,32},{16,48},{32,0},{48,16},{64,96},{80,112},{96,64},{112,80},{1... | collective-permute-start | bytes 110600 | tf_op jit(solution)/shard_map/ppermute | solution.py:17
  109.1 3.9 %collective-permute-start.25 = (f32[1024]{0:T(1024)S(1)}, f32[1024]{0:T(1024)S(1)}, u32[]{:S(2)}, u32[]{:S(2)}) collective-permute-start(f32[1024]{0:T(1024)S(1)} %maximum_select_fusion.11), channel_id=1, source_target_pairs={{0,1},{1,0},{2,3},{3,2},{4,5},{5,4},{6,7},{7,6},{8,9},{9,8},{10,11... | collective-permute-start | bytes 12296 | tf_op jit(solution)/shard_map/ppermute | solution.py:17
  115.3 3.8 %collective-permute-done.8 = f32[40,128]{1,0:T(8,128)S(1)} collective-permute-done((f32[40,128]{1,0:T(8,128)S(1)}, f32[40,128]{1,0:T(8,128)S(1)}, u32[]{:S(2)}, u32[]{:S(2)}) %collective-permute-start.8) | collective-permute-done | bytes 20512 | tf_op jit(solution)/shard_map/ppermute | solution.py:17
  121.4 6.1 %collective-permute-done.9 = f32[24,128]{1,0:T(8,128)S(1)} collective-permute-done((f32[24,128]{1,0:T(8,128)S(1)}, f32[24,128]{1,0:T(8,128)S(1)}, u32[]{:S(2)}, u32[]{:S(2)}) %collective-permute-start.9) | collective-permute-done | bytes 12320 | tf_op jit(solution)/shard_map/ppermute | solution.py:17
  127.5 7.4 %collective-permute-start.10 = (f32[8,128]{1,0:T(8,128)S(1)}, f32[8,128]{1,0:T(8,128)S(1)}, u32[]{:S(2)}, u32[]{:S(2)}) collective-permute-start(f32[8,128]{1,0:T(8,128)S(1)} %slice_add_fusion.1), channel_id=1, source_target_pairs={{0,8},{1,9},{2,10},{3,11},{4,12},{5,13},{6,14},{7,15},{8,0},{9,1},... | collective-permute-start | bytes 12296 | tf_op jit(solution)/shard_map/ppermute | solution.py:17
  136.9 4.0 %collective-permute-start.11 = (f32[8,256]{1,0:T(8,128)S(1)}, f32[8,256]{1,0:T(8,128)S(1)}, u32[]{:S(2)}, u32[]{:S(2)}) collective-permute-start(f32[8,256]{1,0:T(8,128)S(1)} %maximum_select_fusion.7), channel_id=1, source_target_pairs={{0,4},{1,5},{2,6},{3,7},{4,0},{5,1},{6,2},{7,3},{8,12},{9,13},{10,... | collective-permute-start | bytes 24584 | tf_op jit(solution)/shard_map/ppermute | solution.py:17
  143.3 2.4 %collective-permute-start.15 = (f32[16,256]{1,0:T(8,128)S(1)}, f32[16,256]{1,0:T(8,128)S(1)}, u32[]{:S(2)}, u32[]{:S(2)}) collective-permute-start(f32[16,256]{1,0:T(8,128)S(1)} %maximum_select_fusion.6), channel_id=1, source_target_pairs={{0,4},{1,5},{2,6},{3,7},{4,0},{5,1},{6,2},{7,3},{8,12},{9,13},{10,... | collective-permute-start | bytes 49160 | tf_op jit(solution)/shard_map/ppermute | solution.py:17
  148.7 2.4 %collective-permute-start.16 = (f32[16,512]{1,0:T(8,128)S(1)}, f32[16,512]{1,0:T(8,128)S(1)}, u32[]{:S(2)}, u32[]{:S(2)}) collective-permute-start(f32[16,512]{1,0:T(8,128)S(1)} %maximum_select_fusion.4), channel_id=1, source_target_pairs={{0,2},{1,3},{2,0},{3,1},{4,6},{5,7},{6,4},{7,5},{8,10},{9,11},{10,... | collective-permute-start | bytes 98312 | tf_op jit(solution)/shard_map/ppermute | solution.py:17
  151.1 7.0 %collective-permute-start.13 = (f32[8,1024]{1,0:T(8,128)S(1)}, f32[8,1024]{1,0:T(8,128)S(1)}, u32[]{:S(2)}, u32[]{:S(2)}) collective-permute-start(f32[8,1024]{1,0:T(8,128)S(1)} %maximum_select_fusion.3), channel_id=1, source_target_pairs={{0,1},{1,0},{2,3},{3,2},{4,5},{5,4},{6,7},{7,6},{8,9},{9,8},{10,11... | collective-permute-start | bytes 98312 | tf_op jit(solution)/shard_map/ppermute | solution.py:17
  158.2 3.3 %collective-permute-start.17 = (f32[16,1024]{1,0:T(8,128)S(1)}, f32[16,1024]{1,0:T(8,128)S(1)}, u32[]{:S(2)}, u32[]{:S(2)}) collective-permute-start(f32[16,1024]{1,0:T(8,128)S(1)} %maximum_select_fusion.2), channel_id=1, source_target_pairs={{0,1},{1,0},{2,3},{3,2},{4,5},{5,4},{6,7},{7,6},{8,9},{9,8},{10,11... | collective-permute-start | bytes 196616 | tf_op jit(solution)/shard_map/ppermute | solution.py:17
  162.2 3.5 %convolution_multiply_fusion = f32[8,16,64]{2,1,0:T(8,128)} fusion(f32[16,2048]{1,0:T(8,128)S(1)} %maximum_select_fusion, f32[8,2048]{1,0:T(8,128)S(1)} %maximum_select_fusion.1, f32[2048]{0:T(1024)S(1)} %maximum_select_fusion.9, f32[64]{0:T(128)S(1)} %copy-done.8, f32[2048]{0:T(1024)S(1)} %fusion.15), kind=kOutput, calls=%fused_computation.4 | convolution fusion | flops 201990144 | bytes 246016 | tf_op jit(solution)/shard_map/dot_general | solution.py:116
  (115 shorter events, 47.4 us)
Async XLA Ops:
  6.9 17.2 %collective-permute-start = (f32[256,128]{1,0:T(8,128)S(1)}, f32[256,128]{1,0:T(8,128)}, u32[]{:S(2)}, u32[]{:S(2)}) collective-permute-start(f32[256,128]{1,0:T(8,128)S(1)} %fusion.16), channel_id=1, source_target_pairs={{0,16},{16,0},{32,48},{48,32},{64,80},{80,64},{96,112},{112,96},{1... | collective-permute-start | bytes 393224 | tf_op jit(solution)/shard_map/ppermute | solution.py:17
  11.7 49.2 %collective-permute-start.18 = (f32[128]{0:T(128)}, f32[128]{0:T(128)}, u32[]{:S(2)}, u32[]{:S(2)}) collective-permute-start(f32[128]{0:T(128)} %param.17), channel_id=1, source_target_pairs={{0,8},{1,9},{2,10},{3,11},{4,12},{5,13},{6,14},{7,15},{8,0},{9,1},... | collective-permute-start | bytes 1544 | tf_op jit(solution)/shard_map/ppermute | solution.py:17
  19.2 46.5 %collective-permute-start.22 = (f32[128]{0:T(128)}, f32[128]{0:T(128)}, u32[]{:S(2)}, u32[]{:S(2)}) collective-permute-start(f32[128]{0:T(128)} %param.16), channel_id=1, source_target_pairs={{0,8},{1,9},{2,10},{3,11},{4,12},{5,13},{6,14},{7,15},{8,0},{9,1},... | collective-permute-start | bytes 1544 | tf_op jit(solution)/shard_map/ppermute | solution.py:17
  25.0 5.7 %collective-permute-start.1 = (f32[256,128]{1,0:T(8,128)S(1)}, f32[256,128]{1,0:T(8,128)S(1)}, u32[]{:S(2)}, u32[]{:S(2)}) collective-permute-start(f32[256,128]{1,0:T(8,128)S(1)} %add.71), channel_id=1, source_target_pairs={{0,128},{16,144},{32,160},{48,176},{64,192},{80,208},{96,224},{112... | collective-permute-start | bytes 393224 | tf_op jit(solution)/shard_map/ppermute | solution.py:17
  30.7 9.3 %collective-permute-start.2 = (f32[256,128]{1,0:T(8,128)S(1)}, f32[256,128]{1,0:T(8,128)S(1)}, u32[]{:S(2)}, u32[]{:S(2)}) collective-permute-start(f32[256,128]{1,0:T(8,128)S(1)} %add.72), channel_id=1, source_target_pairs={{0,32},{16,48},{32,0},{48,16},{64,96},{80,112},{96,64},{112,80},{1... | collective-permute-start | bytes 393224 | tf_op jit(solution)/shard_map/ppermute | solution.py:17
  40.0 13.5 %collective-permute-start.3 = (f32[256,128]{1,0:T(8,128)S(1)}, f32[256,128]{1,0:T(8,128)}, u32[]{:S(2)}, u32[]{:S(2)}) collective-permute-start(f32[256,128]{1,0:T(8,128)S(1)} %add.73), channel_id=1, source_target_pairs={{0,256},{16,272},{32,288},{48,304},{64,320},{80,336},{96,352},{112... | collective-permute-start | bytes 393224 | tf_op jit(solution)/shard_map/ppermute | solution.py:17
  54.4 14.2 %collective-permute-start.4 = (f32[256,128]{1,0:T(8,128)S(1)}, f32[256,128]{1,0:T(8,128)S(1)}, u32[]{:S(2)}, u32[]{:S(2)}) collective-permute-start(f32[256,128]{1,0:T(8,128)S(1)} %add.74), channel_id=1, source_target_pairs={{0,64},{16,80},{32,96},{48,112},{64,0},{80,16},{96,32},{112,48},{1... | collective-permute-start | bytes 393224 | tf_op jit(solution)/shard_map/ppermute | solution.py:17
  61.7 27.5 %collective-permute-start.19 = (f32[256]{0:T(256)S(1)}, f32[256]{0:T(256)S(1)}, u32[]{:S(2)}, u32[]{:S(2)}) collective-permute-start(f32[256]{0:T(256)S(1)} %maximum_select_fusion.14), channel_id=1, source_target_pairs={{0,4},{1,5},{2,6},{3,7},{4,0},{5,1},{6,2},{7,3},{8,12},{9,13},{10,... | collective-permute-start | bytes 3080 | tf_op jit(solution)/shard_map/ppermute | solution.py:17
  66.5 25.7 %collective-permute-start.23 = (f32[256]{0:T(256)S(1)}, f32[256]{0:T(256)S(1)}, u32[]{:S(2)}, u32[]{:S(2)}) collective-permute-start(f32[256]{0:T(256)S(1)} %maximum_select_fusion.15), channel_id=1, source_target_pairs={{0,4},{1,5},{2,6},{3,7},{4,0},{5,1},{6,2},{7,3},{8,12},{9,13},{10,... | collective-permute-start | bytes 3080 | tf_op jit(solution)/shard_map/ppermute | solution.py:17
  87.2 7.3 %collective-permute-start.5 = (f32[264,128]{1,0:T(8,128)S(1)}, f32[264,128]{1,0:T(8,128)S(1)}, u32[]{:S(2)}, u32[]{:S(2)}) collective-permute-start(f32[264,128]{1,0:T(8,128)S(1)} %pad_maximum_fusion), channel_id=1, source_target_pairs={{0,16},{16,0},{32,48},{48,32},{64,80},{80,64},{96,112},{112,96},{1... | collective-permute-start | bytes 405512 | tf_op jit(solution)/shard_map/ppermute | solution.py:17
  89.2 7.7 %collective-permute-start.20 = (f32[512]{0:T(512)S(1)}, f32[512]{0:T(512)S(1)}, u32[]{:S(2)}, u32[]{:S(2)}) collective-permute-start(f32[512]{0:T(512)S(1)} %maximum_select_fusion.12), channel_id=1, source_target_pairs={{0,2},{1,3},{2,0},{3,1},{4,6},{5,7},{6,4},{7,5},{8,10},{9,11},{10,... | collective-permute-start | bytes 6152 | tf_op jit(solution)/shard_map/ppermute | solution.py:17
  92.2 16.8 %collective-permute-start.24 = (f32[512]{0:T(512)S(1)}, f32[512]{0:T(512)S(1)}, u32[]{:S(2)}, u32[]{:S(2)}) collective-permute-start(f32[512]{0:T(512)S(1)} %maximum_select_fusion.13), channel_id=1, source_target_pairs={{0,2},{1,3},{2,0},{3,1},{4,6},{5,7},{6,4},{7,5},{8,10},{9,11},{10,... | collective-permute-start | bytes 6152 | tf_op jit(solution)/shard_map/ppermute | solution.py:17
  94.6 9.8 %collective-permute-start.6 = (f32[136,128]{1,0:T(8,128)S(1)}, f32[136,128]{1,0:T(8,128)S(1)}, u32[]{:S(2)}, u32[]{:S(2)}) collective-permute-start(f32[136,128]{1,0:T(8,128)S(1)} %pad_maximum_fusion.1), channel_id=1, source_target_pairs={{0,128},{16,144},{32,160},{48,176},{64,192},{80,208},{96,224},{112... | collective-permute-start | bytes 208904 | tf_op jit(solution)/shard_map/ppermute | solution.py:17
  96.9 18.4 %collective-permute-start.21 = (f32[1024]{0:T(1024)S(1)}, f32[1024]{0:T(1024)S(1)}, u32[]{:S(2)}, u32[]{:S(2)}) collective-permute-start(f32[1024]{0:T(1024)S(1)} %maximum_select_fusion.10), channel_id=1, source_target_pairs={{0,1},{1,0},{2,3},{3,2},{4,5},{5,4},{6,7},{7,6},{8,9},{9,8},{10,11... | collective-permute-start | bytes 12296 | tf_op jit(solution)/shard_map/ppermute | solution.py:17
  104.5 8.5 %collective-permute-start.7 = (f32[72,128]{1,0:T(8,128)S(1)}, f32[72,128]{1,0:T(8,128)S(1)}, u32[]{:S(2)}, u32[]{:S(2)}) collective-permute-start(f32[72,128]{1,0:T(8,128)S(1)} %pad_maximum_fusion.2), channel_id=1, source_target_pairs={{0,32},{16,48},{32,0},{48,16},{64,96},{80,112},{96,64},{112,80},{1... | collective-permute-start | bytes 110600 | tf_op jit(solution)/shard_map/ppermute | solution.py:17
  109.1 12.3 %collective-permute-start.25 = (f32[1024]{0:T(1024)S(1)}, f32[1024]{0:T(1024)S(1)}, u32[]{:S(2)}, u32[]{:S(2)}) collective-permute-start(f32[1024]{0:T(1024)S(1)} %maximum_select_fusion.11), channel_id=1, source_target_pairs={{0,1},{1,0},{2,3},{3,2},{4,5},{5,4},{6,7},{7,6},{8,9},{9,8},{10,11... | collective-permute-start | bytes 12296 | tf_op jit(solution)/shard_map/ppermute | solution.py:17
  113.1 6.0 %collective-permute-start.8 = (f32[40,128]{1,0:T(8,128)S(1)}, f32[40,128]{1,0:T(8,128)S(1)}, u32[]{:S(2)}, u32[]{:S(2)}) collective-permute-start(f32[40,128]{1,0:T(8,128)S(1)} %pad_maximum_fusion.3), channel_id=1, source_target_pairs={{0,256},{16,272},{32,288},{48,304},{64,320},{80,336},{96,352},{112... | collective-permute-start | bytes 61448 | tf_op jit(solution)/shard_map/ppermute | solution.py:17
  119.2 8.3 %collective-permute-start.9 = (f32[24,128]{1,0:T(8,128)S(1)}, f32[24,128]{1,0:T(8,128)S(1)}, u32[]{:S(2)}, u32[]{:S(2)}) collective-permute-start(f32[24,128]{1,0:T(8,128)S(1)} %pad_maximum_fusion.4), channel_id=1, source_target_pairs={{0,64},{16,80},{32,96},{48,112},{64,0},{80,16},{96,32},{112,48},{1... | collective-permute-start | bytes 36872 | tf_op jit(solution)/shard_map/ppermute | solution.py:17
  127.5 9.4 %collective-permute-start.10 = (f32[8,128]{1,0:T(8,128)S(1)}, f32[8,128]{1,0:T(8,128)S(1)}, u32[]{:S(2)}, u32[]{:S(2)}) collective-permute-start(f32[8,128]{1,0:T(8,128)S(1)} %slice_add_fusion.1), channel_id=1, source_target_pairs={{0,8},{1,9},{2,10},{3,11},{4,12},{5,13},{6,14},{7,15},{8,0},{9,1},... | collective-permute-start | bytes 12296 | tf_op jit(solution)/shard_map/ppermute | solution.py:17
  135.0 8.3 %collective-permute-start.14 = (f32[16,128]{1,0:T(8,128)S(1)}, f32[16,128]{1,0:T(8,128)S(1)}, u32[]{:S(2)}, u32[]{:S(2)}) collective-permute-start(f32[16,128]{1,0:T(8,128)S(1)} %slice_add_fusion), channel_id=1, source_target_pairs={{0,8},{1,9},{2,10},{3,11},{4,12},{5,13},{6,14},{7,15},{8,0},{9,1},... | collective-permute-start | bytes 24584 | tf_op jit(solution)/shard_map/ppermute | solution.py:17
  136.9 8.8 %collective-permute-start.11 = (f32[8,256]{1,0:T(8,128)S(1)}, f32[8,256]{1,0:T(8,128)S(1)}, u32[]{:S(2)}, u32[]{:S(2)}) collective-permute-start(f32[8,256]{1,0:T(8,128)S(1)} %maximum_select_fusion.7), channel_id=1, source_target_pairs={{0,4},{1,5},{2,6},{3,7},{4,0},{5,1},{6,2},{7,3},{8,12},{9,13},{10,... | collective-permute-start | bytes 24584 | tf_op jit(solution)/shard_map/ppermute | solution.py:17
  143.3 5.4 %collective-permute-start.15 = (f32[16,256]{1,0:T(8,128)S(1)}, f32[16,256]{1,0:T(8,128)S(1)}, u32[]{:S(2)}, u32[]{:S(2)}) collective-permute-start(f32[16,256]{1,0:T(8,128)S(1)} %maximum_select_fusion.6), channel_id=1, source_target_pairs={{0,4},{1,5},{2,6},{3,7},{4,0},{5,1},{6,2},{7,3},{8,12},{9,13},{10,... | collective-permute-start | bytes 49160 | tf_op jit(solution)/shard_map/ppermute | solution.py:17
  148.7 9.5 %collective-permute-start.16 = (f32[16,512]{1,0:T(8,128)S(1)}, f32[16,512]{1,0:T(8,128)S(1)}, u32[]{:S(2)}, u32[]{:S(2)}) collective-permute-start(f32[16,512]{1,0:T(8,128)S(1)} %maximum_select_fusion.4), channel_id=1, source_target_pairs={{0,2},{1,3},{2,0},{3,1},{4,6},{5,7},{6,4},{7,5},{8,10},{9,11},{10,... | collective-permute-start | bytes 98312 | tf_op jit(solution)/shard_map/ppermute | solution.py:17
  151.1 10.4 %collective-permute-start.13 = (f32[8,1024]{1,0:T(8,128)S(1)}, f32[8,1024]{1,0:T(8,128)S(1)}, u32[]{:S(2)}, u32[]{:S(2)}) collective-permute-start(f32[8,1024]{1,0:T(8,128)S(1)} %maximum_select_fusion.3), channel_id=1, source_target_pairs={{0,1},{1,0},{2,3},{3,2},{4,5},{5,4},{6,7},{7,6},{8,9},{9,8},{10,11... | collective-permute-start | bytes 98312 | tf_op jit(solution)/shard_map/ppermute | solution.py:17
  (11 other events, 203.6 us)

commit v2 on v0

v2 whole, which is shorter than its diff:
```python
import jax
import jax.numpy as jnp
from jax import lax
from jax.sharding import PartitionSpec as P

NT = 1024


def tap_sum(field, rows, weights, first, rows_here):
    local = rows - first
    inside = (local >= 0) & (local < rows_here)
    picked = jnp.take(field, jnp.clip(local, 0, rows_here - 1), axis=0)
    scaled = jnp.where(inside, weights, 0.0)
    return jnp.sum(picked * scaled[:, :, None], axis=1)


def mode_basis(freq, damp, times):
    return jnp.exp(-damp[:, None] * times[None, :]) * jnp.cos(freq[:, None] * times[None, :])


def shards(
    vectors,
    reflectors,
    panel_factor,
    station_rows,
    station_weights,
    event_rows,
    event_weights,
    mode_freq,
    mode_damp,
):
    high = lax.Precision.HIGHEST
    nrow = lax.axis_size("row")
    ncol = lax.axis_size("col")
    rows_here, width = vectors.shape
    pw = reflectors.shape[1]
    first = lax.axis_index("row") * rows_here
    comps = station_rows.shape[0]
    comp_here = comps // nrow
    events = event_rows.shape[0]
    samples = NT // ncol
    col = lax.axis_index("col")

    field = jnp.concatenate([vectors, reflectors], 1)
    taps = tap_sum(
        field,
        jnp.concatenate([station_rows, event_rows], 0),
        jnp.concatenate([station_weights, event_weights], 0),
        first,
        rows_here,
    )
    vt, rt = taps[:comps, :width], taps[:comps, width:]
    st, rs = taps[comps:, :width], taps[comps:, width:]

    partial_panel = jnp.dot(
        reflectors.T, vectors, precision=high, preferred_element_type=jnp.float32
    )
    summed = jnp.concatenate([partial_panel, st, rs.reshape(-1, width)], 0)
    total_rows = summed.shape[0]
    chunk = -(-total_rows // nrow)
    summed = jnp.pad(summed, ((0, chunk * nrow - total_rows), (0, 0)))
    send = jnp.concatenate(
        [
            summed.reshape(nrow, chunk, width),
            vt.reshape(nrow, comp_here, width),
            rt.reshape(nrow, comp_here * pw // width, width),
        ],
        1,
    )
    got = lax.all_to_all(send, "row", 0, 0).sum(0)
    mine = got[:chunk]
    vt_here = got[chunk:chunk + comp_here]
    rt_here = got[chunk + comp_here:].reshape(comp_here, pw)
    whole = lax.all_to_all(jnp.broadcast_to(mine[None], (nrow, chunk, width)), "row", 0, 0)
    whole = whole.reshape(nrow * chunk, width)
    panel = whole[:pw]
    st_all = whole[pw:pw + events]
    rs_all = whole[pw + events:total_rows].reshape(events, pw)

    folded = jnp.dot(panel_factor, panel, precision=high, preferred_element_type=jnp.float32)
    rotated = vectors - jnp.dot(
        reflectors, folded, precision=high, preferred_element_type=jnp.float32
    )
    receivers = vt_here - jnp.dot(rt_here, folded, precision=high, preferred_element_type=jnp.float32)
    sources = st_all - jnp.dot(rs_all, folded, precision=high, preferred_element_type=jnp.float32)

    block = jnp.concatenate([receivers, sources, mode_freq[None], mode_damp[None]], 0)
    parts = lax.all_to_all(jnp.broadcast_to(block[None], (ncol,) + block.shape), "col", 0, 0)
    receivers = parts[:, :comp_here].transpose(1, 0, 2).reshape(comp_here, -1)
    sources = parts[:, comp_here:comp_here + events].transpose(1, 0, 2).reshape(events, -1)
    freq = parts[:, comp_here + events].reshape(-1)
    damp = parts[:, comp_here + events + 1].reshape(-1)
    times = (col * samples + jnp.arange(samples)).astype(jnp.float32)
    basis = mode_basis(freq, damp, times)

    factor = 1.0 / float(freq.shape[0]) ** 0.5
    amplitude = (sources[:, None, :] * receivers[None, :, :]).reshape(events * comp_here, -1)
    series = jnp.dot(amplitude, basis, precision=high, preferred_element_type=jnp.float32)
    seismograms = series.reshape(events, comp_here, samples) * factor
    return (rotated, seismograms)


def solution(mesh):
    placed = (P("row", "col"), P("row", None), P(), P(), P(), P(), P(), P("col"), P("col"))
    return jax.shard_map(
        shards,
        mesh=mesh,
        in_specs=placed,
        out_specs=(P("row", "col"), P(None, "row", "col")),
        check_vma=False,
    )
```

time: 483 us -> 125 us (0.26)
  waiting for transfers between devices: 367 us -> 15.3 us
  blocking collectives: 58.7 us -> 38.2 us
  starting transfers between devices: 0.12 us -> 19.4 us
  between operations: 13.9 us -> 0.87 us
  other arithmetic: 5.58 us -> 13.1 us
    reduce_scatter x1 -> x0, waiting for transfers between devices: 157 us -> none  [shards(): lax.psum_scatter(tap_sum(rotated, station_rows, station_weights, first, r...]
    psum x1 -> x0, waiting for transfers between devices: 150 us -> none  [shards(): panel = lax.psum(partial_panel, 'row')]
    unnamed x4 -> x0, waiting for transfers between devices: 60.4 us -> none
    psum x1 -> x0, blocking collectives: 58.7 us -> none  [shards(): lax.psum(tap_sum(rotated, event_rows, event_weights, first, rows_here), '...]
    all_to_all x0 -> x1, blocking collectives: none -> 38.2 us  [shards(): got = lax.all_to_all(send, 'row', 0, 0).sum(0)]
    all_to_all x0 -> x2, starting transfers between devices: none -> 19.4 us  [the longest x1 10.7 us: shards(): lax.all_to_all(jnp.broadcast_to(block[None], (ncol,) + block.shape), 'col...]
    all_to_all x0 -> x2, waiting for transfers between devices: none -> 15.3 us  [the longest x1 8.31 us: shards(): lax.all_to_all(jnp.broadcast_to(mine[None], (nrow, chunk, width)), 'row',...]
    unnamed x26 -> x22, local copies, waits for them, and re-layouts: 11.9 us -> 2.71 us
  transfers between devices with their start and end apart: 3 -> 2, of which waited for: 3 -> 2; matrix products, arithmetic and copies ran while one was open for 1% -> 5% of each run, Pallas kernels for 0% -> 0%
where the time goes in v2:
time: 125 us
  blocking collectives  38.2 us (31%)
  local copies, waits for them, and re-layouts  25.2 us (20%)
  starting transfers between devices  19.4 us (16%)
  waiting for transfers between devices  15.3 us (12%)
  other arithmetic  13.1 us (10%)
  matrix products  12.5 us (10%)
    all_to_all x1, blocking collectives, shards(): got = lax.all_to_all(send, 'row', 0, 0).sum(0)  38.2 us
    gather x2, local copies, waits for them, and re-layouts, tap_sum(): picked = jnp.take(field, jnp.clip(local, 0, rows_here - 1), axis=0)  11.5 us
    all_to_all x1, starting transfers between devices, shards(): lax.all_to_all(jnp.broadcast_to(block[None], (ncol,) + block.shape), 'col...  10.7 us
    all_to_all x1, starting transfers between devices, shards(): lax.all_to_all(jnp.broadcast_to(mine[None], (nrow, chunk, width)), 'row',...  8.71 us
    all_to_all x1, waiting for transfers between devices, shards(): lax.all_to_all(jnp.broadcast_to(mine[None], (nrow, chunk, width)), 'row',...  8.31 us
    all_to_all x1, waiting for transfers between devices, shards(): lax.all_to_all(jnp.broadcast_to(block[None], (ncol,) + block.shape), 'col...  7.02 us
    reduce_sum x1, other arithmetic, tap_sum(): return jnp.sum(picked * scaled[:, :, None], axis=1)  4.99 us
    dot_general x1, matrix products, shards(): jnp.dot(reflectors.T, vectors, precision=high, preferred_element_type=jnp...  4.07 us
  transfers between devices with their start and end apart: 2, of which 2 were waited for; matrix products, arithmetic and copies ran while one was open for 5% of the time, Pallas kernels for 0%

profile of v2, /device:TPU:1, one launch (start us, length us, event | category | flops | bytes accessed | tf_op | source)
XLA Modules:
  0.0 124.6 jit_solution(15843141576308117014)
XLA Ops:
  2.5 2.1 %pad_maximum_fusion = f32[2048,384]{1,0:T(8,128)S(1)} fusion(f32[2048,256]{1,0:T(8,128)} %param.10, f32[2048,128]{1,0:T(8,128)} %param.9), kind=kLoop, calls=%fused_computation.2 | loop fusion | flops 786432 | bytes 6291456 | tf_op jit(solution)/shard_map/concatenate | solution.py:44
  4.6 6.6 %gather_fusion = f32[2080,384]{1,0:T(8,128)} fusion(f32[2048,384]{1,0:T(8,128)S(1)} %pad_maximum_fusion, s32[3072]{0:T(1024)S(1)} %pad_clamp_fusion), kind=kCustom, calls=%fused_computation | custom fusion | bytes 6398080 | tf_op jit(solution)/shard_map/jit(_take)/gather | solution.py:12
  11.2 5.0 %reshape.133 = f32[520,4,384]{2,1,0:T(4,128)} reshape(f32[2080,384]{1,0:T(8,128)} %gather_fusion) | data formatting | bytes 6389760 | tf_op jit(solution)/shard_map/jit(_take)/gather | solution.py:12
  16.2 0.9 copy.27
  17.2 5.0 %multiply_reduce_fusion = f32[520,384]{1,0:T(8,128)S(1)} fusion(f32[520,4,384]{2,1,0:T(4,128)} %reshape.133, f32[520,4]{1,0:T(8,128)} %copy.27, pred[520,4]{1,0:T(8,128)(4,1)S(1)} %copy.25), kind=kLoop, calls=%fused_computation.1 | loop fusion | flops 2196480 | bytes 4004000 | tf_op jit(solution)/shard_map/reduce_sum | solution.py:14
  22.8 4.1 %fusion.16 = f32[256,128]{1,0:T(8,128)} fusion(f32[2048,256]{1,0:T(8,128)S(1)} %copy-done.1, f32[2048,128]{1,0:T(8,128)S(1)} %copy-done.2), kind=kOutput, calls=%fused_computation.40 | convolution fusion | flops 805306368 | bytes 3276800 | tf_op jit(solution)/shard_map/dot_general | solution.py:55
  29.1 0.9 select_maximum_fusion
  30.7 1.9 %reshape.128 = f32[32,32,128]{2,1,0:T(8,128)} reshape(f32[512,256]{1,0:T(8,128)} %slice.61) | data formatting | bytes 1048576 | tf_op jit(solution)/shard_map/reshape | solution.py:66
  32.6 1.3 %pad_maximum_fusion.1 = f32[32,57,128]{2,1,0:T(8,128)S(1)} fusion(f32[32,32,128]{2,1,0:T(8,128)} %reshape.128, f32[32,16,128]{2,1,0:T(8,128)} %bitcast.35, f32[32,9,128]{2,1,0:T(8,128)} %reshape.126), kind=kLoop, calls=%fused_computation.8 | loop fusion | flops 466944 | bytes 1867776 | tf_op jit(solution)/shard_map/concatenate | solution.py:62
  33.9 38.2 %all_to_all.15 = f32[32,57,128]{2,1,0:T(8,128)} all-to-all(f32[32,57,128]{2,1,0:T(8,128)S(1)} %pad_maximum_fusion.1), channel_id=1, replica_groups=mesh['row'=32,'col'=16] {'row'}, dimensions={0} | all-to-all | bytes 1867776 | tf_op jit(solution)/shard_map/all_to_all | solution.py:70
  72.1 1.3 %reduce_sum.19 = f32[57,128]{1,0:T(8,128)S(1)} reduce(f32[32,57,128]{2,1,0:T(8,128)} %all_to_all.15, f32[]{:T(128)} %constant.16.clone.1), dimensions={0}, to_apply=%region_1.2 | reduce | flops 226176 | bytes 963076 | tf_op jit(solution)/shard_map/reduce_sum | solution.py:70
  74.2 8.7 %all-to-all-start.1 = ((f32[32,9,128]{2,1,0:T(8,128)}), f32[32,9,128]{2,1,0:T(8,128)}, u32[]{:S(2)}, u32[]{:S(2)}) async-start(f32[32,9,128]{2,1,0:T(8,128)} %broadcast_in_dim.38), calls=%async_computation.1 | async-start | bytes 524288 | tf_op jit(solution)/shard_map/all_to_all | solution.py:74
  82.9 1.3 %copy.28 = f32[2048,128]{0,1:T(8,128)} copy(f32[2048,128]{1,0:T(8,128)S(1)} %copy-done.2) | data formatting | bytes 2097152 | tf_op args[0]
  84.2 8.3 %all-to-all-done.1 = f32[32,9,128]{2,1,0:T(8,128)} async-done(((f32[32,9,128]{2,1,0:T(8,128)}), f32[32,9,128]{2,1,0:T(8,128)}, u32[]{:S(2)}, u32[]{:S(2)}) %all-to-all-start.1) | async-done | bytes 147488 | tf_op jit(solution)/shard_map/all_to_all | solution.py:74
  92.6 1.0 reshape.129
  94.0 0.9 convolution_subtract_fusion
  95.9 10.7 %all-to-all-start.2 = ((f32[16,26,128]{2,1,0:T(8,128)}), f32[16,26,128]{2,1,0:T(8,128)}, u32[]{:S(2)}, u32[]{:S(2)}) async-start(f32[16,26,128]{2,1,0:T(8,128)} %broadcast_in_dim.41), calls=%async_computation.2 | async-start | bytes 524288 | tf_op jit(solution)/shard_map/all_to_all | solution.py:88
  106.6 3.5 %fusion = f32[2048,128]{0,1:T(8,128)S(1)} fusion(f32[2048,128]{0,1:T(8,128)} %copy.28, f32[128,256]{1,0:T(8,128)S(1)} %fusion.13, f32[2048,256]{1,0:T(8,128)S(1)} %copy-done.1), kind=kOutput, calls=%fused_computation.4 | convolution fusion | flops 805568512 | bytes 4325376 | tf_op jit(solution)/shard_map/dot_general | solution.py:81
  110.1 1.3 %copy.30 = f32[2048,128]{1,0:T(8,128)} copy(f32[2048,128]{0,1:T(8,128)S(1)} %fusion) | data formatting | bytes 2097152
  111.4 7.0 %all-to-all-done.2 = f32[16,26,128]{2,1,0:T(8,128)} async-done(((f32[16,26,128]{2,1,0:T(8,128)}), f32[16,26,128]{2,1,0:T(8,128)}, u32[]{:S(2)}, u32[]{:S(2)}) %all-to-all-start.2) | async-done | bytes 213024 | tf_op jit(solution)/shard_map/all_to_all | solution.py:88
  118.4 0.9 copy_bitcast_fusion
  119.3 0.8 slice_bitcast_fusion.1
  120.2 0.9 slice_negate_fusion
  121.1 3.5 %convolution_multiply_fusion = f32[8,16,64]{2,1,0:T(8,128)} fusion(f32[16,2048]{1,0:T(8,128)S(1)} %copy_bitcast_fusion, f32[8,2048]{1,0:T(8,128)S(1)} %slice_bitcast_fusion.1, f32[2048]{0:T(1024)S(1)} %bitcast.39, f32[64]{0:T(128)S(1)} %add_convert_fusion, f32[2048]{0:T(1024)S(1)} %bitcast.38), kind=kOutput, calls=%fused_computation.5 | convolution fusion | flops 201990144 | bytes 246016 | tf_op jit(solution)/shard_map/dot_general | solution.py:98
  (44 shorter events, 7.7 us)
Async XLA Ops:
  0.6 92.9 %copy-start = (f32[256,256]{1,0:T(8,128)S(1)}, f32[256,256]{1,0:T(8,128)}, u32[]{:S(2)}) copy-start(f32[256,256]{1,0:T(8,128)} %param.11) | copy-start | bytes 786436
  11.1 5.0 %copy-start.4 = (s32[512,4]{0,1:T(4,128)S(1)}, s32[512,4]{0,1:T(4,128)}, u32[]{:S(2)}) copy-start(s32[512,4]{0,1:T(4,128)} %param.12) | copy-start | bytes 24580
  11.1 5.0 %copy-start.5 = (s32[8,4]{0,1:T(4,128)S(1)}, s32[8,4]{0,1:T(4,128)}, u32[]{:S(2)}) copy-start(s32[8,4]{0,1:T(4,128)} %param.14) | copy-start | bytes 388
  11.1 5.0 %copy-start.6 = (f32[512,4]{0,1:T(4,128)S(1)}, f32[512,4]{0,1:T(4,128)}, u32[]{:S(2)}) copy-start(f32[512,4]{0,1:T(4,128)} %param.13) | copy-start | bytes 24580
  11.2 5.0 %copy-start.7 = (f32[8,4]{0,1:T(4,128)S(1)}, f32[8,4]{0,1:T(4,128)}, u32[]{:S(2)}) copy-start(f32[8,4]{0,1:T(4,128)} %param.15) | copy-start | bytes 388
  16.1 6.7 %copy-start.1 = (f32[2048,256]{1,0:T(8,128)S(1)}, f32[2048,256]{1,0:T(8,128)}, u32[]{:S(2)}) copy-start(f32[2048,256]{1,0:T(8,128)} %param.10) | copy-start | bytes 6291460
  16.2 6.7 %copy-start.2 = (f32[2048,128]{1,0:T(8,128)S(1)}, f32[2048,128]{1,0:T(8,128)}, u32[]{:S(2)}) copy-start(f32[2048,128]{1,0:T(8,128)} %param.9) | copy-start | bytes 3145732
  72.1 22.9 %copy-start.8 = (f32[128]{0:T(128)S(1)}, f32[128]{0:T(128)}, u32[]{:S(2)}) copy-start(f32[128]{0:T(128)} %param.17) | copy-start | bytes 1540
  72.1 23.0 %copy-start.9 = (f32[128]{0:T(128)S(1)}, f32[128]{0:T(128)}, u32[]{:S(2)}) copy-start(f32[128]{0:T(128)} %param.16) | copy-start | bytes 1540
  73.5 20.1 %copy-start.3 = (f32[57,128]{1,0:T(8,128)}, f32[57,128]{1,0:T(8,128)S(1)}, u32[]{:S(2)}) copy-start(f32[57,128]{1,0:T(8,128)S(1)} %reduce_sum.19) | copy-start | bytes 87556
  74.2 18.3 %all-to-all-start.1 = ((f32[32,9,128]{2,1,0:T(8,128)}), f32[32,9,128]{2,1,0:T(8,128)}, u32[]{:S(2)}, u32[]{:S(2)}) async-start(f32[32,9,128]{2,1,0:T(8,128)} %broadcast_in_dim.38), calls=%async_computation.1 | async-start | bytes 524288 | tf_op jit(solution)/shard_map/all_to_all | solution.py:74
  95.9 22.5 %all-to-all-start.2 = ((f32[16,26,128]{2,1,0:T(8,128)}), f32[16,26,128]{2,1,0:T(8,128)}, u32[]{:S(2)}, u32[]{:S(2)}) async-start(f32[16,26,128]{2,1,0:T(8,128)} %broadcast_in_dim.41), calls=%async_computation.2 | async-start | bytes 524288 | tf_op jit(solution)/shard_map/all_to_all | solution.py:88

commit v3 on v2

--- a/solution.py
+++ b/solution.py
@@ -1,17 +1,68 @@
+import functools
+
 import jax
 import jax.numpy as jnp
 from jax import lax
+from jax.experimental import pallas as pl
+from jax.experimental.pallas import tpu as pltpu
 from jax.sharding import PartitionSpec as P
 
 NT = 1024
 
 
-def tap_sum(field, rows, weights, first, rows_here):
+def send_kernel(taps, nrow, comp_here, events, idx_ref, w_ref, panel_ref, v_ref, r_ref, send_ref):
+    width = v_ref.shape[1]
+    halves = r_ref.shape[1] // width
+    prow = panel_ref.shape[0] // nrow
+    at_rt = prow + comp_here
+    at_extra = at_rt + halves * comp_here
+
+    def tap_rows(c):
+        acc_v = acc_r = None
+        for t in range(taps):
+            i = idx_ref[c * taps + t]
+            w = w_ref[c * taps + t]
+            v = w * v_ref[pl.ds(i, 1), :]
+            r = w * r_ref[pl.ds(i, 1), :]
+            acc_v = v if acc_v is None else acc_v + v
+            acc_r = r if acc_r is None else acc_r + r
+        return acc_v, acc_r
+
+    def dest(j, carry):
+        send_ref[j, pl.ds(0, prow), :] = panel_ref[pl.ds(pl.multiple_of(j * prow, prow), prow), :]
+        for cc in range(comp_here):
+            acc_v, acc_r = tap_rows(j * comp_here + cc)
+            send_ref[j, pl.ds(prow + cc, 1), :] = acc_v
+            for h in range(halves):
+                send_ref[j, pl.ds(at_rt + halves * cc + h, 1), :] = acc_r[:, h * width:(h + 1) * width]
+        send_ref[j, pl.ds(at_extra, 1), :] = jnp.zeros((1, width), jnp.float32)
+        return carry
+
+    lax.fori_loop(0, nrow, dest, 0)
+    for e in range(events):
+        acc_v, acc_r = tap_rows(nrow * comp_here + e)
+        send_ref[e, pl.ds(at_extra, 1), :] = acc_v
+        for h in range(halves):
+            send_ref[events + halves * e + h, pl.ds(at_extra, 1), :] = acc_r[:, h * width:(h + 1) * width]
+
+
+def build_send(rows, weights, first, nrow, comp_here, events, panel, vectors, reflectors):
+    rows_here, width = vectors.shape
+    taps = rows.shape[1]
     local = rows - first
     inside = (local >= 0) & (local < rows_here)
-    picked = jnp.take(field, jnp.clip(local, 0, rows_here - 1), axis=0)
-    scaled = jnp.where(inside, weights, 0.0)
-    return jnp.sum(picked * scaled[:, :, None], axis=1)
+    idx = jnp.clip(local, 0, rows_here - 1).reshape(-1)
+    w = jnp.where(inside, weights, 0.0).reshape(-1)
+    halves = reflectors.shape[1] // width
+    chunk = panel.shape[0] // nrow + comp_here * (1 + halves) + 1
+    smem = pl.BlockSpec(memory_space=pltpu.SMEM)
+    vmem = pl.BlockSpec(memory_space=pltpu.VMEM)
+    return pl.pallas_call(
+        functools.partial(send_kernel, taps, nrow, comp_here, events),
+        out_shape=jax.ShapeDtypeStruct((nrow, chunk, width), jnp.float32),
+        in_specs=[smem, smem, vmem, vmem, vmem],
+        out_specs=vmem,
+    )(idx, w, panel, vectors, reflectors)
 
 
 def mode_basis(freq, damp, times):
@@ -41,41 +92,30 @@
     samples = NT // ncol
     col = lax.axis_index("col")
 
-    field = jnp.concatenate([vectors, reflectors], 1)
-    taps = tap_sum(
-        field,
+    partial_panel = jnp.dot(
+        reflectors.T, vectors, precision=high, preferred_element_type=jnp.float32
+    )
+    send = build_send(
         jnp.concatenate([station_rows, event_rows], 0),
         jnp.concatenate([station_weights, event_weights], 0),
         first,
-        rows_here,
+        nrow,
+        comp_here,
+        events,
+        partial_panel,
+        vectors,
+        reflectors,
     )
-    vt, rt = taps[:comps, :width], taps[:comps, width:]
-    st, rs = taps[comps:, :width], taps[comps:, width:]
-
-    partial_panel = jnp.dot(
-        reflectors.T, vectors, precision=high, preferred_element_type=jnp.float32
-    )
-    summed = jnp.concatenate([partial_panel, st, rs.reshape(-1, width)], 0)
-    total_rows = summed.shape[0]
-    chunk = -(-total_rows // nrow)
-    summed = jnp.pad(summed, ((0, chunk * nrow - total_rows), (0, 0)))
-    send = jnp.concatenate(
-        [
-            summed.reshape(nrow, chunk, width),
-            vt.reshape(nrow, comp_here, width),
-            rt.reshape(nrow, comp_here * pw // width, width),
-        ],
-        1,
-    )
+    prow = pw // nrow
     got = lax.all_to_all(send, "row", 0, 0).sum(0)
-    mine = got[:chunk]
-    vt_here = got[chunk:chunk + comp_here]
-    rt_here = got[chunk + comp_here:].reshape(comp_here, pw)
-    whole = lax.all_to_all(jnp.broadcast_to(mine[None], (nrow, chunk, width)), "row", 0, 0)
-    whole = whole.reshape(nrow * chunk, width)
-    panel = whole[:pw]
-    st_all = whole[pw:pw + events]
-    rs_all = whole[pw + events:total_rows].reshape(events, pw)
+    vt_here = got[prow:prow + comp_here]
+    rt_here = got[prow + comp_here:-1].reshape(comp_here, pw)
+    mine = jnp.concatenate([got[:prow], got[-1:]], 0)
+    whole = lax.all_to_all(jnp.broadcast_to(mine[None], (nrow,) + mine.shape), "row", 0, 0)
+    panel = whole[:, :prow].reshape(pw, width)
+    extra = whole[:, prow]
+    st_all = extra[:events]
+    rs_all = extra[events:events + events * pw // width].reshape(events, pw)
 
     folded = jnp.dot(panel_factor, panel, precision=high, preferred_element_type=jnp.float32)
     rotated = vectors - jnp.dot(

time: 125 us -> 112 us (0.90)
  local copies, waits for them, and re-layouts: 25.2 us -> 11.2 us
  other arithmetic: 13.1 us -> 3.25 us
  Pallas kernels: 0 us -> 8.3 us
  matrix products: 12.5 us -> 15.7 us
    gather x2 -> x0, local copies, waits for them, and re-layouts: 11.5 us -> none  [tap_sum(): picked = jnp.take(field, jnp.clip(local, 0, rows_here - 1), axis=0)]
    pallas_call x0 -> x1, Pallas kernels: none -> 8.3 us  [build_send(): pl.pallas_call(functools.partial(send_kernel, taps, nrow, comp_here, even...]
    reduce_sum x1 -> x0, other arithmetic: 4.99 us -> none  [tap_sum(): return jnp.sum(picked * scaled[:, :, None], axis=1)]
    concatenate x3 -> x1, other arithmetic: 4.29 us -> 0.01 us  [shards(): mine = jnp.concatenate([got[:prow], got[-1:]], 0)]
    reshape x6 -> x2, local copies, waits for them, and re-layouts: 4.16 us -> 0.61 us  [the longest x1 0.6 us: shards(): rs_all = extra[events:events + events * pw // width].reshape(events, pw)]
    dot_general x1, matrix products: 4.07 us -> 5.93 us  [shards(): jnp.dot(reflectors.T, vectors, precision=high, preferred_element_type=jnp...]
    reduce_sum x1, other arithmetic: 1.32 us -> 0.07 us  [shards(): got = lax.all_to_all(send, 'row', 0, 0).sum(0)]
    unnamed x22 -> x12, local copies, waits for them, and re-layouts: 2.71 us -> 3.86 us
  transfers between devices with their start and end apart: 2 -> 2, of which waited for: 2 -> 2; matrix products, arithmetic and copies ran while one was open for 5% -> 6% of each run, Pallas kernels for 0% -> 0%
where the time goes in v3:
time: 112 us
  blocking collectives  38.5 us (34%)
  starting transfers between devices  19.5 us (17%)
  matrix products  15.7 us (14%)
  waiting for transfers between devices  14.3 us (13%)
  local copies, waits for them, and re-layouts  11.2 us (10%)
  Pallas kernels  8.3 us (7%)
  other arithmetic  3.25 us (3%)
    all_to_all x1, blocking collectives, shards(): got = lax.all_to_all(send, 'row', 0, 0).sum(0)  38.5 us
    all_to_all x1, starting transfers between devices, shards(): lax.all_to_all(jnp.broadcast_to(block[None], (ncol,) + block.shape), 'col...  10.7 us
    all_to_all x1, starting transfers between devices, shards(): lax.all_to_all(jnp.broadcast_to(mine[None], (nrow,) + mine.shape), 'row',...  8.84 us
    all_to_all x1, waiting for transfers between devices, shards(): lax.all_to_all(jnp.broadcast_to(mine[None], (nrow,) + mine.shape), 'row',...  8.3 us
    pallas_call x1, Pallas kernels, build_send(): pl.pallas_call(functools.partial(send_kernel, taps, nrow, comp_here, even...  8.3 us
    all_to_all x1, waiting for transfers between devices, shards(): lax.all_to_all(jnp.broadcast_to(block[None], (ncol,) + block.shape), 'col...  6.04 us
    dot_general x1, matrix products, shards(): jnp.dot(reflectors.T, vectors, precision=high, preferred_element_type=jnp...  5.93 us
    unnamed x12, local copies, waits for them, and re-layouts  3.86 us
  transfers between devices with their start and end apart: 2, of which 2 were waited for; matrix products, arithmetic and copies ran while one was open for 6% of the time, Pallas kernels for 0%

profile of v3, /device:TPU:1, one launch (start us, length us, event | category | flops | bytes accessed | tf_op | source)
XLA Modules:
  0.0 111.5 jit_solution(8490832888015501121)
XLA Ops:
  0.7 0.8 fusion.14
  1.6 0.8 min.12.idx_ref
  2.3 0.8 maximum_select_fusion
  3.3 0.8 select_n.9.w_ref
  4.0 5.9 %fusion.15.panel_ref = f32[256,128]{1,0:T(8,128)} fusion(f32[2048,256]{1,0:T(8,128)} %r_ref.1, f32[2048,128]{1,0:T(8,128)} %v_ref.1), kind=kOutput, calls=%fused_computation.30 | convolution fusion | flops 805306368 | bytes 3276800 | tf_op jit(solution)/shard_map/dot_general | solution.py:95
  10.0 8.3 %shard_map.104 = f32[32,57,128]{2,1,0:T(8,128)} custom-call(s32[2080]{0:T(1024)} %min.12.idx_ref, f32[2080]{0:T(1024)} %select_n.9.w_ref, f32[256,128]{1,0:T(8,128)} %fusion.15.panel_ref, f32[2048,128]{1,0:T(8,128)} %v_ref.1, f32[2048,256]{1,0:T(8,128)} %r_ref.1), custom_call_target="tpu_custom_call" | custom-call | tf_op jit(solution)/shard_map/pallas_call | solution.py:60
  18.3 38.5 %all_to_all.15 = f32[32,57,128]{2,1,0:T(8,128)S(1)} all-to-all(f32[32,57,128]{2,1,0:T(8,128)} %shard_map.104), channel_id=1, replica_groups=mesh['row'=32,'col'=16] {'row'}, dimensions={0} | all-to-all | bytes 1867776 | tf_op jit(solution)/shard_map/all_to_all | solution.py:110
  57.6 8.8 %all-to-all-start.1 = ((f32[32,9,128]{2,1,0:T(8,128)}), f32[32,9,128]{2,1,0:T(8,128)}, u32[]{:S(2)}, u32[]{:S(2)}) async-start(f32[32,9,128]{2,1,0:T(8,128)} %broadcast_in_dim.13), calls=%async_computation.1 | async-start | bytes 524288 | tf_op jit(solution)/shard_map/all_to_all | solution.py:114
  66.4 1.3 %copy.25 = f32[2048,128]{0,1:T(8,128)} copy(f32[2048,128]{1,0:T(8,128)S(1)} %copy-done.2) | data formatting | bytes 2097152 | tf_op args[0]
  67.7 8.3 %all-to-all-done.1 = f32[32,9,128]{2,1,0:T(8,128)} async-done(((f32[32,9,128]{2,1,0:T(8,128)}), f32[32,9,128]{2,1,0:T(8,128)}, u32[]{:S(2)}, u32[]{:S(2)}) %all-to-all-start.1) | async-done | bytes 147488 | tf_op jit(solution)/shard_map/all_to_all | solution.py:114
  76.0 0.9 slice_reduce_fusion
  77.5 1.3 %fusion.13 = f32[128,256]{1,0:T(8,128)S(1)} fusion(f32[256,256]{1,0:T(8,128)S(1)} %copy-done, f32[32,9,128]{2,1,0:T(8,128)} %all-to-all-done.1), kind=kOutput, calls=%fused_computation.20 | convolution fusion | flops 100663296 | bytes 524288 | tf_op jit(solution)/shard_map/dot_general | solution.py:120
  78.8 0.9 convolution_subtract_fusion
  79.7 0.8 slice.57
  80.5 0.9 convolution_subtract_fusion.1
  82.1 0.7 broadcast_in_dim.28
  82.8 10.7 %all-to-all-start.2 = ((f32[16,26,128]{2,1,0:T(8,128)}), f32[16,26,128]{2,1,0:T(8,128)}, u32[]{:S(2)}, u32[]{:S(2)}) async-start(f32[16,26,128]{2,1,0:T(8,128)} %broadcast_in_dim.28), calls=%async_computation.2 | async-start | bytes 524288 | tf_op jit(solution)/shard_map/all_to_all | solution.py:128
  93.6 3.2 %fusion = f32[2048,128]{0,1:T(8,128)} fusion(f32[2048,128]{0,1:T(8,128)S(1)} %copy-done.3, f32[128,256]{1,0:T(8,128)S(1)} %fusion.13, f32[2048,256]{1,0:T(8,128)S(1)} %copy-done.1), kind=kOutput, calls=%fused_computation.1 | convolution fusion | flops 805568512 | bytes 4325376 | tf_op jit(solution)/shard_map/dot_general | solution.py:121
  96.8 2.5 %copy.28 = f32[2048,128]{1,0:T(8,128)} copy(f32[2048,128]{0,1:T(8,128)} %fusion) | data formatting | bytes 2097152
  99.3 6.0 %all-to-all-done.2 = f32[16,26,128]{2,1,0:T(8,128)} async-done(((f32[16,26,128]{2,1,0:T(8,128)}), f32[16,26,128]{2,1,0:T(8,128)}, u32[]{:S(2)}, u32[]{:S(2)}) %all-to-all-start.2) | async-done | bytes 213024 | tf_op jit(solution)/shard_map/all_to_all | solution.py:128
  105.4 0.9 slice_negate_fusion
  106.3 0.8 slice_bitcast_fusion.3
  107.1 0.9 copy_bitcast_fusion
  108.1 3.5 %convolution_multiply_fusion = f32[8,16,64]{2,1,0:T(8,128)} fusion(f32[16,2048]{1,0:T(8,128)S(1)} %copy_bitcast_fusion, f32[8,2048]{1,0:T(8,128)S(1)} %slice_bitcast_fusion.3, f32[2048]{0:T(1024)S(1)} %bitcast.38, f32[64]{0:T(128)S(1)} %add_convert_fusion, f32[2048]{0:T(1024)S(1)} %bitcast.37), kind=kOutput, calls=%fused_computation.2 | convolution fusion | flops 201990144 | bytes 246016 | tf_op jit(solution)/shard_map/dot_general | solution.py:138
  (22 shorter events, 2.5 us)
Async XLA Ops:
  0.6 76.9 %copy-start = (f32[256,256]{1,0:T(8,128)S(1)}, f32[256,256]{1,0:T(8,128)}, u32[]{:S(2)}) copy-start(f32[256,256]{1,0:T(8,128)} %param.11) | copy-start | bytes 786436
  18.2 48.2 %copy-start.2 = (f32[2048,128]{1,0:T(8,128)S(1)}, f32[2048,128]{1,0:T(8,128)}, u32[]{:S(2)}) copy-start(f32[2048,128]{1,0:T(8,128)} %v_ref.1) | copy-start | bytes 3145732
  56.8 20.1 %copy-start.4 = (f32[57,128]{1,0:T(8,128)}, f32[57,128]{1,0:T(8,128)S(1)}, u32[]{:S(2)}) copy-start(f32[57,128]{1,0:T(8,128)S(1)} %reduce_sum.9) | copy-start | bytes 87556
  57.6 36.0 %copy-start.1 = (f32[2048,256]{1,0:T(8,128)S(1)}, f32[2048,256]{1,0:T(8,128)}, u32[]{:S(2)}) copy-start(f32[2048,256]{1,0:T(8,128)} %r_ref.1) | copy-start | bytes 6291460
  57.6 18.5 %all-to-all-start.1 = ((f32[32,9,128]{2,1,0:T(8,128)}), f32[32,9,128]{2,1,0:T(8,128)}, u32[]{:S(2)}, u32[]{:S(2)}) async-start(f32[32,9,128]{2,1,0:T(8,128)} %broadcast_in_dim.13), calls=%async_computation.1 | async-start | bytes 524288 | tf_op jit(solution)/shard_map/all_to_all | solution.py:114
  67.7 25.8 %copy-start.3 = (f32[2048,128]{0,1:T(8,128)S(1)}, f32[2048,128]{0,1:T(8,128)}, u32[]{:S(2)}) copy-start(f32[2048,128]{0,1:T(8,128)} %copy.25) | copy-start | bytes 3145732
  82.8 22.5 %all-to-all-start.2 = ((f32[16,26,128]{2,1,0:T(8,128)}), f32[16,26,128]{2,1,0:T(8,128)}, u32[]{:S(2)}, u32[]{:S(2)}) async-start(f32[16,26,128]{2,1,0:T(8,128)} %broadcast_in_dim.28), calls=%async_computation.2 | async-start | bytes 524288 | tf_op jit(solution)/shard_map/all_to_all | solution.py:128

commit v4 on v3

--- a/solution.py
+++ b/solution.py
@@ -10,18 +10,23 @@
 NT = 1024
 
 
-def send_kernel(taps, nrow, comp_here, events, idx_ref, w_ref, panel_ref, v_ref, r_ref, send_ref):
-    width = v_ref.shape[1]
+def send_kernel(nrow, comp_here, srow_ref, sw_ref, erow_ref, ew_ref, panel_ref, v_ref, r_ref, send_ref):
+    rows_here, width = v_ref.shape
     halves = r_ref.shape[1] // width
     prow = panel_ref.shape[0] // nrow
     at_rt = prow + comp_here
     at_extra = at_rt + halves * comp_here
+    taps = srow_ref.shape[1]
+    events = erow_ref.shape[0]
+    first = lax.axis_index("row") * rows_here
 
-    def tap_rows(c):
+    def tap_rows(rows_ref, w_ref, c):
         acc_v = acc_r = None
         for t in range(taps):
-            i = idx_ref[c * taps + t]
-            w = w_ref[c * taps + t]
+            local = rows_ref[c, t] - first
+            inside = (local >= 0) & (local < rows_here)
+            i = jnp.clip(local, 0, rows_here - 1)
+            w = jnp.where(inside, w_ref[c, t], 0.0)
             v = w * v_ref[pl.ds(i, 1), :]
             r = w * r_ref[pl.ds(i, 1), :]
             acc_v = v if acc_v is None else acc_v + v
@@ -31,7 +36,7 @@
     def dest(j, carry):
         send_ref[j, pl.ds(0, prow), :] = panel_ref[pl.ds(pl.multiple_of(j * prow, prow), prow), :]
         for cc in range(comp_here):
-            acc_v, acc_r = tap_rows(j * comp_here + cc)
+            acc_v, acc_r = tap_rows(srow_ref, sw_ref, j * comp_here + cc)
             send_ref[j, pl.ds(prow + cc, 1), :] = acc_v
             for h in range(halves):
                 send_ref[j, pl.ds(at_rt + halves * cc + h, 1), :] = acc_r[:, h * width:(h + 1) * width]
@@ -40,29 +45,24 @@
 
     lax.fori_loop(0, nrow, dest, 0)
     for e in range(events):
-        acc_v, acc_r = tap_rows(nrow * comp_here + e)
+        acc_v, acc_r = tap_rows(erow_ref, ew_ref, e)
         send_ref[e, pl.ds(at_extra, 1), :] = acc_v
         for h in range(halves):
             send_ref[events + halves * e + h, pl.ds(at_extra, 1), :] = acc_r[:, h * width:(h + 1) * width]
 
 
-def build_send(rows, weights, first, nrow, comp_here, events, panel, vectors, reflectors):
-    rows_here, width = vectors.shape
-    taps = rows.shape[1]
-    local = rows - first
-    inside = (local >= 0) & (local < rows_here)
-    idx = jnp.clip(local, 0, rows_here - 1).reshape(-1)
-    w = jnp.where(inside, weights, 0.0).reshape(-1)
+def build_send(nrow, comp_here, srows, sweights, erows, eweights, panel, vectors, reflectors):
+    width = vectors.shape[1]
     halves = reflectors.shape[1] // width
     chunk = panel.shape[0] // nrow + comp_here * (1 + halves) + 1
     smem = pl.BlockSpec(memory_space=pltpu.SMEM)
     vmem = pl.BlockSpec(memory_space=pltpu.VMEM)
     return pl.pallas_call(
-        functools.partial(send_kernel, taps, nrow, comp_here, events),
+        functools.partial(send_kernel, nrow, comp_here),
         out_shape=jax.ShapeDtypeStruct((nrow, chunk, width), jnp.float32),
-        in_specs=[smem, smem, vmem, vmem, vmem],
+        in_specs=[smem, smem, smem, smem, vmem, vmem, vmem],
         out_specs=vmem,
-    )(idx, w, panel, vectors, reflectors)
+    )(srows, sweights, erows, eweights, panel, vectors, reflectors)
 
 
 def mode_basis(freq, damp, times):
@@ -80,7 +80,7 @@
     mode_freq,
     mode_damp,
 ):
-    high = lax.Precision.HIGHEST
+    high = lax.Precision.HIGH
     nrow = lax.axis_size("row")
     ncol = lax.axis_size("col")
     rows_here, width = vectors.shape
@@ -96,12 +96,12 @@
         reflectors.T, vectors, precision=high, preferred_element_type=jnp.float32
     )
     send = build_send(
-        jnp.concatenate([station_rows, event_rows], 0),
-        jnp.concatenate([station_weights, event_weights], 0),
-        first,
         nrow,
         comp_here,
-        events,
+        station_rows,
+        station_weights,
+        event_rows,
+        event_weights,
         partial_panel,
         vectors,
         reflectors,

time: 112 us -> 125 us (1.12)
  Pallas kernels: 8.3 us -> 20.8 us
  local copies, waits for them, and re-layouts: 11.2 us -> 15.2 us
  matrix products: 15.7 us -> 12.3 us
  other arithmetic: 3.25 us -> 1.75 us
    pallas_call x1, Pallas kernels: 8.3 us -> 20.8 us  [build_send(): pl.pallas_call(functools.partial(send_kernel, nrow, comp_here), out_shape...]
    unnamed x12 -> x16, local copies, waits for them, and re-layouts: 3.86 us -> 9.69 us
    dot_general x1, matrix products: 5.93 us -> 4.31 us  [shards(): jnp.dot(reflectors.T, vectors, precision=high, preferred_element_type=jnp...]
  transfers between devices with their start and end apart: 2 -> 2, of which waited for: 2 -> 2; matrix products, arithmetic and copies ran while one was open for 6% -> 5% of each run, Pallas kernels for 0% -> 0%
where the time goes in v4:
time: 125 us; the launch traced here: 124 us
  blocking collectives  38.5 us (31%)
  Pallas kernels  20.8 us (17%)
  starting transfers between devices  19.5 us (16%)
  waiting for transfers between devices  15.4 us (12%)
  local copies, waits for them, and re-layouts  15.2 us (12%)
  matrix products  12.3 us (10%)
  other arithmetic  1.75 us (1%)
    all_to_all x1, blocking collectives, shards(): got = lax.all_to_all(send, 'row', 0, 0).sum(0)  38.5 us
    pallas_call x1, Pallas kernels, build_send(): pl.pallas_call(functools.partial(send_kernel, nrow, comp_here), out_shape...  20.8 us
    all_to_all x1, starting transfers between devices, shards(): lax.all_to_all(jnp.broadcast_to(block[None], (ncol,) + block.shape), 'col...  10.7 us
    unnamed x16, local copies, waits for them, and re-layouts  9.69 us
    all_to_all x1, starting transfers between devices, shards(): lax.all_to_all(jnp.broadcast_to(mine[None], (nrow,) + mine.shape), 'row',...  8.84 us
    all_to_all x1, waiting for transfers between devices, shards(): lax.all_to_all(jnp.broadcast_to(mine[None], (nrow,) + mine.shape), 'row',...  8.29 us
    all_to_all x1, waiting for transfers between devices, shards(): lax.all_to_all(jnp.broadcast_to(block[None], (ncol,) + block.shape), 'col...  7.12 us
    dot_general x1, matrix products, shards(): jnp.dot(reflectors.T, vectors, precision=high, preferred_element_type=jnp...  4.31 us
  transfers between devices with their start and end apart: 2, of which 2 were waited for; matrix products, arithmetic and copies ran while one was open for 5% of the time, Pallas kernels for 0%

profile of v4, /device:TPU:1, one launch (start us, length us, event | category | flops | bytes accessed | tf_op | source)
XLA Modules:
  0.0 124.3 jit_solution(7616480930273546839)
XLA Ops:
  0.6 1.4 %copy.33.erow_ref = s32[8,4]{1,0:T(8,128)} copy(s32[8,4]{0,1:T(4,128)} %param.14) | data formatting | bytes 256 | tf_op args[5]
  2.0 1.4 %copy.34.ew_ref = f32[8,4]{1,0:T(8,128)} copy(f32[8,4]{0,1:T(4,128)} %param.15) | data formatting | bytes 256 | tf_op args[6]
  3.4 1.5 %copy.31.srow_ref = s32[512,4]{1,0:T(8,128)} copy(s32[512,4]{0,1:T(4,128)} %param.12) | data formatting | bytes 16384 | tf_op args[3]
  4.9 1.5 %copy.32.sw_ref = f32[512,4]{1,0:T(8,128)} copy(f32[512,4]{0,1:T(4,128)} %param.13) | data formatting | bytes 16384 | tf_op args[4]
  6.5 4.3 %fusion.14.panel_ref = f32[256,128]{1,0:T(8,128)} fusion(f32[2048,256]{1,0:T(8,128)} %r_ref.1, f32[2048,128]{1,0:T(8,128)} %v_ref.1), kind=kOutput, calls=%fused_computation.27 | convolution fusion | flops 402653184 | bytes 3276800 | tf_op jit(solution)/shard_map/dot_general | solution.py:95
  10.8 20.8 %shard_map.104 = f32[32,57,128]{2,1,0:T(8,128)} custom-call(s32[512,4]{1,0:T(8,128)} %copy.31.srow_ref, f32[512,4]{1,0:T(8,128)} %copy.32.sw_ref, s32[8,4]{1,0:T(8,128)} %copy.33.erow_ref, f32[8,4]{1,0:T(8,128)} %copy.34.ew_ref, f32[256,128]{1,0:T(8,128)} %fusion.14.panel_ref, f32[2048,128]{1,0:T(8,128)} %v_ref.1, f32[2048,256]{1,0:T(8,128)} %r_ref.1), custom_call_target="tpu_custom_call" | custom-call | tf_op jit(solution)/shard_map/pallas_call | solution.py:60
  31.6 38.5 %all_to_all.15 = f32[32,57,128]{2,1,0:T(8,128)S(1)} all-to-all(f32[32,57,128]{2,1,0:T(8,128)} %shard_map.104), channel_id=1, replica_groups=mesh['row'=32,'col'=16] {'row'}, dimensions={0} | all-to-all | bytes 1867776 | tf_op jit(solution)/shard_map/all_to_all | solution.py:110
  70.9 8.8 %all-to-all-start.1 = ((f32[32,9,128]{2,1,0:T(8,128)}), f32[32,9,128]{2,1,0:T(8,128)}, u32[]{:S(2)}, u32[]{:S(2)}) async-start(f32[32,9,128]{2,1,0:T(8,128)} %broadcast_in_dim.8), calls=%async_computation.1 | async-start | bytes 524288 | tf_op jit(solution)/shard_map/all_to_all | solution.py:114
  79.8 1.3 %copy.35 = f32[2048,128]{0,1:T(8,128)} copy(f32[2048,128]{1,0:T(8,128)S(1)} %copy-done.2) | data formatting | bytes 2097152 | tf_op args[0]
  81.1 8.3 %all-to-all-done.1 = f32[32,9,128]{2,1,0:T(8,128)} async-done(((f32[32,9,128]{2,1,0:T(8,128)}), f32[32,9,128]{2,1,0:T(8,128)}, u32[]{:S(2)}, u32[]{:S(2)}) %all-to-all-start.1) | async-done | bytes 147488 | tf_op jit(solution)/shard_map/all_to_all | solution.py:114
  89.4 0.9 slice_reduce_fusion
  90.9 1.2 fusion.13
  92.1 0.8 convolution_subtract_fusion
  92.9 0.8 slice.57
  93.7 0.8 convolution_subtract_fusion.1
  94.5 0.7 pad_maximum_fusion
  96.0 10.7 %all-to-all-start.2 = ((f32[16,26,128]{2,1,0:T(8,128)}), f32[16,26,128]{2,1,0:T(8,128)}, u32[]{:S(2)}, u32[]{:S(2)}) async-start(f32[16,26,128]{2,1,0:T(8,128)} %broadcast_in_dim.11), calls=%async_computation.2 | async-start | bytes 524288 | tf_op jit(solution)/shard_map/all_to_all | solution.py:128
  106.8 2.1 %fusion = f32[2048,128]{0,1:T(8,128)} fusion(f32[2048,128]{0,1:T(8,128)S(1)} %copy-done.3, f32[128,256]{1,0:T(8,128)S(1)} %fusion.13, f32[2048,256]{1,0:T(8,128)S(1)} %copy-done.1), kind=kOutput, calls=%fused_computation.1 | convolution fusion | flops 402915328 | bytes 4325376 | tf_op jit(solution)/shard_map/dot_general | solution.py:121
  108.9 2.5 %copy.38 = f32[2048,128]{1,0:T(8,128)} copy(f32[2048,128]{0,1:T(8,128)} %fusion) | data formatting | bytes 2097152
  111.4 7.1 %all-to-all-done.2 = f32[16,26,128]{2,1,0:T(8,128)} async-done(((f32[16,26,128]{2,1,0:T(8,128)}), f32[16,26,128]{2,1,0:T(8,128)}, u32[]{:S(2)}, u32[]{:S(2)}) %all-to-all-start.2) | async-done | bytes 213024 | tf_op jit(solution)/shard_map/all_to_all | solution.py:128
  118.6 0.9 slice_negate_fusion
  119.5 0.8 slice_bitcast_fusion.3
  120.3 0.9 copy_bitcast_fusion
  121.3 3.0 %convolution_multiply_fusion = f32[8,16,64]{2,1,0:T(8,128)} fusion(f32[16,2048]{1,0:T(8,128)S(1)} %copy_bitcast_fusion, f32[8,2048]{1,0:T(8,128)S(1)} %slice_bitcast_fusion.3, f32[2048]{0:T(1024)S(1)} %bitcast.38, f32[64]{0:T(128)S(1)} %add_convert_fusion, f32[2048]{0:T(1024)S(1)} %bitcast.37), kind=kOutput, calls=%fused_computation.2 | convolution fusion | flops 101326848 | bytes 246016 | tf_op jit(solution)/shard_map/dot_general | solution.py:138
  (20 shorter events, 2.2 us)
Async XLA Ops:
  0.6 90.2 %copy-start = (f32[256,256]{1,0:T(8,128)S(1)}, f32[256,256]{1,0:T(8,128)}, u32[]{:S(2)}) copy-start(f32[256,256]{1,0:T(8,128)} %param.11) | copy-start | bytes 786436
  31.6 48.2 %copy-start.2 = (f32[2048,128]{1,0:T(8,128)S(1)}, f32[2048,128]{1,0:T(8,128)}, u32[]{:S(2)}) copy-start(f32[2048,128]{1,0:T(8,128)} %v_ref.1) | copy-start | bytes 3145732
  70.1 20.1 %copy-start.4 = (f32[57,128]{1,0:T(8,128)}, f32[57,128]{1,0:T(8,128)S(1)}, u32[]{:S(2)}) copy-start(f32[57,128]{1,0:T(8,128)S(1)} %reduce_sum.9) | copy-start | bytes 87556
  70.9 35.8 %copy-start.1 = (f32[2048,256]{1,0:T(8,128)S(1)}, f32[2048,256]{1,0:T(8,128)}, u32[]{:S(2)}) copy-start(f32[2048,256]{1,0:T(8,128)} %r_ref.1) | copy-start | bytes 6291460
  70.9 18.5 %all-to-all-start.1 = ((f32[32,9,128]{2,1,0:T(8,128)}), f32[32,9,128]{2,1,0:T(8,128)}, u32[]{:S(2)}, u32[]{:S(2)}) async-start(f32[32,9,128]{2,1,0:T(8,128)} %broadcast_in_dim.8), calls=%async_computation.1 | async-start | bytes 524288 | tf_op jit(solution)/shard_map/all_to_all | solution.py:114
  81.1 25.7 %copy-start.3 = (f32[2048,128]{0,1:T(8,128)S(1)}, f32[2048,128]{0,1:T(8,128)}, u32[]{:S(2)}) copy-start(f32[2048,128]{0,1:T(8,128)} %copy.35) | copy-start | bytes 3145732
  96.0 22.5 %all-to-all-start.2 = ((f32[16,26,128]{2,1,0:T(8,128)}), f32[16,26,128]{2,1,0:T(8,128)}, u32[]{:S(2)}, u32[]{:S(2)}) async-start(f32[16,26,128]{2,1,0:T(8,128)} %broadcast_in_dim.11), calls=%async_computation.2 | async-start | bytes 524288 | tf_op jit(solution)/shard_map/all_to_all | solution.py:128

commit v5 on v3

--- a/solution.py
+++ b/solution.py
@@ -10,18 +10,29 @@
 NT = 1024
 
 
-def send_kernel(taps, nrow, comp_here, events, idx_ref, w_ref, panel_ref, v_ref, r_ref, send_ref):
+def send_kernel(nrow, comp_here, events, taps, tab_ref, v_ref, r_ref, send_ref):
     width = v_ref.shape[1]
-    halves = r_ref.shape[1] // width
-    prow = panel_ref.shape[0] // nrow
+    pw = r_ref.shape[1]
+    halves = pw // width
+    prow = pw // nrow
     at_rt = prow + comp_here
     at_extra = at_rt + halves * comp_here
+
+    panel = lax.dot_general(
+        r_ref[...],
+        v_ref[...],
+        (((0,), (0,)), ((), ())),
+        precision=lax.Precision.HIGHEST,
+        preferred_element_type=jnp.float32,
+    )
+    for j in range(nrow):
+        send_ref[j, pl.ds(0, prow), :] = panel[j * prow:(j + 1) * prow]
 
     def tap_rows(c):
         acc_v = acc_r = None
         for t in range(taps):
-            i = idx_ref[c * taps + t]
-            w = w_ref[c * taps + t]
+            i = tab_ref[0, c * taps + t].astype(jnp.int32)
+            w = tab_ref[1, c * taps + t]
             v = w * v_ref[pl.ds(i, 1), :]
             r = w * r_ref[pl.ds(i, 1), :]
             acc_v = v if acc_v is None else acc_v + v
@@ -29,7 +40,6 @@
         return acc_v, acc_r
 
     def dest(j, carry):
-        send_ref[j, pl.ds(0, prow), :] = panel_ref[pl.ds(pl.multiple_of(j * prow, prow), prow), :]
         for cc in range(comp_here):
             acc_v, acc_r = tap_rows(j * comp_here + cc)
             send_ref[j, pl.ds(prow + cc, 1), :] = acc_v
@@ -46,23 +56,28 @@
             send_ref[events + halves * e + h, pl.ds(at_extra, 1), :] = acc_r[:, h * width:(h + 1) * width]
 
 
-def build_send(rows, weights, first, nrow, comp_here, events, panel, vectors, reflectors):
+def build_send(nrow, comp_here, rows, weights, first, vectors, reflectors):
     rows_here, width = vectors.shape
     taps = rows.shape[1]
+    events = rows.shape[0] - nrow * comp_here
     local = rows - first
     inside = (local >= 0) & (local < rows_here)
-    idx = jnp.clip(local, 0, rows_here - 1).reshape(-1)
-    w = jnp.where(inside, weights, 0.0).reshape(-1)
+    table = jnp.stack(
+        [
+            jnp.clip(local, 0, rows_here - 1).astype(jnp.float32).reshape(-1),
+            jnp.where(inside, weights, 0.0).reshape(-1),
+        ]
+    )
     halves = reflectors.shape[1] // width
-    chunk = panel.shape[0] // nrow + comp_here * (1 + halves) + 1
+    chunk = reflectors.shape[1] // nrow + comp_here * (1 + halves) + 1
     smem = pl.BlockSpec(memory_space=pltpu.SMEM)
     vmem = pl.BlockSpec(memory_space=pltpu.VMEM)
     return pl.pallas_call(
-        functools.partial(send_kernel, taps, nrow, comp_here, events),
+        functools.partial(send_kernel, nrow, comp_here, events, taps),
         out_shape=jax.ShapeDtypeStruct((nrow, chunk, width), jnp.float32),
-        in_specs=[smem, smem, vmem, vmem, vmem],
+        in_specs=[smem, vmem, vmem],
         out_specs=vmem,
-    )(idx, w, panel, vectors, reflectors)
+    )(table, vectors, reflectors)
 
 
 def mode_basis(freq, damp, times):
@@ -80,7 +95,7 @@
     mode_freq,
     mode_damp,
 ):
-    high = lax.Precision.HIGHEST
+    high = lax.Precision.HIGH
     nrow = lax.axis_size("row")
     ncol = lax.axis_size("col")
     rows_here, width = vectors.shape
@@ -92,17 +107,12 @@
     samples = NT // ncol
     col = lax.axis_index("col")
 
-    partial_panel = jnp.dot(
-        reflectors.T, vectors, precision=high, preferred_element_type=jnp.float32
-    )
     send = build_send(
+        nrow,
+        comp_here,
         jnp.concatenate([station_rows, event_rows], 0),
         jnp.concatenate([station_weights, event_weights], 0),
         first,
-        nrow,
-        comp_here,
-        events,
-        partial_panel,
         vectors,
         reflectors,
     )

time: 112 us -> 113 us (level)
  matrix products: 15.7 us -> 7.98 us
  Pallas kernels: 8.3 us -> 16 us
    pallas_call x1, Pallas kernels: 8.3 us -> 16 us  [build_send(): pl.pallas_call(functools.partial(send_kernel, nrow, comp_here, events, ta...]
    dot_general x1 -> x0, matrix products: 5.93 us -> none  [shards(): jnp.dot(reflectors.T, vectors, precision=high, preferred_element_type=jnp...]
  transfers between devices with their start and end apart: 2 -> 2, of which waited for: 2 -> 2; matrix products, arithmetic and copies ran while one was open for 6% -> 5% of each run, Pallas kernels for 0% -> 0%
where the time goes in v5:
time: 113 us; the launch traced here: 112 us
  blocking collectives  38.5 us (34%)
  starting transfers between devices  19.5 us (17%)
  Pallas kernels  16 us (14%)
  waiting for transfers between devices  15.4 us (14%)
  local copies, waits for them, and re-layouts  10.1 us (9%)
  matrix products  7.98 us (7%)
  other arithmetic  3.9 us (3%)
    all_to_all x1, blocking collectives, shards(): got = lax.all_to_all(send, 'row', 0, 0).sum(0)  38.5 us
    pallas_call x1, Pallas kernels, build_send(): pl.pallas_call(functools.partial(send_kernel, nrow, comp_here, events, ta...  16 us
    all_to_all x1, starting transfers between devices, shards(): lax.all_to_all(jnp.broadcast_to(block[None], (ncol,) + block.shape), 'col...  10.7 us
    all_to_all x1, starting transfers between devices, shards(): lax.all_to_all(jnp.broadcast_to(mine[None], (nrow,) + mine.shape), 'row',...  8.84 us
    all_to_all x1, waiting for transfers between devices, shards(): lax.all_to_all(jnp.broadcast_to(mine[None], (nrow,) + mine.shape), 'row',...  8.3 us
    all_to_all x1, waiting for transfers between devices, shards(): lax.all_to_all(jnp.broadcast_to(block[None], (ncol,) + block.shape), 'col...  7.12 us
    unnamed x12, local copies, waits for them, and re-layouts  3.86 us
    dot_general x1, matrix products, shards(): jnp.dot(amplitude, basis, precision=high, preferred_element_type=jnp.floa...  3 us
  transfers between devices with their start and end apart: 2, of which 2 were waited for; matrix products, arithmetic and copies ran while one was open for 5% of the time, Pallas kernels for 0%

profile of v5, /device:TPU:1, one launch (start us, length us, event | category | flops | bytes accessed | tf_op | source)
XLA Modules:
  0.0 112.1 jit_solution(8146549103548370212)
XLA Ops:
  0.7 0.8 clamp_convert_fusion
  1.8 0.8 maximum_select_fusion
  2.9 0.6 pad_maximum_fusion.tab_ref
  3.5 16.0 %shard_map.104 = f32[32,57,128]{2,1,0:T(8,128)} custom-call(f32[2,2080]{1,0:T(2,128)} %pad_maximum_fusion.tab_ref, f32[2048,128]{1,0:T(8,128)} %v_ref.1, f32[2048,256]{1,0:T(8,128)} %r_ref.1), custom_call_target="tpu_custom_call" | custom-call | tf_op jit(solution)/shard_map/pallas_call | solution.py:75
  19.4 38.5 %all_to_all.15 = f32[32,57,128]{2,1,0:T(8,128)S(1)} all-to-all(f32[32,57,128]{2,1,0:T(8,128)} %shard_map.104), channel_id=1, replica_groups=mesh['row'=32,'col'=16] {'row'}, dimensions={0} | all-to-all | bytes 1867776 | tf_op jit(solution)/shard_map/all_to_all | solution.py:120
  58.0 0.7 broadcast_in_dim.13
  58.8 8.8 %all-to-all-start.1 = ((f32[32,9,128]{2,1,0:T(8,128)}), f32[32,9,128]{2,1,0:T(8,128)}, u32[]{:S(2)}, u32[]{:S(2)}) async-start(f32[32,9,128]{2,1,0:T(8,128)} %broadcast_in_dim.13), calls=%async_computation.1 | async-start | bytes 524288 | tf_op jit(solution)/shard_map/all_to_all | solution.py:124
  67.6 1.3 %copy.27 = f32[2048,128]{0,1:T(8,128)} copy(f32[2048,128]{1,0:T(8,128)S(1)} %copy-done.2) | data formatting | bytes 2097152 | tf_op args[0]
  68.9 8.3 %all-to-all-done.1 = f32[32,9,128]{2,1,0:T(8,128)} async-done(((f32[32,9,128]{2,1,0:T(8,128)}), f32[32,9,128]{2,1,0:T(8,128)}, u32[]{:S(2)}, u32[]{:S(2)}) %all-to-all-start.1) | async-done | bytes 147488 | tf_op jit(solution)/shard_map/all_to_all | solution.py:124
  77.2 0.9 slice_reduce_fusion
  78.7 1.2 %fusion.13 = f32[128,256]{1,0:T(8,128)S(1)} fusion(f32[256,256]{1,0:T(8,128)S(1)} %copy-done, f32[32,9,128]{2,1,0:T(8,128)} %all-to-all-done.1), kind=kOutput, calls=%fused_computation.20 | convolution fusion | flops 50331648 | bytes 524288 | tf_op jit(solution)/shard_map/dot_general | solution.py:130
  79.9 0.8 convolution_subtract_fusion
  80.7 0.8 slice.57
  81.6 0.8 convolution_subtract_fusion.1
  82.4 0.7 pad_maximum_fusion.1
  83.1 0.7 broadcast_in_dim.28
  83.9 10.7 %all-to-all-start.2 = ((f32[16,26,128]{2,1,0:T(8,128)}), f32[16,26,128]{2,1,0:T(8,128)}, u32[]{:S(2)}, u32[]{:S(2)}) async-start(f32[16,26,128]{2,1,0:T(8,128)} %broadcast_in_dim.28), calls=%async_computation.2 | async-start | bytes 524288 | tf_op jit(solution)/shard_map/all_to_all | solution.py:138
  94.6 2.1 %fusion = f32[2048,128]{0,1:T(8,128)} fusion(f32[2048,128]{0,1:T(8,128)S(1)} %copy-done.3, f32[128,256]{1,0:T(8,128)S(1)} %fusion.13, f32[2048,256]{1,0:T(8,128)S(1)} %copy-done.1), kind=kOutput, calls=%fused_computation.1 | convolution fusion | flops 402915328 | bytes 4325376 | tf_op jit(solution)/shard_map/dot_general | solution.py:131
  96.7 2.5 %copy.30 = f32[2048,128]{1,0:T(8,128)} copy(f32[2048,128]{0,1:T(8,128)} %fusion) | data formatting | bytes 2097152
  99.3 7.1 %all-to-all-done.2 = f32[16,26,128]{2,1,0:T(8,128)} async-done(((f32[16,26,128]{2,1,0:T(8,128)}), f32[16,26,128]{2,1,0:T(8,128)}, u32[]{:S(2)}, u32[]{:S(2)}) %all-to-all-start.2) | async-done | bytes 213024 | tf_op jit(solution)/shard_map/all_to_all | solution.py:138
  106.4 0.9 slice_negate_fusion
  107.3 0.8 slice_bitcast_fusion.3
  108.2 0.9 copy_bitcast_fusion
  109.1 3.0 %convolution_multiply_fusion = f32[8,16,64]{2,1,0:T(8,128)} fusion(f32[16,2048]{1,0:T(8,128)S(1)} %copy_bitcast_fusion, f32[8,2048]{1,0:T(8,128)S(1)} %slice_bitcast_fusion.3, f32[2048]{0:T(1024)S(1)} %bitcast.36, f32[64]{0:T(128)S(1)} %add_convert_fusion, f32[2048]{0:T(1024)S(1)} %bitcast.35), kind=kOutput, calls=%fused_computation.2 | convolution fusion | flops 101326848 | bytes 246016 | tf_op jit(solution)/shard_map/dot_general | solution.py:148
  (22 shorter events, 1.4 us)
Async XLA Ops:
  0.6 78.1 %copy-start = (f32[256,256]{1,0:T(8,128)S(1)}, f32[256,256]{1,0:T(8,128)}, u32[]{:S(2)}) copy-start(f32[256,256]{1,0:T(8,128)} %param.11) | copy-start | bytes 786436
  19.4 48.2 %copy-start.2 = (f32[2048,128]{1,0:T(8,128)S(1)}, f32[2048,128]{1,0:T(8,128)}, u32[]{:S(2)}) copy-start(f32[2048,128]{1,0:T(8,128)} %v_ref.1) | copy-start | bytes 3145732
  58.0 20.1 %copy-start.4 = (f32[57,128]{1,0:T(8,128)}, f32[57,128]{1,0:T(8,128)S(1)}, u32[]{:S(2)}) copy-start(f32[57,128]{1,0:T(8,128)S(1)} %reduce_sum.9) | copy-start | bytes 87556
  58.7 35.8 %copy-start.1 = (f32[2048,256]{1,0:T(8,128)S(1)}, f32[2048,256]{1,0:T(8,128)}, u32[]{:S(2)}) copy-start(f32[2048,256]{1,0:T(8,128)} %r_ref.1) | copy-start | bytes 6291460
  58.8 18.5 %all-to-all-start.1 = ((f32[32,9,128]{2,1,0:T(8,128)}), f32[32,9,128]{2,1,0:T(8,128)}, u32[]{:S(2)}, u32[]{:S(2)}) async-start(f32[32,9,128]{2,1,0:T(8,128)} %broadcast_in_dim.13), calls=%async_computation.1 | async-start | bytes 524288 | tf_op jit(solution)/shard_map/all_to_all | solution.py:124
  68.9 25.7 %copy-start.3 = (f32[2048,128]{0,1:T(8,128)S(1)}, f32[2048,128]{0,1:T(8,128)}, u32[]{:S(2)}) copy-start(f32[2048,128]{0,1:T(8,128)} %copy.27) | copy-start | bytes 3145732
  83.9 22.5 %all-to-all-start.2 = ((f32[16,26,128]{2,1,0:T(8,128)}), f32[16,26,128]{2,1,0:T(8,128)}, u32[]{:S(2)}, u32[]{:S(2)}) async-start(f32[16,26,128]{2,1,0:T(8,128)} %broadcast_in_dim.28), calls=%async_computation.2 | async-start | bytes 524288 | tf_op jit(solution)/shard_map/all_to_all | solution.py:138

commit v6 on v3

--- a/solution.py
+++ b/solution.py
@@ -10,7 +10,7 @@
 NT = 1024
 
 
-def send_kernel(taps, nrow, comp_here, events, idx_ref, w_ref, panel_ref, v_ref, r_ref, send_ref):
+def send_kernel(taps, nrow, comp_here, events, tab_ref, panel_ref, v_ref, r_ref, send_ref):
     width = v_ref.shape[1]
     halves = r_ref.shape[1] // width
     prow = panel_ref.shape[0] // nrow
@@ -20,8 +20,8 @@
     def tap_rows(c):
         acc_v = acc_r = None
         for t in range(taps):
-            i = idx_ref[c * taps + t]
-            w = w_ref[c * taps + t]
+            i = tab_ref[0, c * taps + t].astype(jnp.int32)
+            w = tab_ref[1, c * taps + t]
             v = w * v_ref[pl.ds(i, 1), :]
             r = w * r_ref[pl.ds(i, 1), :]
             acc_v = v if acc_v is None else acc_v + v
@@ -51,8 +51,12 @@
     taps = rows.shape[1]
     local = rows - first
     inside = (local >= 0) & (local < rows_here)
-    idx = jnp.clip(local, 0, rows_here - 1).reshape(-1)
-    w = jnp.where(inside, weights, 0.0).reshape(-1)
+    table = jnp.stack(
+        [
+            jnp.clip(local, 0, rows_here - 1).astype(jnp.float32).reshape(-1),
+            jnp.where(inside, weights, 0.0).reshape(-1),
+        ]
+    )
     halves = reflectors.shape[1] // width
     chunk = panel.shape[0] // nrow + comp_here * (1 + halves) + 1
     smem = pl.BlockSpec(memory_space=pltpu.SMEM)
@@ -60,9 +64,9 @@
     return pl.pallas_call(
         functools.partial(send_kernel, taps, nrow, comp_here, events),
         out_shape=jax.ShapeDtypeStruct((nrow, chunk, width), jnp.float32),
-        in_specs=[smem, smem, vmem, vmem, vmem],
+        in_specs=[smem, vmem, vmem, vmem],
         out_specs=vmem,
-    )(idx, w, panel, vectors, reflectors)
+    )(table, panel, vectors, reflectors)
 
 
 def mode_basis(freq, damp, times):
@@ -80,7 +84,7 @@
     mode_freq,
     mode_damp,
 ):
-    high = lax.Precision.HIGHEST
+    high = lax.Precision.HIGH
     nrow = lax.axis_size("row")
     ncol = lax.axis_size("col")
     rows_here, width = vectors.shape

time: 112 us -> 115 us (1.027)
  Pallas kernels: 8.3 us -> 14 us
  matrix products: 15.7 us -> 12.3 us
    pallas_call x1, Pallas kernels: 8.3 us -> 14 us  [build_send(): pl.pallas_call(functools.partial(send_kernel, taps, nrow, comp_here, even...]
    dot_general x1, matrix products: 5.93 us -> 4.31 us  [shards(): jnp.dot(reflectors.T, vectors, precision=high, preferred_element_type=jnp...]
  transfers between devices with their start and end apart: 2 -> 2, of which waited for: 2 -> 2; matrix products, arithmetic and copies ran while one was open for 6% -> 5% of each run, Pallas kernels for 0% -> 0%
where the time goes in v6:
time: 115 us; the launch traced here: 114 us
  blocking collectives  38.5 us (33%)
  starting transfers between devices  19.5 us (17%)
  waiting for transfers between devices  15.4 us (13%)
  Pallas kernels  14 us (12%)
  matrix products  12.3 us (11%)
  local copies, waits for them, and re-layouts  10.1 us (9%)
  other arithmetic  3.9 us (3%)
    all_to_all x1, blocking collectives, shards(): got = lax.all_to_all(send, 'row', 0, 0).sum(0)  38.5 us
    pallas_call x1, Pallas kernels, build_send(): pl.pallas_call(functools.partial(send_kernel, taps, nrow, comp_here, even...  14 us
    all_to_all x1, starting transfers between devices, shards(): lax.all_to_all(jnp.broadcast_to(block[None], (ncol,) + block.shape), 'col...  10.7 us
    all_to_all x1, starting transfers between devices, shards(): lax.all_to_all(jnp.broadcast_to(mine[None], (nrow,) + mine.shape), 'row',...  8.84 us
    all_to_all x1, waiting for transfers between devices, shards(): lax.all_to_all(jnp.broadcast_to(mine[None], (nrow,) + mine.shape), 'row',...  8.3 us
    all_to_all x1, waiting for transfers between devices, shards(): lax.all_to_all(jnp.broadcast_to(block[None], (ncol,) + block.shape), 'col...  7.12 us
    dot_general x1, matrix products, shards(): jnp.dot(reflectors.T, vectors, precision=high, preferred_element_type=jnp...  4.31 us
    unnamed x12, local copies, waits for them, and re-layouts  3.86 us
  transfers between devices with their start and end apart: 2, of which 2 were waited for; matrix products, arithmetic and copies ran while one was open for 5% of the time, Pallas kernels for 0%

profile of v6, /device:TPU:1, one launch (start us, length us, event | category | flops | bytes accessed | tf_op | source)
XLA Modules:
  0.0 114.5 jit_solution(9451215484045808595)
XLA Ops:
  0.7 0.8 clamp_convert_fusion
  1.8 0.8 maximum_select_fusion
  2.9 4.3 %fusion.14.panel_ref = f32[256,128]{1,0:T(8,128)} fusion(f32[2048,256]{1,0:T(8,128)} %r_ref.1, f32[2048,128]{1,0:T(8,128)} %v_ref.1), kind=kOutput, calls=%fused_computation.31 | convolution fusion | flops 402653184 | bytes 3276800 | tf_op jit(solution)/shard_map/dot_general | solution.py:99
  7.8 14.0 %shard_map.104 = f32[32,57,128]{2,1,0:T(8,128)} custom-call(f32[2,2080]{1,0:T(2,128)} %pad_maximum_fusion.tab_ref, f32[256,128]{1,0:T(8,128)} %fusion.14.panel_ref, f32[2048,128]{1,0:T(8,128)} %v_ref.1, f32[2048,256]{1,0:T(8,128)} %r_ref.1), custom_call_target="tpu_custom_call" | custom-call | tf_op jit(solution)/shard_map/pallas_call | solution.py:64
  21.8 38.5 %all_to_all.15 = f32[32,57,128]{2,1,0:T(8,128)S(1)} all-to-all(f32[32,57,128]{2,1,0:T(8,128)} %shard_map.104), channel_id=1, replica_groups=mesh['row'=32,'col'=16] {'row'}, dimensions={0} | all-to-all | bytes 1867776 | tf_op jit(solution)/shard_map/all_to_all | solution.py:114
  60.4 0.7 broadcast_in_dim.13
  61.2 8.8 %all-to-all-start.1 = ((f32[32,9,128]{2,1,0:T(8,128)}), f32[32,9,128]{2,1,0:T(8,128)}, u32[]{:S(2)}, u32[]{:S(2)}) async-start(f32[32,9,128]{2,1,0:T(8,128)} %broadcast_in_dim.13), calls=%async_computation.1 | async-start | bytes 524288 | tf_op jit(solution)/shard_map/all_to_all | solution.py:118
  70.0 1.3 %copy.27 = f32[2048,128]{0,1:T(8,128)} copy(f32[2048,128]{1,0:T(8,128)S(1)} %copy-done.2) | data formatting | bytes 2097152 | tf_op args[0]
  71.3 8.3 %all-to-all-done.1 = f32[32,9,128]{2,1,0:T(8,128)} async-done(((f32[32,9,128]{2,1,0:T(8,128)}), f32[32,9,128]{2,1,0:T(8,128)}, u32[]{:S(2)}, u32[]{:S(2)}) %all-to-all-start.1) | async-done | bytes 147488 | tf_op jit(solution)/shard_map/all_to_all | solution.py:118
  79.6 0.9 slice_reduce_fusion
  81.1 1.2 %fusion.13 = f32[128,256]{1,0:T(8,128)S(1)} fusion(f32[256,256]{1,0:T(8,128)S(1)} %copy-done, f32[32,9,128]{2,1,0:T(8,128)} %all-to-all-done.1), kind=kOutput, calls=%fused_computation.20 | convolution fusion | flops 50331648 | bytes 524288 | tf_op jit(solution)/shard_map/dot_general | solution.py:124
  82.3 0.8 convolution_subtract_fusion
  83.1 0.8 slice.57
  84.0 0.8 convolution_subtract_fusion.1
  84.8 0.7 pad_maximum_fusion.1
  85.5 0.7 broadcast_in_dim.28
  86.3 10.7 %all-to-all-start.2 = ((f32[16,26,128]{2,1,0:T(8,128)}), f32[16,26,128]{2,1,0:T(8,128)}, u32[]{:S(2)}, u32[]{:S(2)}) async-start(f32[16,26,128]{2,1,0:T(8,128)} %broadcast_in_dim.28), calls=%async_computation.2 | async-start | bytes 524288 | tf_op jit(solution)/shard_map/all_to_all | solution.py:132
  97.0 2.1 %fusion = f32[2048,128]{0,1:T(8,128)} fusion(f32[2048,128]{0,1:T(8,128)S(1)} %copy-done.3, f32[128,256]{1,0:T(8,128)S(1)} %fusion.13, f32[2048,256]{1,0:T(8,128)S(1)} %copy-done.1), kind=kOutput, calls=%fused_computation.1 | convolution fusion | flops 402915328 | bytes 4325376 | tf_op jit(solution)/shard_map/dot_general | solution.py:125
  99.1 2.5 %copy.30 = f32[2048,128]{1,0:T(8,128)} copy(f32[2048,128]{0,1:T(8,128)} %fusion) | data formatting | bytes 2097152
  101.7 7.1 %all-to-all-done.2 = f32[16,26,128]{2,1,0:T(8,128)} async-done(((f32[16,26,128]{2,1,0:T(8,128)}), f32[16,26,128]{2,1,0:T(8,128)}, u32[]{:S(2)}, u32[]{:S(2)}) %all-to-all-start.2) | async-done | bytes 213024 | tf_op jit(solution)/shard_map/all_to_all | solution.py:132
  108.8 0.9 slice_negate_fusion
  109.7 0.8 slice_bitcast_fusion.3
  110.6 0.9 copy_bitcast_fusion
  111.5 3.0 %convolution_multiply_fusion = f32[8,16,64]{2,1,0:T(8,128)} fusion(f32[16,2048]{1,0:T(8,128)S(1)} %copy_bitcast_fusion, f32[8,2048]{1,0:T(8,128)S(1)} %slice_bitcast_fusion.3, f32[2048]{0:T(1024)S(1)} %bitcast.38, f32[64]{0:T(128)S(1)} %add_convert_fusion, f32[2048]{0:T(1024)S(1)} %bitcast.37), kind=kOutput, calls=%fused_computation.2 | convolution fusion | flops 101326848 | bytes 246016 | tf_op jit(solution)/shard_map/dot_general | solution.py:142
  (23 shorter events, 2.0 us)
Async XLA Ops:
  0.6 80.5 %copy-start = (f32[256,256]{1,0:T(8,128)S(1)}, f32[256,256]{1,0:T(8,128)}, u32[]{:S(2)}) copy-start(f32[256,256]{1,0:T(8,128)} %param.11) | copy-start | bytes 786436
  21.8 48.2 %copy-start.2 = (f32[2048,128]{1,0:T(8,128)S(1)}, f32[2048,128]{1,0:T(8,128)}, u32[]{:S(2)}) copy-start(f32[2048,128]{1,0:T(8,128)} %v_ref.1) | copy-start | bytes 3145732
  60.4 20.1 %copy-start.4 = (f32[57,128]{1,0:T(8,128)}, f32[57,128]{1,0:T(8,128)S(1)}, u32[]{:S(2)}) copy-start(f32[57,128]{1,0:T(8,128)S(1)} %reduce_sum.9) | copy-start | bytes 87556
  61.1 35.8 %copy-start.1 = (f32[2048,256]{1,0:T(8,128)S(1)}, f32[2048,256]{1,0:T(8,128)}, u32[]{:S(2)}) copy-start(f32[2048,256]{1,0:T(8,128)} %r_ref.1) | copy-start | bytes 6291460
  61.2 18.5 %all-to-all-start.1 = ((f32[32,9,128]{2,1,0:T(8,128)}), f32[32,9,128]{2,1,0:T(8,128)}, u32[]{:S(2)}, u32[]{:S(2)}) async-start(f32[32,9,128]{2,1,0:T(8,128)} %broadcast_in_dim.13), calls=%async_computation.1 | async-start | bytes 524288 | tf_op jit(solution)/shard_map/all_to_all | solution.py:118
  71.3 25.7 %copy-start.3 = (f32[2048,128]{0,1:T(8,128)S(1)}, f32[2048,128]{0,1:T(8,128)}, u32[]{:S(2)}) copy-start(f32[2048,128]{0,1:T(8,128)} %copy.27) | copy-start | bytes 3145732
  86.3 22.5 %all-to-all-start.2 = ((f32[16,26,128]{2,1,0:T(8,128)}), f32[16,26,128]{2,1,0:T(8,128)}, u32[]{:S(2)}, u32[]{:S(2)}) async-start(f32[16,26,128]{2,1,0:T(8,128)} %broadcast_in_dim.28), calls=%async_computation.2 | async-start | bytes 524288 | tf_op jit(solution)/shard_map/all_to_all | solution.py:132

commit v7 on v3

--- a/solution.py
+++ b/solution.py
@@ -65,6 +65,54 @@
     )(idx, w, panel, vectors, reflectors)
 
 
+def post_kernel(nrow, comp_here, events, got_ref, whole_ref, t_ref, freq_ref, damp_ref, folded_ref, send_ref, extra_ref):
+    width = got_ref.shape[1]
+    pw = t_ref.shape[0]
+    prow = pw // nrow
+    hi = lax.Precision.HIGHEST
+    panel = whole_ref[:, pl.ds(0, prow), :].reshape(pw, width)
+    folded = jnp.dot(t_ref[...], panel, precision=hi, preferred_element_type=jnp.float32)
+    folded_ref[...] = folded
+    f_lo, f_hi = folded[:width], folded[width:]
+    vt = got_ref[pl.ds(prow, comp_here), :]
+    rt_lo = got_ref[pl.ds(prow + comp_here, comp_here, stride=2), :]
+    rt_hi = got_ref[pl.ds(prow + comp_here + 1, comp_here, stride=2), :]
+    receivers = vt - (
+        jnp.dot(rt_lo, f_lo, precision=hi, preferred_element_type=jnp.float32)
+        + jnp.dot(rt_hi, f_hi, precision=hi, preferred_element_type=jnp.float32)
+    )
+    for j in range(3 * events):
+        extra_ref[pl.ds(j, 1), :] = whole_ref[j, pl.ds(prow, 1), :]
+    st = extra_ref[pl.ds(0, events), :]
+    rs_lo = extra_ref[pl.ds(events, events, stride=2), :]
+    rs_hi = extra_ref[pl.ds(events + 1, events, stride=2), :]
+    sources = st - (
+        jnp.dot(rs_lo, f_lo, precision=hi, preferred_element_type=jnp.float32)
+        + jnp.dot(rs_hi, f_hi, precision=hi, preferred_element_type=jnp.float32)
+    )
+    for k in range(send_ref.shape[0]):
+        send_ref[k, pl.ds(0, comp_here), :] = receivers
+        send_ref[k, pl.ds(comp_here, events), :] = sources
+        send_ref[k, pl.ds(comp_here + events, 1), :] = freq_ref[...]
+        send_ref[k, pl.ds(comp_here + events + 1, 1), :] = damp_ref[...]
+
+
+def build_post(nrow, ncol, comp_here, events, got, whole, panel_factor, mode_freq, mode_damp):
+    width = got.shape[1]
+    pw = panel_factor.shape[0]
+    vmem = pl.BlockSpec(memory_space=pltpu.VMEM)
+    return pl.pallas_call(
+        functools.partial(post_kernel, nrow, comp_here, events),
+        out_shape=(
+            jax.ShapeDtypeStruct((pw, width), jnp.float32),
+            jax.ShapeDtypeStruct((ncol, comp_here + events + 2, width), jnp.float32),
+        ),
+        in_specs=[vmem] * 5,
+        out_specs=(vmem, vmem),
+        scratch_shapes=[pltpu.VMEM((3 * events, width), jnp.float32)],
+    )(got, whole, panel_factor, mode_freq.reshape(1, -1), mode_damp.reshape(1, -1))
+
+
 def mode_basis(freq, damp, times):
     return jnp.exp(-damp[:, None] * times[None, :]) * jnp.cos(freq[:, None] * times[None, :])
 
@@ -80,7 +128,7 @@
     mode_freq,
     mode_damp,
 ):
-    high = lax.Precision.HIGHEST
+    high = lax.Precision.HIGH
     nrow = lax.axis_size("row")
     ncol = lax.axis_size("col")
     rows_here, width = vectors.shape
@@ -108,24 +156,15 @@
     )
     prow = pw // nrow
     got = lax.all_to_all(send, "row", 0, 0).sum(0)
-    vt_here = got[prow:prow + comp_here]
-    rt_here = got[prow + comp_here:-1].reshape(comp_here, pw)
     mine = jnp.concatenate([got[:prow], got[-1:]], 0)
     whole = lax.all_to_all(jnp.broadcast_to(mine[None], (nrow,) + mine.shape), "row", 0, 0)
-    panel = whole[:, :prow].reshape(pw, width)
-    extra = whole[:, prow]
-    st_all = extra[:events]
-    rs_all = extra[events:events + events * pw // width].reshape(events, pw)
-
-    folded = jnp.dot(panel_factor, panel, precision=high, preferred_element_type=jnp.float32)
+    folded, block = build_post(
+        nrow, ncol, comp_here, events, got, whole, panel_factor, mode_freq, mode_damp
+    )
     rotated = vectors - jnp.dot(
         reflectors, folded, precision=high, preferred_element_type=jnp.float32
     )
-    receivers = vt_here - jnp.dot(rt_here, folded, precision=high, preferred_element_type=jnp.float32)
-    sources = st_all - jnp.dot(rs_all, folded, precision=high, preferred_element_type=jnp.float32)
-
-    block = jnp.concatenate([receivers, sources, mode_freq[None], mode_damp[None]], 0)
-    parts = lax.all_to_all(jnp.broadcast_to(block[None], (ncol,) + block.shape), "col", 0, 0)
+    parts = lax.all_to_all(block, "col", 0, 0)
     receivers = parts[:, :comp_here].transpose(1, 0, 2).reshape(comp_here, -1)
     sources = parts[:, comp_here:comp_here + events].transpose(1, 0, 2).reshape(events, -1)
     freq = parts[:, comp_here + events].reshape(-1)

time: 112 us -> 104 us (0.929)
  matrix products: 15.7 us -> 9.84 us
  local copies, waits for them, and re-layouts: 11.2 us -> 5.9 us
  Pallas kernels: 8.3 us -> 11.1 us
  waiting for transfers between devices: 14.3 us -> 16.2 us
  other arithmetic: 3.25 us -> 1.57 us
    dot_general x3 -> x0, matrix products: 3.05 us -> none  [the longest x1 1.29 us: shards(): jnp.dot(panel_factor, panel, precision=high, preferred_element_type=jnp.f...]
    pallas_call x0 -> x1, Pallas kernels: none -> 2.83 us  [build_post(): pl.pallas_call(functools.partial(post_kernel, nrow, comp_here, events), o...]
    all_to_all x1, waiting for transfers between devices: 6.04 us -> 7.85 us  [shards(): parts = lax.all_to_all(block, 'col', 0, 0)]
    mul x2, local copies, waits for them, and re-layouts: 1.76 us -> 0.02 us  [shards(): sources[:, None, :] * receivers[None, :, :]]
    slice x3 -> x0, local copies, waits for them, and re-layouts: 1.66 us -> none  [the longest x1 0.86 us: shards(): rs_all = extra[events:events + events * pw // width].reshape(events, pw)]
    dot_general x1, matrix products: 5.93 us -> 4.31 us  [shards(): jnp.dot(reflectors.T, vectors, precision=high, preferred_element_type=jnp...]
    unnamed x12 -> x10, local copies, waits for them, and re-layouts: 3.86 us -> 3.32 us
  transfers between devices with their start and end apart: 2 -> 2, of which waited for: 2 -> 2; matrix products, arithmetic and copies ran while one was open for 6% -> 5% of each run, Pallas kernels for 0% -> 0%
where the time goes in v7:
time: 104 us; the launch traced here: 103 us
  blocking collectives  38.5 us (37%)
  starting transfers between devices  19.3 us (19%)
  waiting for transfers between devices  16.2 us (16%)
  Pallas kernels  11.1 us (11%)
  matrix products  9.84 us (9%)
  local copies, waits for them, and re-layouts  5.9 us (6%)
  other arithmetic  1.57 us (2%)
    all_to_all x1, blocking collectives, shards(): got = lax.all_to_all(send, 'row', 0, 0).sum(0)  38.5 us
    all_to_all x1, starting transfers between devices, shards(): parts = lax.all_to_all(block, 'col', 0, 0)  10.7 us
    all_to_all x1, starting transfers between devices, shards(): lax.all_to_all(jnp.broadcast_to(mine[None], (nrow,) + mine.shape), 'row',...  8.58 us
    all_to_all x1, waiting for transfers between devices, shards(): lax.all_to_all(jnp.broadcast_to(mine[None], (nrow,) + mine.shape), 'row',...  8.34 us
    pallas_call x1, Pallas kernels, build_send(): pl.pallas_call(functools.partial(send_kernel, taps, nrow, comp_here, even...  8.3 us
    all_to_all x1, waiting for transfers between devices, shards(): parts = lax.all_to_all(block, 'col', 0, 0)  7.85 us
    dot_general x1, matrix products, shards(): jnp.dot(reflectors.T, vectors, precision=high, preferred_element_type=jnp...  4.31 us
    unnamed x10, local copies, waits for them, and re-layouts  3.32 us
  transfers between devices with their start and end apart: 2, of which 2 were waited for; matrix products, arithmetic and copies ran while one was open for 5% of the time, Pallas kernels for 0%

profile of v7, /device:TPU:1, one launch (start us, length us, event | category | flops | bytes accessed | tf_op | source)
XLA Modules:
  0.0 103.1 jit_solution(5251730552743421868)
XLA Ops:
  0.6 0.7 fusion.13
  1.4 0.1 copy.13
  1.5 0.8 min.12.idx_ref
  2.3 0.8 maximum_select_fusion
  3.0 0.1 copy.14
  3.2 0.8 select_n.9.w_ref
  4.0 4.3 %fusion.14.panel_ref = f32[256,128]{1,0:T(8,128)} fusion(f32[2048,256]{1,0:T(8,128)} %r_ref.1, f32[2048,128]{1,0:T(8,128)} %v_ref.1), kind=kOutput, calls=%fused_computation.24 | convolution fusion | flops 402653184 | bytes 3276800 | tf_op jit(solution)/shard_map/dot_general | solution.py:143
  8.3 8.3 %shard_map.104 = f32[32,57,128]{2,1,0:T(8,128)} custom-call(s32[2080]{0:T(1024)} %min.12.idx_ref, f32[2080]{0:T(1024)} %select_n.9.w_ref, f32[256,128]{1,0:T(8,128)} %fusion.14.panel_ref, f32[2048,128]{1,0:T(8,128)} %v_ref.1, f32[2048,256]{1,0:T(8,128)} %r_ref.1), custom_call_target="tpu_custom_call" | custom-call | tf_op jit(solution)/shard_map/pallas_call | solution.py:60
  16.6 38.5 %all_to_all.15 = f32[32,57,128]{2,1,0:T(8,128)S(1)} all-to-all(f32[32,57,128]{2,1,0:T(8,128)} %shard_map.104), channel_id=1, replica_groups=mesh['row'=32,'col'=16] {'row'}, dimensions={0} | all-to-all | bytes 1867776 | tf_op jit(solution)/shard_map/all_to_all | solution.py:158
  55.1 0.1 reduce_sum.9.got_ref
  55.1 0.0 copy-start.3
  55.1 0.0 copy-start
  55.2 0.7 broadcast_in_dim.7
  55.9 8.6 %all-to-all-start.1 = ((f32[32,9,128]{2,1,0:T(8,128)}), f32[32,9,128]{2,1,0:T(8,128)S(1)}, u32[]{:S(2)}, u32[]{:S(2)}) async-start(f32[32,9,128]{2,1,0:T(8,128)} %broadcast_in_dim.7), calls=%async_computation.1 | async-start | bytes 524288 | tf_op jit(solution)/shard_map/all_to_all | solution.py:160
  64.5 1.3 %copy.15 = f32[2048,128]{0,1:T(8,128)} copy(f32[2048,128]{1,0:T(8,128)S(1)} %copy-done.1) | data formatting | bytes 2097152 | tf_op args[0]
  65.8 8.3 %all-to-all-done.1.whole_ref = f32[32,9,128]{2,1,0:T(8,128)S(1)} async-done(((f32[32,9,128]{2,1,0:T(8,128)}), f32[32,9,128]{2,1,0:T(8,128)S(1)}, u32[]{:S(2)}, u32[]{:S(2)}) %all-to-all-start.1) | async-done | bytes 147488 | tf_op jit(solution)/shard_map/all_to_all | solution.py:160
  74.1 0.0 copy-done.3
  74.1 0.7 copy-done.2
  74.8 2.8 %shard_map.105 = (f32[256,128]{1,0:T(8,128)}, f32[16,26,128]{2,1,0:T(8,128)}) custom-call(f32[57,128]{1,0:T(8,128)} %copy-done.3, f32[32,9,128]{2,1,0:T(8,128)} %copy-done.2, f32[256,256]{1,0:T(8,128)} %t_ref.1, f32[1,128]{1,0:T(1,128)} %bitcast.27, f32[1,128]{1,0:T(1,128)} %bitcast.28), custom_call_target="tpu_custom_call" | custom-call | tf_op jit(solution)/shard_map/pallas_call | solution.py:104
  77.7 10.7 %all-to-all-start.2 = ((f32[16,26,128]{2,1,0:T(8,128)}), f32[16,26,128]{2,1,0:T(8,128)S(1)}, u32[]{:S(2)}, u32[]{:S(2)}) async-start(f32[16,26,128]{2,1,0:T(8,128)} %get-tuple-element.5), calls=%async_computation.2 | async-start | bytes 524288 | tf_op jit(solution)/shard_map/all_to_all | solution.py:167
  88.4 2.5 %fusion = f32[2048,128]{0,1:T(8,128)S(1)} fusion(f32[2048,128]{0,1:T(8,128)} %copy.15, f32[256,128]{1,0:T(8,128)} %get-tuple-element.4, f32[2048,256]{1,0:T(8,128)S(1)} %copy-done), kind=kOutput, calls=%fused_computation.1 | convolution fusion | flops 402915328 | bytes 4325376 | tf_op jit(solution)/shard_map/dot_general | solution.py:164
  90.9 1.3 %copy.17 = f32[2048,128]{1,0:T(8,128)} copy(f32[2048,128]{0,1:T(8,128)S(1)} %fusion) | data formatting | bytes 2097152
  92.2 7.9 %all-to-all-done.2 = f32[16,26,128]{2,1,0:T(8,128)S(1)} async-done(((f32[16,26,128]{2,1,0:T(8,128)}), f32[16,26,128]{2,1,0:T(8,128)S(1)}, u32[]{:S(2)}, u32[]{:S(2)}) %all-to-all-start.2) | async-done | bytes 213024 | tf_op jit(solution)/shard_map/all_to_all | solution.py:167
  100.1 3.0 %convolution_multiply_fusion = f32[8,16,64]{2,1,0:T(8,128)} fusion(f32[16,2048]{1,0:T(8,128)S(1)} %copy_bitcast_fusion, f32[8,2048]{1,0:T(8,128)S(1)} %slice_bitcast_fusion.1, f32[2048]{0:T(1024)S(1)} %bitcast.26, f32[64]{0:T(128)S(1)} %add_convert_fusion, f32[2048]{0:T(1024)S(1)} %bitcast.25), kind=kOutput, calls=%fused_computation.2 | convolution fusion | flops 101326848 | bytes 246016 | tf_op jit(solution)/shard_map/dot_general | solution.py:177
  (11 shorter events, 0.1 us)
Async XLA Ops:
  16.6 47.9 %copy-start.1 = (f32[2048,128]{1,0:T(8,128)S(1)}, f32[2048,128]{1,0:T(8,128)}, u32[]{:S(2)}) copy-start(f32[2048,128]{1,0:T(8,128)} %v_ref.1) | copy-start | bytes 3145732
  55.1 19.0 %copy-start.3 = (f32[57,128]{1,0:T(8,128)}, f32[57,128]{1,0:T(8,128)S(1)}, u32[]{:S(2)}) copy-start(f32[57,128]{1,0:T(8,128)S(1)} %reduce_sum.9.got_ref) | copy-start | bytes 87556
  55.1 33.3 %copy-start = (f32[2048,256]{1,0:T(8,128)S(1)}, f32[2048,256]{1,0:T(8,128)}, u32[]{:S(2)}) copy-start(f32[2048,256]{1,0:T(8,128)} %r_ref.1) | copy-start | bytes 6291460
  55.9 18.2 %all-to-all-start.1 = ((f32[32,9,128]{2,1,0:T(8,128)}), f32[32,9,128]{2,1,0:T(8,128)S(1)}, u32[]{:S(2)}, u32[]{:S(2)}) async-start(f32[32,9,128]{2,1,0:T(8,128)} %broadcast_in_dim.7), calls=%async_computation.1 | async-start | bytes 524288 | tf_op jit(solution)/shard_map/all_to_all | solution.py:160
  74.1 0.7 copy-start.2
  77.7 22.4 %all-to-all-start.2 = ((f32[16,26,128]{2,1,0:T(8,128)}), f32[16,26,128]{2,1,0:T(8,128)S(1)}, u32[]{:S(2)}, u32[]{:S(2)}) async-start(f32[16,26,128]{2,1,0:T(8,128)} %get-tuple-element.5), calls=%async_computation.2 | async-start | bytes 524288 | tf_op jit(solution)/shard_map/all_to_all | solution.py:167

commit v8 on v3

v8 whole, which is shorter than its diff:
```python
import functools

import jax
import jax.numpy as jnp
from jax import lax
from jax.experimental import pallas as pl
from jax.experimental.pallas import tpu as pltpu
from jax.sharding import PartitionSpec as P

NT = 1024


def tap_kernel(taps, nrow, comp_here, events, idx_ref, w_ref, rot_ref, send_ref):
    def tap_row(c):
        acc = None
        for t in range(taps):
            i = idx_ref[c * taps + t]
            w = w_ref[c * taps + t]
            v = w * rot_ref[pl.ds(i, 1), :]
            acc = v if acc is None else acc + v
        return acc

    ev = [tap_row(nrow * comp_here + e) for e in range(events)]

    def dest(j, carry):
        for cc in range(comp_here):
            send_ref[j, pl.ds(cc, 1), :] = tap_row(j * comp_here + cc)
        for e in range(events):
            send_ref[j, pl.ds(comp_here + e, 1), :] = ev[e]
        return carry

    lax.fori_loop(0, nrow, dest, 0)


def build_taps(rows, weights, first, nrow, comp_here, events, rotated):
    rows_here, width = rotated.shape
    taps = rows.shape[1]
    local = rows - first
    inside = (local >= 0) & (local < rows_here)
    idx = jnp.clip(local, 0, rows_here - 1).reshape(-1)
    w = jnp.where(inside, weights, 0.0).reshape(-1)
    smem = pl.BlockSpec(memory_space=pltpu.SMEM)
    vmem = pl.BlockSpec(memory_space=pltpu.VMEM)
    return pl.pallas_call(
        functools.partial(tap_kernel, taps, nrow, comp_here, events),
        out_shape=jax.ShapeDtypeStruct((nrow, comp_here + events, width), jnp.float32),
        in_specs=[smem, smem, vmem],
        out_specs=vmem,
    )(idx, w, rotated)


def mode_basis(freq, damp, times):
    return jnp.exp(-damp[:, None] * times[None, :]) * jnp.cos(freq[:, None] * times[None, :])


def shards(
    vectors,
    reflectors,
    panel_factor,
    station_rows,
    station_weights,
    event_rows,
    event_weights,
    mode_freq,
    mode_damp,
):
    high = lax.Precision.HIGH
    nrow = lax.axis_size("row")
    ncol = lax.axis_size("col")
    rows_here, width = vectors.shape
    pw = reflectors.shape[1]
    first = lax.axis_index("row") * rows_here
    comps = station_rows.shape[0]
    comp_here = comps // nrow
    events = event_rows.shape[0]
    samples = NT // ncol
    col = lax.axis_index("col")

    partial_panel = jnp.dot(
        reflectors.T, vectors, precision=high, preferred_element_type=jnp.float32
    )
    prow = pw // nrow
    mine = lax.all_to_all(partial_panel.reshape(nrow, prow, width), "row", 0, 0).sum(0)
    whole = lax.all_to_all(jnp.broadcast_to(mine[None], (nrow,) + mine.shape), "row", 0, 0)
    panel = whole.reshape(pw, width)
    folded = jnp.dot(panel_factor, panel, precision=high, preferred_element_type=jnp.float32)
    rotated = vectors - jnp.dot(
        reflectors, folded, precision=high, preferred_element_type=jnp.float32
    )
    send = build_taps(
        jnp.concatenate([station_rows, event_rows], 0),
        jnp.concatenate([station_weights, event_weights], 0),
        first,
        nrow,
        comp_here,
        events,
        rotated,
    )
    got = lax.all_to_all(send, "row", 0, 0).sum(0)
    block = jnp.concatenate([got, mode_freq[None], mode_damp[None]], 0)
    parts = lax.all_to_all(jnp.broadcast_to(block[None], (ncol,) + block.shape), "col", 0, 0)
    receivers = parts[:, :comp_here].transpose(1, 0, 2).reshape(comp_here, -1)
    sources = parts[:, comp_here:comp_here + events].transpose(1, 0, 2).reshape(events, -1)
    freq = parts[:, comp_here + events].reshape(-1)
    damp = parts[:, comp_here + events + 1].reshape(-1)
    times = (col * samples + jnp.arange(samples)).astype(jnp.float32)
    basis = mode_basis(freq, damp, times)

    factor = 1.0 / float(freq.shape[0]) ** 0.5
    amplitude = (sources[:, None, :] * receivers[None, :, :]).reshape(events * comp_here, -1)
    series = jnp.dot(amplitude, basis, precision=high, preferred_element_type=jnp.float32)
    seismograms = series.reshape(events, comp_here, samples) * factor
    return (rotated, seismograms)


def solution(mesh):
    placed = (P("row", "col"), P("row", None), P(), P(), P(), P(), P(), P("col"), P("col"))
    return jax.shard_map(
        shards,
        mesh=mesh,
        in_specs=placed,
        out_specs=(P("row", "col"), P(None, "row", "col")),
        check_vma=False,
    )
```

time: 112 us -> 92.5 us (0.83)
  matrix products: 15.7 us -> 9.24 us
  local copies, waits for them, and re-layouts: 11.2 us -> 4.86 us
  Pallas kernels: 8.3 us -> 4.39 us
  waiting for transfers between devices: 14.3 us -> 18.2 us
  starting transfers between devices: 19.5 us -> 16.8 us
  other arithmetic: 3.25 us -> 0.87 us
  blocking collectives: 38.5 us -> 36.8 us
    all_to_all x1, blocking collectives: 38.5 us -> 14.1 us  [shards(): got = lax.all_to_all(send, 'row', 0, 0).sum(0)]
    all_to_all x0 -> x1, blocking collectives: none -> 22.7 us  [shards(): lax.all_to_all(partial_panel.reshape(nrow, prow, width), 'row', 0, 0).sum(0)]
    all_to_all x1, waiting for transfers between devices: 6.04 us -> 11.7 us  [shards(): lax.all_to_all(jnp.broadcast_to(block[None], (ncol,) + block.shape), 'col...]
    all_to_all x1, starting transfers between devices: 8.84 us -> 3.86 us  [shards(): lax.all_to_all(jnp.broadcast_to(mine[None], (nrow,) + mine.shape), 'row',...]
    pallas_call x1, Pallas kernels: 8.3 us -> 4.39 us  [build_taps(): pl.pallas_call(functools.partial(tap_kernel, taps, nrow, comp_here, event...]
    dot_general x1, matrix products: 5.93 us -> 3.02 us  [shards(): jnp.dot(reflectors.T, vectors, precision=high, preferred_element_type=jnp...]
    unnamed x12, local copies, waits for them, and re-layouts: 3.86 us -> 1.61 us
    all_to_all x1, starting transfers between devices: 10.7 us -> 12.9 us  [shards(): lax.all_to_all(jnp.broadcast_to(block[None], (ncol,) + block.shape), 'col...]
  transfers between devices with their start and end apart: 2 -> 2, of which waited for: 2 -> 2; matrix products, arithmetic and copies ran while one was open for 6% -> 3% of each run, Pallas kernels for 0% -> 0%
where the time goes in v8:
time: 92.5 us; the launch traced here: 91.9 us
  blocking collectives  36.8 us (40%)
  waiting for transfers between devices  18.2 us (20%)
  starting transfers between devices  16.8 us (18%)
  matrix products  9.24 us (10%)
  local copies, waits for them, and re-layouts  4.86 us (5%)
  Pallas kernels  4.39 us (5%)
    all_to_all x1, blocking collectives, shards(): lax.all_to_all(partial_panel.reshape(nrow, prow, width), 'row', 0, 0).sum(0)  22.7 us
    all_to_all x1, blocking collectives, shards(): got = lax.all_to_all(send, 'row', 0, 0).sum(0)  14.1 us
    all_to_all x1, starting transfers between devices, shards(): lax.all_to_all(jnp.broadcast_to(block[None], (ncol,) + block.shape), 'col...  12.9 us
    all_to_all x1, waiting for transfers between devices, shards(): lax.all_to_all(jnp.broadcast_to(block[None], (ncol,) + block.shape), 'col...  11.7 us
    all_to_all x1, waiting for transfers between devices, shards(): lax.all_to_all(jnp.broadcast_to(mine[None], (nrow,) + mine.shape), 'row',...  6.49 us
    pallas_call x1, Pallas kernels, build_taps(): pl.pallas_call(functools.partial(tap_kernel, taps, nrow, comp_here, event...  4.39 us
    all_to_all x1, starting transfers between devices, shards(): lax.all_to_all(jnp.broadcast_to(mine[None], (nrow,) + mine.shape), 'row',...  3.86 us
    dot_general x1, matrix products, shards(): jnp.dot(reflectors.T, vectors, precision=high, preferred_element_type=jnp...  3.02 us
  transfers between devices with their start and end apart: 2, of which 2 were waited for; matrix products, arithmetic and copies ran while one was open for 3% of the time, Pallas kernels for 0%

profile of v8, /device:TPU:1, one launch (start us, length us, event | category | flops | bytes accessed | tf_op | source)
XLA Modules:
  0.0 91.9 jit_solution(8611386617648672058)
XLA Ops:
  0.6 0.0 copy-start
  0.7 0.0 copy-start.3
  0.7 0.0 copy-start.2
  0.7 1.6 %copy-done = f32[2048,256]{1,0:T(8,128)S(1)} copy-done((f32[2048,256]{1,0:T(8,128)S(1)}, f32[2048,256]{1,0:T(8,128)}, u32[]{:S(2)}) %copy-start) | copy-done | bytes 2097176
  2.3 3.0 %convolution_bitcast_fusion.1 = f32[32,8,128]{2,1,0:T(8,128)S(1)} fusion(f32[2048,256]{1,0:T(8,128)S(1)} %copy-done, f32[2048,128]{1,0:T(8,128)} %param.9), kind=kOutput, calls=%fused_computation.2 | convolution fusion | flops 402653184 | bytes 3276800 | tf_op jit(solution)/shard_map/dot_general | solution.py:79
  5.3 22.7 %all_to_all.20 = f32[32,8,128]{2,1,0:T(8,128)S(1)} all-to-all(f32[32,8,128]{2,1,0:T(8,128)S(1)} %convolution_bitcast_fusion.1), channel_id=1, replica_groups=mesh['row'=32,'col'=16] {'row'}, dimensions={0} | all-to-all | bytes 262144 | tf_op jit(solution)/shard_map/all_to_all | solution.py:83
  28.0 0.7 broadcast_in_dim.12
  28.7 3.9 %all-to-all-start.1 = ((f32[32,8,128]{2,1,0:T(8,128)}), f32[32,8,128]{2,1,0:T(8,128)S(1)}, u32[]{:S(2)}, u32[]{:S(2)}) async-start(f32[32,8,128]{2,1,0:T(8,128)} %broadcast_in_dim.12), calls=%async_computation.1 | async-start | bytes 262144 | tf_op jit(solution)/shard_map/all_to_all | solution.py:84
  32.5 0.0 copy-done.3
  32.5 0.0 copy-done.2
  32.6 0.1 copy.19
  32.7 0.8 min.12.idx_ref
  33.5 0.8 maximum_select_fusion
  34.3 0.1 copy.20
  34.4 0.8 select_n.9.w_ref
  35.2 6.5 %all-to-all-done.1 = f32[32,8,128]{2,1,0:T(8,128)S(1)} async-done(((f32[32,8,128]{2,1,0:T(8,128)}), f32[32,8,128]{2,1,0:T(8,128)S(1)}, u32[]{:S(2)}, u32[]{:S(2)}) %all-to-all-start.1) | async-done | bytes 131104 | tf_op jit(solution)/shard_map/all_to_all | solution.py:84
  41.7 1.2 %fusion.13 = f32[128,256]{1,0:T(8,128)S(1)} fusion(f32[256,256]{1,0:T(8,128)} %param.11, f32[32,8,128]{2,1,0:T(8,128)S(1)} %all-to-all-done.1), kind=kOutput, calls=%fused_computation.18 | convolution fusion | flops 50331648 | bytes 524288 | tf_op jit(solution)/shard_map/dot_general | solution.py:86
  42.9 2.0 %fusion.rot_ref = f32[2048,128]{1,0:T(8,128)} fusion(f32[2048,128]{1,0:T(8,128)S(1)} %copy-done.1, f32[128,256]{1,0:T(8,128)S(1)} %fusion.13, f32[2048,256]{1,0:T(8,128)S(1)} %copy-done), kind=kOutput, calls=%fused_computation.1 | convolution fusion | flops 402915328 | bytes 4325376 | tf_op jit(solution)/shard_map/dot_general | solution.py:87
  44.9 4.4 %shard_map.104 = f32[32,24,128]{2,1,0:T(8,128)} custom-call(s32[2080]{0:T(1024)} %min.12.idx_ref, f32[2080]{0:T(1024)} %select_n.9.w_ref, f32[2048,128]{1,0:T(8,128)} %fusion.rot_ref), custom_call_target="tpu_custom_call" | custom-call | tf_op jit(solution)/shard_map/pallas_call | solution.py:44
  49.3 14.1 %all_to_all.21 = f32[32,24,128]{2,1,0:T(8,128)S(1)} all-to-all(f32[32,24,128]{2,1,0:T(8,128)} %shard_map.104), channel_id=1, replica_groups=mesh['row'=32,'col'=16] {'row'}, dimensions={0} | all-to-all | bytes 786432 | tf_op jit(solution)/shard_map/all_to_all | solution.py:99
  63.5 0.7 broadcast_in_dim.28
  64.2 12.9 %all-to-all-start.3 = ((f32[16,26,128]{2,1,0:T(8,128)}), f32[16,26,128]{2,1,0:T(8,128)S(1)}, u32[]{:S(2)}, u32[]{:S(2)}) async-start(f32[16,26,128]{2,1,0:T(8,128)} %broadcast_in_dim.28), calls=%async_computation.3 | async-start | bytes 524288 | tf_op jit(solution)/shard_map/all_to_all | solution.py:101
  77.1 11.7 %all-to-all-done.3 = f32[16,26,128]{2,1,0:T(8,128)S(1)} async-done(((f32[16,26,128]{2,1,0:T(8,128)}), f32[16,26,128]{2,1,0:T(8,128)S(1)}, u32[]{:S(2)}, u32[]{:S(2)}) %all-to-all-start.3) | async-done | bytes 213024 | tf_op jit(solution)/shard_map/all_to_all | solution.py:101
  88.9 3.0 %convolution_multiply_fusion = f32[8,16,64]{2,1,0:T(8,128)} fusion(f32[16,2048]{1,0:T(8,128)S(1)} %copy_bitcast_fusion, f32[8,2048]{1,0:T(8,128)S(1)} %slice_bitcast_fusion.1, f32[2048]{0:T(1024)S(1)} %bitcast.32, f32[64]{0:T(128)S(1)} %add_convert_fusion, f32[2048]{0:T(1024)S(1)} %bitcast.31), kind=kOutput, calls=%fused_computation.3 | convolution fusion | flops 101326848 | bytes 246016 | tf_op jit(solution)/shard_map/dot_general | solution.py:111
  (14 shorter events, 0.1 us)
Async XLA Ops:
  0.6 1.6 %copy-start = (f32[2048,256]{1,0:T(8,128)S(1)}, f32[2048,256]{1,0:T(8,128)}, u32[]{:S(2)}) copy-start(f32[2048,256]{1,0:T(8,128)} %param.10) | copy-start | bytes 6291460
  0.6 42.3 %copy-start.1 = (f32[2048,128]{1,0:T(8,128)S(1)}, f32[2048,128]{1,0:T(8,128)}, u32[]{:S(2)}) copy-start(f32[2048,128]{1,0:T(8,128)} %param.9) | copy-start | bytes 3145732
  0.7 31.9 %copy-start.3 = (s32[8,4]{0,1:T(4,128)S(1)}, s32[8,4]{0,1:T(4,128)}, u32[]{:S(2)}) copy-start(s32[8,4]{0,1:T(4,128)} %param.14) | copy-start | bytes 388
  0.7 31.9 %copy-start.2 = (s32[512,4]{0,1:T(4,128)S(1)}, s32[512,4]{0,1:T(4,128)}, u32[]{:S(2)}) copy-start(s32[512,4]{0,1:T(4,128)} %param.12) | copy-start | bytes 24580
  28.7 13.0 %all-to-all-start.1 = ((f32[32,8,128]{2,1,0:T(8,128)}), f32[32,8,128]{2,1,0:T(8,128)S(1)}, u32[]{:S(2)}, u32[]{:S(2)}) async-start(f32[32,8,128]{2,1,0:T(8,128)} %broadcast_in_dim.12), calls=%async_computation.1 | async-start | bytes 262144 | tf_op jit(solution)/shard_map/all_to_all | solution.py:84
  44.9 18.6 %copy-start.4 = (f32[128]{0:T(128)S(1)}, f32[128]{0:T(128)}, u32[]{:S(2)}) copy-start(f32[128]{0:T(128)} %param.17) | copy-start | bytes 1540
  44.9 18.6 %copy-start.5 = (f32[128]{0:T(128)S(1)}, f32[128]{0:T(128)}, u32[]{:S(2)}) copy-start(f32[128]{0:T(128)} %param.16) | copy-start | bytes 1540
  64.2 24.6 %all-to-all-start.3 = ((f32[16,26,128]{2,1,0:T(8,128)}), f32[16,26,128]{2,1,0:T(8,128)S(1)}, u32[]{:S(2)}, u32[]{:S(2)}) async-start(f32[16,26,128]{2,1,0:T(8,128)} %broadcast_in_dim.28), calls=%async_computation.3 | async-start | bytes 524288 | tf_op jit(solution)/shard_map/all_to_all | solution.py:101

commit v9 on v8

--- a/solution.py
+++ b/solution.py
@@ -10,43 +10,63 @@
 NT = 1024
 
 
-def tap_kernel(taps, nrow, comp_here, events, idx_ref, w_ref, rot_ref, send_ref):
-    def tap_row(c):
-        acc = None
+def tap_kernel(taps, comp_here, idx_ref, w_ref, v_ref, r_ref, after_ref, tv_ref, tr_ref):
+    del after_ref
+    blocks = tv_ref.shape[0]
+    count = idx_ref.shape[0] // taps
+
+    def tap_rows(c):
+        acc_v = acc_r = None
         for t in range(taps):
             i = idx_ref[c * taps + t]
             w = w_ref[c * taps + t]
-            v = w * rot_ref[pl.ds(i, 1), :]
-            acc = v if acc is None else acc + v
-        return acc
+            v = w * v_ref[pl.ds(i, 1), :]
+            r = w * r_ref[pl.ds(i, 1), :]
+            acc_v = v if acc_v is None else acc_v + v
+            acc_r = r if acc_r is None else acc_r + r
+        return acc_v, acc_r
 
-    ev = [tap_row(nrow * comp_here + e) for e in range(events)]
-
-    def dest(j, carry):
+    def block(j, carry):
         for cc in range(comp_here):
-            send_ref[j, pl.ds(cc, 1), :] = tap_row(j * comp_here + cc)
-        for e in range(events):
-            send_ref[j, pl.ds(comp_here + e, 1), :] = ev[e]
+            acc_v, acc_r = tap_rows(j * comp_here + cc)
+            tv_ref[j, pl.ds(cc, 1), :] = acc_v
+            tr_ref[j, pl.ds(cc, 1), :] = acc_r
         return carry
 
-    lax.fori_loop(0, nrow, dest, 0)
+    lax.fori_loop(0, blocks - 1, block, 0)
+    last = blocks - 1
+    tv_ref[last] = jnp.zeros(tv_ref.shape[1:], jnp.float32)
+    tr_ref[last] = jnp.zeros(tr_ref.shape[1:], jnp.float32)
+    for e in range(count - last * comp_here):
+        acc_v, acc_r = tap_rows(last * comp_here + e)
+        tv_ref[last, pl.ds(e, 1), :] = acc_v
+        tr_ref[last, pl.ds(e, 1), :] = acc_r
 
 
-def build_taps(rows, weights, first, nrow, comp_here, events, rotated):
-    rows_here, width = rotated.shape
+def build_taps(rows, weights, first, comp_here, vectors, reflectors, after):
+    rows_here, width = vectors.shape
+    pw = reflectors.shape[1]
     taps = rows.shape[1]
+    blocks = -(-rows.shape[0] // comp_here)
     local = rows - first
     inside = (local >= 0) & (local < rows_here)
     idx = jnp.clip(local, 0, rows_here - 1).reshape(-1)
     w = jnp.where(inside, weights, 0.0).reshape(-1)
     smem = pl.BlockSpec(memory_space=pltpu.SMEM)
     vmem = pl.BlockSpec(memory_space=pltpu.VMEM)
+    taps_n = rows.shape[0] * taps
     return pl.pallas_call(
-        functools.partial(tap_kernel, taps, nrow, comp_here, events),
-        out_shape=jax.ShapeDtypeStruct((nrow, comp_here + events, width), jnp.float32),
-        in_specs=[smem, smem, vmem],
-        out_specs=vmem,
-    )(idx, w, rotated)
+        functools.partial(tap_kernel, taps, comp_here),
+        out_shape=(
+            jax.ShapeDtypeStruct((blocks, comp_here, width), jnp.float32),
+            jax.ShapeDtypeStruct((blocks, comp_here, pw), jnp.float32),
+        ),
+        in_specs=[smem, smem, vmem, vmem, vmem],
+        out_specs=(vmem, vmem),
+        cost_estimate=pl.CostEstimate(
+            flops=2 * taps_n * (width + pw), transcendentals=0, bytes_accessed=4 * taps_n * (width + pw)
+        ),
+    )(idx, w, vectors, reflectors, after)
 
 
 def mode_basis(freq, damp, times):
@@ -81,20 +101,31 @@
     )
     prow = pw // nrow
     mine = lax.all_to_all(partial_panel.reshape(nrow, prow, width), "row", 0, 0).sum(0)
+    tv, tr = build_taps(
+        jnp.concatenate([station_rows, event_rows], 0),
+        jnp.concatenate([station_weights, event_weights], 0),
+        first,
+        comp_here,
+        vectors,
+        reflectors,
+        mine,
+    )
     whole = lax.all_to_all(jnp.broadcast_to(mine[None], (nrow,) + mine.shape), "row", 0, 0)
     panel = whole.reshape(pw, width)
     folded = jnp.dot(panel_factor, panel, precision=high, preferred_element_type=jnp.float32)
+    blocks = tv.shape[0]
+    rot_taps = tv - jnp.dot(
+        tr.reshape(-1, pw), folded, precision=high, preferred_element_type=jnp.float32
+    ).reshape(blocks, comp_here, width)
+    send = jnp.concatenate(
+        [
+            rot_taps[:nrow],
+            jnp.broadcast_to(rot_taps[nrow, :events][None], (nrow, events, width)),
+        ],
+        1,
+    )
     rotated = vectors - jnp.dot(
         reflectors, folded, precision=high, preferred_element_type=jnp.float32
-    )
-    send = build_taps(
-        jnp.concatenate([station_rows, event_rows], 0),
-        jnp.concatenate([station_weights, event_weights], 0),
-        first,
-        nrow,
-        comp_here,
-        events,
-        rotated,
     )
     got = lax.all_to_all(send, "row", 0, 0).sum(0)
     block = jnp.concatenate([got, mode_freq[None], mode_damp[None]], 0)

time: 92.5 us -> 96.2 us (1.040)
  blocking collectives: 36.8 us -> 22.7 us
  starting transfers between devices: 16.8 us -> 25.7 us
  Pallas kernels: 4.39 us -> 7.9 us
  local copies, waits for them, and re-layouts: 4.86 us -> 7.69 us
  other arithmetic: 0.87 us -> 2.81 us
  matrix products: 9.24 us -> 10.9 us
  waiting for transfers between devices: 18.2 us -> 17 us
    all_to_all x1 -> x0, blocking collectives: 14.1 us -> none  [shards(): got = lax.all_to_all(send, 'row', 0, 0).sum(0)]
    all_to_all x0 -> x1, starting transfers between devices: none -> 9.47 us  [shards(): got = lax.all_to_all(send, 'row', 0, 0).sum(0)]
    all_to_all x0 -> x1, waiting for transfers between devices: none -> 8.92 us  [shards(): got = lax.all_to_all(send, 'row', 0, 0).sum(0)]
    all_to_all x1, waiting for transfers between devices: 6.49 us -> 0.01 us  [shards(): lax.all_to_all(jnp.broadcast_to(mine[None], (nrow,) + mine.shape), 'row',...]
    all_to_all x1, waiting for transfers between devices: 11.7 us -> 8.09 us  [shards(): lax.all_to_all(jnp.broadcast_to(block[None], (ncol,) + block.shape), 'col...]
    pallas_call x1, Pallas kernels: 4.39 us -> 7.9 us  [build_taps(): pl.pallas_call(functools.partial(tap_kernel, taps, comp_here), out_shape=...]
    mul x2, local copies, waits for them, and re-layouts: 0.02 us -> 1.76 us  [shards(): sources[:, None, :] * receivers[None, :, :]]
    dot_general x0 -> x1, matrix products: none -> 1.5 us  [shards(): jnp.dot(tr.reshape(-1, pw), folded, precision=high, preferred_element_typ...]
  transfers between devices with their start and end apart: 2 -> 3, of which waited for: 2 -> 2; matrix products, arithmetic and copies ran while one was open for 3% -> 7% of each run, Pallas kernels for 0% -> 8%
where the time goes in v9:
time: 96.2 us; the launch traced here: 95.5 us
  starting transfers between devices  25.7 us (27%)
  blocking collectives  22.7 us (24%)
  waiting for transfers between devices  17 us (18%)
  matrix products  10.9 us (11%)
  Pallas kernels  7.9 us (8%)
  local copies, waits for them, and re-layouts  7.69 us (8%)
  other arithmetic  2.81 us (3%)
    all_to_all x1, blocking collectives, shards(): lax.all_to_all(partial_panel.reshape(nrow, prow, width), 'row', 0, 0).sum(0)  22.7 us
    all_to_all x1, starting transfers between devices, shards(): lax.all_to_all(jnp.broadcast_to(block[None], (ncol,) + block.shape), 'col...  12.4 us
    all_to_all x1, starting transfers between devices, shards(): got = lax.all_to_all(send, 'row', 0, 0).sum(0)  9.47 us
    all_to_all x1, waiting for transfers between devices, shards(): got = lax.all_to_all(send, 'row', 0, 0).sum(0)  8.92 us
    all_to_all x1, waiting for transfers between devices, shards(): lax.all_to_all(jnp.broadcast_to(block[None], (ncol,) + block.shape), 'col...  8.09 us
    pallas_call x1, Pallas kernels, build_taps(): pl.pallas_call(functools.partial(tap_kernel, taps, comp_here), out_shape=...  7.9 us
    all_to_all x1, starting transfers between devices, shards(): lax.all_to_all(jnp.broadcast_to(mine[None], (nrow,) + mine.shape), 'row',...  3.85 us
    dot_general x1, matrix products, shards(): jnp.dot(reflectors.T, vectors, precision=high, preferred_element_type=jnp...  3.72 us
  transfers between devices with their start and end apart: 3, of which 2 were waited for; matrix products, arithmetic and copies ran while one was open for 7% of the time, Pallas kernels for 8%

profile of v9, /device:TPU:1, one launch (start us, length us, event | category | flops | bytes accessed | tf_op | source)
XLA Modules:
  0.0 95.5 jit_solution(15304958949959091163)
XLA Ops:
  0.7 3.7 %convolution_bitcast_fusion.1 = f32[32,8,128]{2,1,0:T(8,128)S(1)} fusion(f32[2048,256]{1,0:T(8,128)} %r_ref.1, f32[2048,128]{1,0:T(8,128)} %v_ref.1), kind=kOutput, calls=%fused_computation.3 | convolution fusion | flops 402653184 | bytes 3276800 | tf_op jit(solution)/shard_map/dot_general | solution.py:99
  4.4 22.7 %all_to_all.20 = f32[32,8,128]{2,1,0:T(8,128)S(1)} all-to-all(f32[32,8,128]{2,1,0:T(8,128)S(1)} %convolution_bitcast_fusion.1), channel_id=1, replica_groups=mesh['row'=32,'col'=16] {'row'}, dimensions={0} | all-to-all | bytes 262144 | tf_op jit(solution)/shard_map/all_to_all | solution.py:103
  27.1 0.7 broadcast_in_dim.16
  27.8 3.9 %all-to-all-start.1 = ((f32[32,8,128]{2,1,0:T(8,128)}), f32[32,8,128]{2,1,0:T(8,128)S(1)}, u32[]{:S(2)}, u32[]{:S(2)}) async-start(f32[32,8,128]{2,1,0:T(8,128)} %broadcast_in_dim.16), calls=%async_computation.1 | async-start | bytes 262144 | tf_op jit(solution)/shard_map/all_to_all | solution.py:113
  31.7 0.1 copy.22
  31.8 0.8 min.12.idx_ref
  32.8 0.8 select_n.9.w_ref
  33.6 7.9 %shard_map.104 = (f32[33,16,128]{2,1,0:T(8,128)}, f32[33,16,256]{2,1,0:T(8,128)}) custom-call(s32[2080]{0:T(1024)} %min.12.idx_ref, f32[2080]{0:T(1024)} %select_n.9.w_ref, f32[2048,128]{1,0:T(8,128)} %v_ref.1, f32[2048,256]{1,0:T(8,128)} %r_ref.1, f32[8,128]{1,0:T(8,128)} %copy-done.3), custom_call_target="tpu_custom_call" | custom-call | flops 1597440 | bytes 3194880 | tf_op jit(solution)/shard_map/pallas_call | solution.py:58
  41.5 0.3 fusion.14
  41.8 1.5 %convolution_subtract_fusion = f32[33,16,128]{2,1,0:T(8,128)S(1)} fusion(f32[33,16,128]{2,1,0:T(8,128)} %get-tuple-element.4, f32[33,16,256]{2,1,0:T(8,128)} %get-tuple-element.5, f32[128,256]{1,0:T(8,128)S(1)} %fusion.14), kind=kOutput, calls=%fused_computation.2 | convolution fusion | flops 103876608 | bytes 1212416 | tf_op jit(solution)/shard_map/dot_general | solution.py:117
  43.4 0.8 pad_maximum_fusion
  44.1 9.5 %all-to-all-start.2 = ((f32[32,24,128]{2,1,0:T(8,128)}), f32[32,24,128]{2,1,0:T(8,128)}, u32[]{:S(2)}, u32[]{:S(2)}) async-start(f32[32,24,128]{2,1,0:T(8,128)} %pad_maximum_fusion), calls=%async_computation.2 | async-start | bytes 786432 | tf_op jit(solution)/shard_map/all_to_all | solution.py:130
  53.6 1.3 %copy.21 = f32[2048,128]{0,1:T(8,128)} copy(f32[2048,128]{1,0:T(8,128)S(1)} %copy-done.2) | data formatting | bytes 2097152 | tf_op args[0]
  54.9 8.9 %all-to-all-done.2 = f32[32,24,128]{2,1,0:T(8,128)} async-done(((f32[32,24,128]{2,1,0:T(8,128)}), f32[32,24,128]{2,1,0:T(8,128)}, u32[]{:S(2)}, u32[]{:S(2)}) %all-to-all-start.2) | async-done | bytes 393248 | tf_op jit(solution)/shard_map/all_to_all | solution.py:130
  63.9 1.0 %reduce_sum.19 = f32[24,128]{1,0:T(8,128)S(1)} reduce(f32[32,24,128]{2,1,0:T(8,128)} %all-to-all-done.2, f32[]{:T(128)} %constant.9.clone.1), dimensions={0}, to_apply=%region_1.2 | reduce | flops 95232 | bytes 405508 | tf_op jit(solution)/shard_map/reduce_sum | solution.py:130
  64.9 0.7 broadcast_in_dim.37
  65.7 12.4 %all-to-all-start.3 = ((f32[16,26,128]{2,1,0:T(8,128)}), f32[16,26,128]{2,1,0:T(8,128)}, u32[]{:S(2)}, u32[]{:S(2)}) async-start(f32[16,26,128]{2,1,0:T(8,128)} %broadcast_in_dim.37), calls=%async_computation.3 | async-start | bytes 524288 | tf_op jit(solution)/shard_map/all_to_all | solution.py:132
  78.0 2.4 %fusion = f32[2048,128]{0,1:T(8,128)S(1)} fusion(f32[2048,128]{0,1:T(8,128)} %copy.21, f32[128,256]{1,0:T(8,128)S(1)} %fusion.14, f32[2048,256]{1,0:T(8,128)S(1)} %copy-done.1), kind=kOutput, calls=%fused_computation.1 | convolution fusion | flops 402915328 | bytes 4325376 | tf_op jit(solution)/shard_map/dot_general | solution.py:127
  80.4 1.3 %copy.25 = f32[2048,128]{1,0:T(8,128)} copy(f32[2048,128]{0,1:T(8,128)S(1)} %fusion) | data formatting | bytes 2097152
  81.8 8.1 %all-to-all-done.3 = f32[16,26,128]{2,1,0:T(8,128)} async-done(((f32[16,26,128]{2,1,0:T(8,128)}), f32[16,26,128]{2,1,0:T(8,128)}, u32[]{:S(2)}, u32[]{:S(2)}) %all-to-all-start.3) | async-done | bytes 213024 | tf_op jit(solution)/shard_map/all_to_all | solution.py:132
  89.8 0.9 slice_negate_fusion
  90.8 0.8 slice_bitcast_fusion.1
  91.6 0.9 copy_bitcast_fusion
  92.5 3.0 %convolution_multiply_fusion = f32[8,16,64]{2,1,0:T(8,128)} fusion(f32[16,2048]{1,0:T(8,128)S(1)} %copy_bitcast_fusion, f32[8,2048]{1,0:T(8,128)S(1)} %slice_bitcast_fusion.1, f32[2048]{0:T(1024)S(1)} %bitcast.38, f32[64]{0:T(128)S(1)} %add_convert_fusion, f32[2048]{0:T(1024)S(1)} %bitcast.37), kind=kOutput, calls=%fused_computation.4 | convolution fusion | flops 101326848 | bytes 246016 | tf_op jit(solution)/shard_map/dot_general | solution.py:142
  (30 shorter events, 0.3 us)
Async XLA Ops:
  0.6 40.8 %copy-start = (f32[256,256]{1,0:T(8,128)S(1)}, f32[256,256]{1,0:T(8,128)}, u32[]{:S(2)}) copy-start(f32[256,256]{1,0:T(8,128)} %param.11) | copy-start | bytes 786436
  0.6 31.0 %copy-start.6 = (s32[8,4]{0,1:T(4,128)S(1)}, s32[8,4]{0,1:T(4,128)}, u32[]{:S(2)}) copy-start(s32[8,4]{0,1:T(4,128)} %param.14) | copy-start | bytes 388
  0.7 31.0 %copy-start.4 = (s32[512,4]{0,1:T(4,128)S(1)}, s32[512,4]{0,1:T(4,128)}, u32[]{:S(2)}) copy-start(s32[512,4]{0,1:T(4,128)} %param.12) | copy-start | bytes 24580
  0.7 31.9 %copy-start.7 = (f32[8,4]{0,1:T(4,128)S(1)}, f32[8,4]{0,1:T(4,128)}, u32[]{:S(2)}) copy-start(f32[8,4]{0,1:T(4,128)} %param.15) | copy-start | bytes 388
  0.7 31.9 %copy-start.5 = (f32[512,4]{0,1:T(4,128)S(1)}, f32[512,4]{0,1:T(4,128)}, u32[]{:S(2)}) copy-start(f32[512,4]{0,1:T(4,128)} %param.13) | copy-start | bytes 24580
  27.1 6.4 %copy-start.3 = (f32[8,128]{1,0:T(8,128)}, f32[8,128]{1,0:T(8,128)S(1)}, u32[]{:S(2)}) copy-start(f32[8,128]{1,0:T(8,128)S(1)} %reduce_sum.18.after_ref) | copy-start | bytes 12292
  27.8 13.7 %all-to-all-start.1 = ((f32[32,8,128]{2,1,0:T(8,128)}), f32[32,8,128]{2,1,0:T(8,128)S(1)}, u32[]{:S(2)}, u32[]{:S(2)}) async-start(f32[32,8,128]{2,1,0:T(8,128)} %broadcast_in_dim.16), calls=%async_computation.1 | async-start | bytes 262144 | tf_op jit(solution)/shard_map/all_to_all | solution.py:113
  41.5 12.2 %copy-start.2 = (f32[2048,128]{1,0:T(8,128)S(1)}, f32[2048,128]{1,0:T(8,128)}, u32[]{:S(2)}) copy-start(f32[2048,128]{1,0:T(8,128)} %v_ref.1) | copy-start | bytes 3145732
  43.3 21.6 %copy-start.8 = (f32[128]{0:T(128)S(1)}, f32[128]{0:T(128)}, u32[]{:S(2)}) copy-start(f32[128]{0:T(128)} %param.17) | copy-start | bytes 1540
  43.3 21.6 %copy-start.9 = (f32[128]{0:T(128)S(1)}, f32[128]{0:T(128)}, u32[]{:S(2)}) copy-start(f32[128]{0:T(128)} %param.16) | copy-start | bytes 1540
  44.1 33.9 %copy-start.1 = (f32[2048,256]{1,0:T(8,128)S(1)}, f32[2048,256]{1,0:T(8,128)}, u32[]{:S(2)}) copy-start(f32[2048,256]{1,0:T(8,128)} %r_ref.1) | copy-start | bytes 6291460
  44.1 19.7 %all-to-all-start.2 = ((f32[32,24,128]{2,1,0:T(8,128)}), f32[32,24,128]{2,1,0:T(8,128)}, u32[]{:S(2)}, u32[]{:S(2)}) async-start(f32[32,24,128]{2,1,0:T(8,128)} %pad_maximum_fusion), calls=%async_computation.2 | async-start | bytes 786432 | tf_op jit(solution)/shard_map/all_to_all | solution.py:130
  65.7 24.2 %all-to-all-start.3 = ((f32[16,26,128]{2,1,0:T(8,128)}), f32[16,26,128]{2,1,0:T(8,128)}, u32[]{:S(2)}, u32[]{:S(2)}) async-start(f32[16,26,128]{2,1,0:T(8,128)} %broadcast_in_dim.37), calls=%async_computation.3 | async-start | bytes 524288 | tf_op jit(solution)/shard_map/all_to_all | solution.py:132

commit v10 on v9

--- a/solution.py
+++ b/solution.py
@@ -124,10 +124,11 @@
         ],
         1,
     )
-    rotated = vectors - jnp.dot(
+    got = lax.all_to_all(send, "row", 0, 0).sum(0)
+    held, got = lax.optimization_barrier((vectors, got))
+    rotated = held - jnp.dot(
         reflectors, folded, precision=high, preferred_element_type=jnp.float32
     )
-    got = lax.all_to_all(send, "row", 0, 0).sum(0)
     block = jnp.concatenate([got, mode_freq[None], mode_damp[None]], 0)
     parts = lax.all_to_all(jnp.broadcast_to(block[None], (ncol,) + block.shape), "col", 0, 0)
     receivers = parts[:, :comp_here].transpose(1, 0, 2).reshape(comp_here, -1)

time: 96.2 us -> 96.9 us (level)
    all_to_all x1, waiting for transfers between devices: 8.09 us -> 6.76 us  [shards(): lax.all_to_all(jnp.broadcast_to(block[None], (ncol,) + block.shape), 'col...]
    unnamed x22 -> x19, local copies, waits for them, and re-layouts: 2.66 us -> 1.35 us
    all_to_all x1, waiting for transfers between devices: 8.92 us -> 10.2 us  [shards(): got = lax.all_to_all(send, 'row', 0, 0).sum(0)]
    optimization_barrier x0 -> x1, local copies, waits for them, and re-layouts: none -> 1.31 us  [shards(): held, got = lax.optimization_barrier((vectors, got))]
where the time goes in v10:
time: 96.9 us; the launch traced here: 96.3 us
  starting transfers between devices  25.7 us (27%)
  blocking collectives  22.7 us (23%)
  waiting for transfers between devices  17 us (18%)
  matrix products  11 us (11%)
  Pallas kernels  7.9 us (8%)
  local copies, waits for them, and re-layouts  7.68 us (8%)
  other arithmetic  3.47 us (4%)
    all_to_all x1, blocking collectives, shards(): lax.all_to_all(partial_panel.reshape(nrow, prow, width), 'row', 0, 0).sum(0)  22.7 us
    all_to_all x1, starting transfers between devices, shards(): lax.all_to_all(jnp.broadcast_to(block[None], (ncol,) + block.shape), 'col...  12.4 us
    all_to_all x1, waiting for transfers between devices, shards(): got = lax.all_to_all(send, 'row', 0, 0).sum(0)  10.2 us
    all_to_all x1, starting transfers between devices, shards(): got = lax.all_to_all(send, 'row', 0, 0).sum(0)  9.47 us
    pallas_call x1, Pallas kernels, build_taps(): pl.pallas_call(functools.partial(tap_kernel, taps, comp_here), out_shape=...  7.9 us
    all_to_all x1, waiting for transfers between devices, shards(): lax.all_to_all(jnp.broadcast_to(block[None], (ncol,) + block.shape), 'col...  6.76 us
    all_to_all x1, starting transfers between devices, shards(): lax.all_to_all(jnp.broadcast_to(mine[None], (nrow,) + mine.shape), 'row',...  3.85 us
    dot_general x1, matrix products, shards(): jnp.dot(reflectors.T, vectors, precision=high, preferred_element_type=jnp...  3.72 us
  transfers between devices with their start and end apart: 3, of which 2 were waited for; matrix products, arithmetic and copies ran while one was open for 7% of the time, Pallas kernels for 8%

profile of v10, /device:TPU:1, one launch (start us, length us, event | category | flops | bytes accessed | tf_op | source)
XLA Modules:
  0.0 96.3 jit_solution(5453945947294750841)
XLA Ops:
  0.7 3.7 %convolution_bitcast_fusion.1 = f32[32,8,128]{2,1,0:T(8,128)S(1)} fusion(f32[2048,256]{1,0:T(8,128)} %r_ref.1, f32[2048,128]{1,0:T(8,128)} %v_ref.1), kind=kOutput, calls=%fused_computation.3 | convolution fusion | flops 402653184 | bytes 3276800 | tf_op jit(solution)/shard_map/dot_general | solution.py:99
  4.4 22.7 %all_to_all.20 = f32[32,8,128]{2,1,0:T(8,128)S(1)} all-to-all(f32[32,8,128]{2,1,0:T(8,128)S(1)} %convolution_bitcast_fusion.1), channel_id=1, replica_groups=mesh['row'=32,'col'=16] {'row'}, dimensions={0} | all-to-all | bytes 262144 | tf_op jit(solution)/shard_map/all_to_all | solution.py:103
  27.1 0.7 broadcast_in_dim.32
  27.8 3.8 %all-to-all-start.1 = ((f32[32,8,128]{2,1,0:T(8,128)}), f32[32,8,128]{2,1,0:T(8,128)S(1)}, u32[]{:S(2)}, u32[]{:S(2)}) async-start(f32[32,8,128]{2,1,0:T(8,128)} %broadcast_in_dim.32), calls=%async_computation.1 | async-start | bytes 262144 | tf_op jit(solution)/shard_map/all_to_all | solution.py:113
  31.9 0.8 min.12.idx_ref
  32.8 0.8 select_n.9.w_ref
  33.6 7.9 %shard_map.104 = (f32[33,16,128]{2,1,0:T(8,128)}, f32[33,16,256]{2,1,0:T(8,128)}) custom-call(s32[2080]{0:T(1024)} %min.12.idx_ref, f32[2080]{0:T(1024)} %select_n.9.w_ref, f32[2048,128]{1,0:T(8,128)} %v_ref.1, f32[2048,256]{1,0:T(8,128)} %r_ref.1, f32[8,128]{1,0:T(8,128)} %copy-done.3), custom_call_target="tpu_custom_call" | custom-call | flops 1597440 | bytes 3194880 | tf_op jit(solution)/shard_map/pallas_call | solution.py:58
  41.5 0.3 fusion.14
  41.8 1.6 %convolution_subtract_fusion = f32[33,16,128]{2,1,0:T(8,128)S(1)} fusion(f32[33,16,128]{2,1,0:T(8,128)} %get-tuple-element.6, f32[33,16,256]{2,1,0:T(8,128)} %get-tuple-element.7, f32[128,256]{1,0:T(8,128)S(1)} %fusion.14), kind=kOutput, calls=%fused_computation.2 | convolution fusion | flops 103876608 | bytes 1212416 | tf_op jit(solution)/shard_map/dot_general | solution.py:117
  43.4 0.8 pad_maximum_fusion
  44.2 9.5 %all-to-all-start.2 = ((f32[32,24,128]{2,1,0:T(8,128)}), f32[32,24,128]{2,1,0:T(8,128)}, u32[]{:S(2)}, u32[]{:S(2)}) async-start(f32[32,24,128]{2,1,0:T(8,128)} %pad_maximum_fusion), calls=%async_computation.2 | async-start | bytes 786432 | tf_op jit(solution)/shard_map/all_to_all | solution.py:127
  53.7 10.2 %all-to-all-done.2 = f32[32,24,128]{2,1,0:T(8,128)} async-done(((f32[32,24,128]{2,1,0:T(8,128)}), f32[32,24,128]{2,1,0:T(8,128)}, u32[]{:S(2)}, u32[]{:S(2)}) %all-to-all-start.2) | async-done | bytes 393248 | tf_op jit(solution)/shard_map/all_to_all | solution.py:127
  63.9 1.0 %reduce_sum.19 = f32[24,128]{1,0:T(8,128)S(1)} reduce(f32[32,24,128]{2,1,0:T(8,128)} %all-to-all-done.2, f32[]{:T(128)} %constant.6.clone.1), dimensions={0}, to_apply=%region_1.2 | reduce | flops 95232 | bytes 405508 | tf_op jit(solution)/shard_map/reduce_sum | solution.py:127
  65.0 0.7 pad_maximum_fusion.1
  65.7 0.7 broadcast_in_dim.37
  66.4 12.4 %all-to-all-start.3 = ((f32[16,26,128]{2,1,0:T(8,128)}), f32[16,26,128]{2,1,0:T(8,128)}, u32[]{:S(2)}, u32[]{:S(2)}) async-start(f32[16,26,128]{2,1,0:T(8,128)} %broadcast_in_dim.37), calls=%async_computation.3 | async-start | bytes 524288 | tf_op jit(solution)/shard_map/all_to_all | solution.py:133
  78.8 1.3 %copy.23 = f32[2048,128]{0,1:T(8,128)} copy(f32[2048,128]{1,0:T(8,128)S(1)} %copy-done.2) | data formatting | bytes 2097152 | tf_op jit(solution)/shard_map/optimization_barrier | solution.py:128
  80.1 2.4 %fusion = f32[2048,128]{0,1:T(8,128)S(1)} fusion(f32[2048,128]{0,1:T(8,128)} %copy.23, f32[128,256]{1,0:T(8,128)S(1)} %fusion.14, f32[2048,256]{1,0:T(8,128)S(1)} %copy-done.1), kind=kOutput, calls=%fused_computation.1 | convolution fusion | flops 402915328 | bytes 4325376 | tf_op jit(solution)/shard_map/dot_general | solution.py:129
  82.5 1.3 %copy.25 = f32[2048,128]{1,0:T(8,128)} copy(f32[2048,128]{0,1:T(8,128)S(1)} %fusion) | data formatting | bytes 2097152
  83.8 6.8 %all-to-all-done.3 = f32[16,26,128]{2,1,0:T(8,128)} async-done(((f32[16,26,128]{2,1,0:T(8,128)}), f32[16,26,128]{2,1,0:T(8,128)}, u32[]{:S(2)}, u32[]{:S(2)}) %all-to-all-start.3) | async-done | bytes 213024 | tf_op jit(solution)/shard_map/all_to_all | solution.py:133
  90.6 0.9 copy_bitcast_fusion
  91.5 0.8 slice_bitcast_fusion.1
  92.3 0.9 slice_negate_fusion
  93.3 3.0 %convolution_multiply_fusion = f32[8,16,64]{2,1,0:T(8,128)} fusion(f32[16,2048]{1,0:T(8,128)S(1)} %copy_bitcast_fusion, f32[8,2048]{1,0:T(8,128)S(1)} %slice_bitcast_fusion.1, f32[2048]{0:T(1024)S(1)} %bitcast.38, f32[64]{0:T(128)S(1)} %add_convert_fusion, f32[2048]{0:T(1024)S(1)} %bitcast.37), kind=kOutput, calls=%fused_computation.4 | convolution fusion | flops 101326848 | bytes 246016 | tf_op jit(solution)/shard_map/dot_general | solution.py:143
  (28 shorter events, 0.4 us)
Async XLA Ops:
  0.6 40.8 %copy-start = (f32[256,256]{1,0:T(8,128)S(1)}, f32[256,256]{1,0:T(8,128)}, u32[]{:S(2)}) copy-start(f32[256,256]{1,0:T(8,128)} %param.11) | copy-start | bytes 786436
  0.6 31.0 %copy-start.6 = (s32[8,4]{0,1:T(4,128)S(1)}, s32[8,4]{0,1:T(4,128)}, u32[]{:S(2)}) copy-start(s32[8,4]{0,1:T(4,128)} %param.14) | copy-start | bytes 388
  0.7 31.0 %copy-start.4 = (s32[512,4]{0,1:T(4,128)S(1)}, s32[512,4]{0,1:T(4,128)}, u32[]{:S(2)}) copy-start(s32[512,4]{0,1:T(4,128)} %param.12) | copy-start | bytes 24580
  0.7 32.0 %copy-start.7 = (f32[8,4]{0,1:T(4,128)S(1)}, f32[8,4]{0,1:T(4,128)}, u32[]{:S(2)}) copy-start(f32[8,4]{0,1:T(4,128)} %param.15) | copy-start | bytes 388
  0.7 32.0 %copy-start.5 = (f32[512,4]{0,1:T(4,128)S(1)}, f32[512,4]{0,1:T(4,128)}, u32[]{:S(2)}) copy-start(f32[512,4]{0,1:T(4,128)} %param.13) | copy-start | bytes 24580
  27.1 6.5 %copy-start.3 = (f32[8,128]{1,0:T(8,128)}, f32[8,128]{1,0:T(8,128)S(1)}, u32[]{:S(2)}) copy-start(f32[8,128]{1,0:T(8,128)S(1)} %reduce_sum.18.after_ref) | copy-start | bytes 12292
  27.8 13.7 %all-to-all-start.1 = ((f32[32,8,128]{2,1,0:T(8,128)}), f32[32,8,128]{2,1,0:T(8,128)S(1)}, u32[]{:S(2)}, u32[]{:S(2)}) async-start(f32[32,8,128]{2,1,0:T(8,128)} %broadcast_in_dim.32), calls=%async_computation.1 | async-start | bytes 262144 | tf_op jit(solution)/shard_map/all_to_all | solution.py:113
  41.5 23.5 %copy-start.8 = (f32[128]{0:T(128)S(1)}, f32[128]{0:T(128)}, u32[]{:S(2)}) copy-start(f32[128]{0:T(128)} %param.17) | copy-start | bytes 1540
  41.8 37.0 %copy-start.2 = (f32[2048,128]{1,0:T(8,128)S(1)}, f32[2048,128]{1,0:T(8,128)}, u32[]{:S(2)}) copy-start(f32[2048,128]{1,0:T(8,128)} %v_ref.1) | copy-start | bytes 3145732
  44.2 35.8 %copy-start.1 = (f32[2048,256]{1,0:T(8,128)S(1)}, f32[2048,256]{1,0:T(8,128)}, u32[]{:S(2)}) copy-start(f32[2048,256]{1,0:T(8,128)} %r_ref.1) | copy-start | bytes 6291460
  44.2 19.7 %all-to-all-start.2 = ((f32[32,24,128]{2,1,0:T(8,128)}), f32[32,24,128]{2,1,0:T(8,128)}, u32[]{:S(2)}, u32[]{:S(2)}) async-start(f32[32,24,128]{2,1,0:T(8,128)} %pad_maximum_fusion), calls=%async_computation.2 | async-start | bytes 786432 | tf_op jit(solution)/shard_map/all_to_all | solution.py:127
  66.4 24.2 %all-to-all-start.3 = ((f32[16,26,128]{2,1,0:T(8,128)}), f32[16,26,128]{2,1,0:T(8,128)}, u32[]{:S(2)}, u32[]{:S(2)}) async-start(f32[16,26,128]{2,1,0:T(8,128)} %broadcast_in_dim.37), calls=%async_computation.3 | async-start | bytes 524288 | tf_op jit(solution)/shard_map/all_to_all | solution.py:133

commit v11 on v10

--- a/solution.py
+++ b/solution.py
@@ -69,6 +69,38 @@
     )(idx, w, vectors, reflectors, after)
 
 
+def post_kernel(nrow, whole_ref, t_ref, tv_ref, tr_ref, folded_ref, send_ref):
+    blocks, comp_here, width = tv_ref.shape
+    pw = t_ref.shape[0]
+    events = send_ref.shape[1] - comp_here
+    hi = lax.Precision.HIGHEST
+    panel = whole_ref[...].reshape(pw, width)
+    folded = jnp.dot(t_ref[...], panel, precision=hi, preferred_element_type=jnp.float32)
+    folded_ref[...] = folded
+    tv = tv_ref[...].reshape(blocks * comp_here, width)
+    tr = tr_ref[...].reshape(blocks * comp_here, pw)
+    rot = tv - jnp.dot(tr, folded, precision=hi, preferred_element_type=jnp.float32)
+    ev = rot[nrow * comp_here:nrow * comp_here + events]
+    for j in range(nrow):
+        send_ref[j, pl.ds(0, comp_here), :] = rot[j * comp_here:(j + 1) * comp_here]
+        send_ref[j, pl.ds(comp_here, events), :] = ev
+
+
+def build_post(nrow, events, whole, panel_factor, tv, tr):
+    _, comp_here, width = tv.shape
+    pw = panel_factor.shape[0]
+    vmem = pl.BlockSpec(memory_space=pltpu.VMEM)
+    return pl.pallas_call(
+        functools.partial(post_kernel, nrow),
+        out_shape=(
+            jax.ShapeDtypeStruct((pw, width), jnp.float32),
+            jax.ShapeDtypeStruct((nrow, comp_here + events, width), jnp.float32),
+        ),
+        in_specs=[vmem] * 4,
+        out_specs=(vmem, vmem),
+    )(whole, panel_factor, tv, tr)
+
+
 def mode_basis(freq, damp, times):
     return jnp.exp(-damp[:, None] * times[None, :]) * jnp.cos(freq[:, None] * times[None, :])
 
@@ -111,19 +143,7 @@
         mine,
     )
     whole = lax.all_to_all(jnp.broadcast_to(mine[None], (nrow,) + mine.shape), "row", 0, 0)
-    panel = whole.reshape(pw, width)
-    folded = jnp.dot(panel_factor, panel, precision=high, preferred_element_type=jnp.float32)
-    blocks = tv.shape[0]
-    rot_taps = tv - jnp.dot(
-        tr.reshape(-1, pw), folded, precision=high, preferred_element_type=jnp.float32
-    ).reshape(blocks, comp_here, width)
-    send = jnp.concatenate(
-        [
-            rot_taps[:nrow],
-            jnp.broadcast_to(rot_taps[nrow, :events][None], (nrow, events, width)),
-        ],
-        1,
-    )
+    folded, send = build_post(nrow, events, whole, panel_factor, tv, tr)
     got = lax.all_to_all(send, "row", 0, 0).sum(0)
     held, got = lax.optimization_barrier((vectors, got))
     rotated = held - jnp.dot(

time: 96.9 us -> 94.1 us (0.971)
  Pallas kernels: 7.9 us -> 11.2 us
  other arithmetic: 3.47 us -> 0.82 us
  matrix products: 11 us -> 9.16 us
  local copies, waits for them, and re-layouts: 7.68 us -> 6.53 us
    pallas_call x0 -> x1, Pallas kernels: none -> 3.32 us  [build_post(): pl.pallas_call(functools.partial(post_kernel, nrow), out_shape=(jax.Shape...]
    dot_general x2 -> x0, matrix products: 1.89 us -> none  [the longest x1 1.59 us: shards(): jnp.dot(tr.reshape(-1, pw), folded, precision=high, preferred_element_typ...]
    mul x2, local copies, waits for them, and re-layouts: 1.76 us -> 0.02 us  [shards(): sources[:, None, :] * receivers[None, :, :]]
    reduce_sum x1, other arithmetic: 1.04 us -> 0.04 us  [shards(): got = lax.all_to_all(send, 'row', 0, 0).sum(0)]
    unnamed x19 -> x21, local copies, waits for them, and re-layouts: 1.35 us -> 1.99 us
where the time goes in v11:
time: 94.1 us; the launch traced here: 93.6 us
  starting transfers between devices  25.6 us (27%)
  blocking collectives  22.7 us (24%)
  waiting for transfers between devices  16.8 us (18%)
  Pallas kernels  11.2 us (12%)
  matrix products  9.16 us (10%)
  local copies, waits for them, and re-layouts  6.53 us (7%)
    all_to_all x1, blocking collectives, shards(): lax.all_to_all(partial_panel.reshape(nrow, prow, width), 'row', 0, 0).sum(0)  22.7 us
    all_to_all x1, starting transfers between devices, shards(): lax.all_to_all(jnp.broadcast_to(block[None], (ncol,) + block.shape), 'col...  12.4 us
    all_to_all x1, waiting for transfers between devices, shards(): got = lax.all_to_all(send, 'row', 0, 0).sum(0)  10.2 us
    all_to_all x1, starting transfers between devices, shards(): got = lax.all_to_all(send, 'row', 0, 0).sum(0)  9.35 us
    pallas_call x1, Pallas kernels, build_taps(): pl.pallas_call(functools.partial(tap_kernel, taps, comp_here), out_shape=...  7.91 us
    all_to_all x1, waiting for transfers between devices, shards(): lax.all_to_all(jnp.broadcast_to(block[None], (ncol,) + block.shape), 'col...  6.59 us
    all_to_all x1, starting transfers between devices, shards(): lax.all_to_all(jnp.broadcast_to(mine[None], (nrow,) + mine.shape), 'row',...  3.85 us
    dot_general x1, matrix products, shards(): jnp.dot(reflectors.T, vectors, precision=high, preferred_element_type=jnp...  3.68 us
  transfers between devices with their start and end apart: 3, of which 2 were waited for; matrix products, arithmetic and copies ran while one was open for 7% of the time, Pallas kernels for 8%

profile of v11, /device:TPU:1, one launch (start us, length us, event | category | flops | bytes accessed | tf_op | source)
XLA Modules:
  0.0 93.6 jit_solution(2087246123125591518)
XLA Ops:
  0.6 0.0 copy-start.7
  0.6 0.0 copy-start.5
  0.7 3.7 %convolution_bitcast_fusion.1 = f32[32,8,128]{2,1,0:T(8,128)S(1)} fusion(f32[2048,256]{1,0:T(8,128)} %r_ref.1, f32[2048,128]{1,0:T(8,128)} %v_ref.1), kind=kOutput, calls=%fused_computation.2 | convolution fusion | flops 402653184 | bytes 3276800 | tf_op jit(solution)/shard_map/dot_general | solution.py:131
  4.4 22.7 %all_to_all.20 = f32[32,8,128]{2,1,0:T(8,128)S(1)} all-to-all(f32[32,8,128]{2,1,0:T(8,128)S(1)} %convolution_bitcast_fusion.1), channel_id=1, replica_groups=mesh['row'=32,'col'=16] {'row'}, dimensions={0} | all-to-all | bytes 262144 | tf_op jit(solution)/shard_map/all_to_all | solution.py:135
  27.1 0.7 broadcast_in_dim.12
  27.7 3.8 %all-to-all-start.1 = ((f32[32,8,128]{2,1,0:T(8,128)}), f32[32,8,128]{2,1,0:T(8,128)S(1)}, u32[]{:S(2)}, u32[]{:S(2)}) async-start(f32[32,8,128]{2,1,0:T(8,128)} %broadcast_in_dim.12), calls=%async_computation.1 | async-start | bytes 262144 | tf_op jit(solution)/shard_map/all_to_all | solution.py:145
  31.6 0.1 copy.21
  31.8 0.8 min.12.idx_ref
  32.6 0.1 copy.22
  32.7 0.8 select_n.9.w_ref
  33.5 7.9 %shard_map.104 = (f32[33,16,128]{2,1,0:T(8,128)}, f32[33,16,256]{2,1,0:T(8,128)}) custom-call(s32[2080]{0:T(1024)} %min.12.idx_ref, f32[2080]{0:T(1024)} %select_n.9.w_ref, f32[2048,128]{1,0:T(8,128)} %v_ref.1, f32[2048,256]{1,0:T(8,128)} %r_ref.1, f32[8,128]{1,0:T(8,128)} %copy-done.4), custom_call_target="tpu_custom_call" | custom-call | flops 1597440 | bytes 3194880 | tf_op jit(solution)/shard_map/pallas_call | solution.py:58
  41.4 0.0 all-to-all-done.1.whole_ref
  41.4 0.6 copy-done.2
  42.1 3.3 %shard_map.105 = (f32[256,128]{1,0:T(8,128)}, f32[32,24,128]{2,1,0:T(8,128)}) custom-call(f32[32,8,128]{2,1,0:T(8,128)} %copy-done.2, f32[256,256]{1,0:T(8,128)} %t_ref.1, f32[33,16,128]{2,1,0:T(8,128)} %get-tuple-element.8.tv_ref, f32[33,16,256]{2,1,0:T(8,128)} %get-tuple-element.9.tr_ref), custom_call_target="tpu_custom_call" | custom-call | tf_op jit(solution)/shard_map/pallas_call | solution.py:93
  45.4 9.4 %all-to-all-start.2 = ((f32[32,24,128]{2,1,0:T(8,128)}), f32[32,24,128]{2,1,0:T(8,128)S(1)}, u32[]{:S(2)}, u32[]{:S(2)}) async-start(f32[32,24,128]{2,1,0:T(8,128)} %get-tuple-element.10), calls=%async_computation.2 | async-start | bytes 786432 | tf_op jit(solution)/shard_map/all_to_all | solution.py:147
  54.7 10.2 %all-to-all-done.2 = f32[32,24,128]{2,1,0:T(8,128)S(1)} async-done(((f32[32,24,128]{2,1,0:T(8,128)}), f32[32,24,128]{2,1,0:T(8,128)S(1)}, u32[]{:S(2)}, u32[]{:S(2)}) %all-to-all-start.2) | async-done | bytes 393248 | tf_op jit(solution)/shard_map/all_to_all | solution.py:147
  65.0 0.7 pad_maximum_fusion
  65.7 0.7 broadcast_in_dim.28
  66.5 12.4 %all-to-all-start.3 = ((f32[16,26,128]{2,1,0:T(8,128)}), f32[16,26,128]{2,1,0:T(8,128)S(1)}, u32[]{:S(2)}, u32[]{:S(2)}) async-start(f32[16,26,128]{2,1,0:T(8,128)} %broadcast_in_dim.28), calls=%async_computation.3 | async-start | bytes 524288 | tf_op jit(solution)/shard_map/all_to_all | solution.py:153
  78.9 1.3 %copy.23 = f32[2048,128]{0,1:T(8,128)} copy(f32[2048,128]{1,0:T(8,128)S(1)} %copy-done.1) | data formatting | bytes 2097152 | tf_op jit(solution)/shard_map/optimization_barrier | solution.py:148
  80.2 2.5 %fusion = f32[2048,128]{0,1:T(8,128)S(1)} fusion(f32[2048,128]{0,1:T(8,128)} %copy.23, f32[256,128]{1,0:T(8,128)S(1)} %copy-done.3, f32[2048,256]{1,0:T(8,128)S(1)} %copy-done), kind=kOutput, calls=%fused_computation.1 | convolution fusion | flops 402915328 | bytes 4325376 | tf_op jit(solution)/shard_map/dot_general | solution.py:149
  82.7 1.3 %copy.25 = f32[2048,128]{1,0:T(8,128)} copy(f32[2048,128]{0,1:T(8,128)S(1)} %fusion) | data formatting | bytes 2097152
  84.0 6.6 %all-to-all-done.3 = f32[16,26,128]{2,1,0:T(8,128)S(1)} async-done(((f32[16,26,128]{2,1,0:T(8,128)}), f32[16,26,128]{2,1,0:T(8,128)S(1)}, u32[]{:S(2)}, u32[]{:S(2)}) %all-to-all-start.3) | async-done | bytes 213024 | tf_op jit(solution)/shard_map/all_to_all | solution.py:153
  90.6 3.0 %convolution_multiply_fusion = f32[8,16,64]{2,1,0:T(8,128)} fusion(f32[16,2048]{1,0:T(8,128)S(1)} %copy_bitcast_fusion, f32[8,2048]{1,0:T(8,128)S(1)} %slice_bitcast_fusion.1, f32[2048]{0:T(1024)S(1)} %bitcast.28, f32[64]{0:T(128)S(1)} %add_convert_fusion, f32[2048]{0:T(1024)S(1)} %bitcast.27), kind=kOutput, calls=%fused_computation.3 | convolution fusion | flops 101326848 | bytes 246016 | tf_op jit(solution)/shard_map/dot_general | solution.py:163
  (25 shorter events, 0.2 us)
Async XLA Ops:
  0.6 31.0 %copy-start.7 = (s32[8,4]{0,1:T(4,128)S(1)}, s32[8,4]{0,1:T(4,128)}, u32[]{:S(2)}) copy-start(s32[8,4]{0,1:T(4,128)} %param.14) | copy-start | bytes 388
  0.6 31.0 %copy-start.5 = (s32[512,4]{0,1:T(4,128)S(1)}, s32[512,4]{0,1:T(4,128)}, u32[]{:S(2)}) copy-start(s32[512,4]{0,1:T(4,128)} %param.12) | copy-start | bytes 24580
  0.7 31.9 %copy-start.8 = (f32[8,4]{0,1:T(4,128)S(1)}, f32[8,4]{0,1:T(4,128)}, u32[]{:S(2)}) copy-start(f32[8,4]{0,1:T(4,128)} %param.15) | copy-start | bytes 388
  0.7 31.9 %copy-start.6 = (f32[512,4]{0,1:T(4,128)S(1)}, f32[512,4]{0,1:T(4,128)}, u32[]{:S(2)}) copy-start(f32[512,4]{0,1:T(4,128)} %param.13) | copy-start | bytes 24580
  27.1 6.4 %copy-start.4 = (f32[8,128]{1,0:T(8,128)}, f32[8,128]{1,0:T(8,128)S(1)}, u32[]{:S(2)}) copy-start(f32[8,128]{1,0:T(8,128)S(1)} %reduce_sum.18.after_ref) | copy-start | bytes 12292
  27.7 13.7 %all-to-all-start.1 = ((f32[32,8,128]{2,1,0:T(8,128)}), f32[32,8,128]{2,1,0:T(8,128)S(1)}, u32[]{:S(2)}, u32[]{:S(2)}) async-start(f32[32,8,128]{2,1,0:T(8,128)} %broadcast_in_dim.12), calls=%async_computation.1 | async-start | bytes 262144 | tf_op jit(solution)/shard_map/all_to_all | solution.py:145
  33.5 31.5 %copy-start.9 = (f32[128]{0:T(128)S(1)}, f32[128]{0:T(128)}, u32[]{:S(2)}) copy-start(f32[128]{0:T(128)} %param.17) | copy-start | bytes 1540
  41.4 37.4 %copy-start.1 = (f32[2048,128]{1,0:T(8,128)S(1)}, f32[2048,128]{1,0:T(8,128)}, u32[]{:S(2)}) copy-start(f32[2048,128]{1,0:T(8,128)} %v_ref.1) | copy-start | bytes 3145732
  41.4 0.6 copy-start.2
  45.4 34.8 %copy-start = (f32[2048,256]{1,0:T(8,128)S(1)}, f32[2048,256]{1,0:T(8,128)}, u32[]{:S(2)}) copy-start(f32[2048,256]{1,0:T(8,128)} %r_ref.1) | copy-start | bytes 6291460
  45.4 19.6 %all-to-all-start.2 = ((f32[32,24,128]{2,1,0:T(8,128)}), f32[32,24,128]{2,1,0:T(8,128)S(1)}, u32[]{:S(2)}, u32[]{:S(2)}) async-start(f32[32,24,128]{2,1,0:T(8,128)} %get-tuple-element.10), calls=%async_computation.2 | async-start | bytes 786432 | tf_op jit(solution)/shard_map/all_to_all | solution.py:147
  65.0 15.1 %copy-start.3 = (f32[256,128]{1,0:T(8,128)S(1)}, f32[256,128]{1,0:T(8,128)}, u32[]{:S(2)}) copy-start(f32[256,128]{1,0:T(8,128)} %get-tuple-element.12) | copy-start | bytes 393220
  66.5 24.1 %all-to-all-start.3 = ((f32[16,26,128]{2,1,0:T(8,128)}), f32[16,26,128]{2,1,0:T(8,128)S(1)}, u32[]{:S(2)}, u32[]{:S(2)}) async-start(f32[16,26,128]{2,1,0:T(8,128)} %broadcast_in_dim.28), calls=%async_computation.3 | async-start | bytes 524288 | tf_op jit(solution)/shard_map/all_to_all | solution.py:153

commit v12 on v8

--- a/solution.py
+++ b/solution.py
@@ -81,11 +81,12 @@
     )
     prow = pw // nrow
     mine = lax.all_to_all(partial_panel.reshape(nrow, prow, width), "row", 0, 0).sum(0)
+    held, mine = lax.optimization_barrier((reflectors, mine))
     whole = lax.all_to_all(jnp.broadcast_to(mine[None], (nrow,) + mine.shape), "row", 0, 0)
+    factored = jnp.dot(held, panel_factor, precision=high, preferred_element_type=jnp.float32)
     panel = whole.reshape(pw, width)
-    folded = jnp.dot(panel_factor, panel, precision=high, preferred_element_type=jnp.float32)
     rotated = vectors - jnp.dot(
-        reflectors, folded, precision=high, preferred_element_type=jnp.float32
+        factored, panel, precision=high, preferred_element_type=jnp.float32
     )
     send = build_taps(
         jnp.concatenate([station_rows, event_rows], 0),

time: 92.5 us -> 93.6 us (1.012)
  blocking collectives: 36.8 us -> 14.1 us
  starting transfers between devices: 16.8 us -> 30.5 us
  waiting for transfers between devices: 18.2 us -> 25.7 us
  matrix products: 9.24 us -> 12.6 us
    all_to_all x1 -> x0, blocking collectives: 22.7 us -> none  [shards(): lax.all_to_all(partial_panel.reshape(nrow, prow, width), 'row', 0, 0).sum(0)]
    all_to_all x0 -> x1, starting transfers between devices: none -> 13.7 us  [shards(): lax.all_to_all(partial_panel.reshape(nrow, prow, width), 'row', 0, 0).sum(0)]
    all_to_all x0 -> x1, waiting for transfers between devices: none -> 7.24 us  [shards(): lax.all_to_all(partial_panel.reshape(nrow, prow, width), 'row', 0, 0).sum(0)]
    dot_general x2, matrix products: 3.21 us -> 5.89 us  [the longest x1 3.56 us: shards(): jnp.dot(factored, panel, precision=high, preferred_element_type=jnp.float32)]
  transfers between devices with their start and end apart: 2 -> 3, of which waited for: 2 -> 3; matrix products, arithmetic and copies ran while one was open for 3% -> 5% of each run, Pallas kernels for 0% -> 0%
where the time goes in v12:
time: 93.6 us; the launch traced here: 93.1 us
  starting transfers between devices  30.5 us (33%)
  waiting for transfers between devices  25.7 us (27%)
  blocking collectives  14.1 us (15%)
  matrix products  12.6 us (13%)
  local copies, waits for them, and re-layouts  4.84 us (5%)
  Pallas kernels  4.39 us (5%)
    all_to_all x1, blocking collectives, shards(): got = lax.all_to_all(send, 'row', 0, 0).sum(0)  14.1 us
    all_to_all x1, starting transfers between devices, shards(): lax.all_to_all(partial_panel.reshape(nrow, prow, width), 'row', 0, 0).sum(0)  13.7 us
    all_to_all x1, starting transfers between devices, shards(): lax.all_to_all(jnp.broadcast_to(block[None], (ncol,) + block.shape), 'col...  12.9 us
    all_to_all x1, waiting for transfers between devices, shards(): lax.all_to_all(jnp.broadcast_to(block[None], (ncol,) + block.shape), 'col...  11.7 us
    all_to_all x1, waiting for transfers between devices, shards(): lax.all_to_all(partial_panel.reshape(nrow, prow, width), 'row', 0, 0).sum(0)  7.24 us
    all_to_all x1, waiting for transfers between devices, shards(): lax.all_to_all(jnp.broadcast_to(mine[None], (nrow,) + mine.shape), 'row',...  6.78 us
    pallas_call x1, Pallas kernels, build_taps(): pl.pallas_call(functools.partial(tap_kernel, taps, nrow, comp_here, event...  4.39 us
    all_to_all x1, starting transfers between devices, shards(): lax.all_to_all(jnp.broadcast_to(mine[None], (nrow,) + mine.shape), 'row',...  3.86 us
  transfers between devices with their start and end apart: 3, of which 3 were waited for; matrix products, arithmetic and copies ran while one was open for 5% of the time, Pallas kernels for 0%

profile of v12, /device:TPU:1, one launch (start us, length us, event | category | flops | bytes accessed | tf_op | source)
XLA Modules:
  0.0 93.1 jit_solution(10218988819498356188)
XLA Ops:
  0.6 0.0 copy-start
  0.6 0.0 copy-start.3
  0.7 0.0 copy-start.5
  0.7 0.0 copy-start.4
  0.7 1.5 %copy-done = f32[2048,256]{1,0:T(8,128)S(1)} copy-done((f32[2048,256]{1,0:T(8,128)S(1)}, f32[2048,256]{1,0:T(8,128)}, u32[]{:S(2)}) %copy-start) | copy-done | bytes 2097176
  2.2 3.7 %convolution_bitcast_fusion = f32[32,8,128]{2,1,0:T(8,128)} fusion(f32[2048,256]{1,0:T(8,128)S(1)} %copy-done, f32[2048,128]{1,0:T(8,128)} %param.9), kind=kOutput, calls=%fused_computation.1 | convolution fusion | flops 402653184 | bytes 3276800 | tf_op jit(solution)/shard_map/dot_general | solution.py:79
  5.9 13.7 %all-to-all-start = ((f32[32,8,128]{2,1,0:T(8,128)}), f32[32,8,128]{2,1,0:T(8,128)S(1)}, u32[]{:S(2)}, u32[]{:S(2)}) async-start(f32[32,8,128]{2,1,0:T(8,128)} %convolution_bitcast_fusion), calls=%async_computation | async-start | bytes 262144 | tf_op jit(solution)/shard_map/all_to_all | solution.py:83
  19.7 0.1 copy.15
  19.8 0.8 min.12.idx_ref
  20.6 0.1 copy.16
  20.8 0.8 select_n.9.w_ref
  21.6 7.2 %all-to-all-done = f32[32,8,128]{2,1,0:T(8,128)S(1)} async-done(((f32[32,8,128]{2,1,0:T(8,128)}), f32[32,8,128]{2,1,0:T(8,128)S(1)}, u32[]{:S(2)}, u32[]{:S(2)}) %all-to-all-start) | async-done | bytes 131104 | tf_op jit(solution)/shard_map/all_to_all | solution.py:83
  28.8 0.7 broadcast_in_dim.12
  29.5 3.9 %all-to-all-start.1 = ((f32[32,8,128]{2,1,0:T(8,128)}), f32[32,8,128]{2,1,0:T(8,128)S(1)}, u32[]{:S(2)}, u32[]{:S(2)}) async-start(f32[32,8,128]{2,1,0:T(8,128)} %broadcast_in_dim.12), calls=%async_computation.1 | async-start | bytes 262144 | tf_op jit(solution)/shard_map/all_to_all | solution.py:85
  33.4 0.0 copy-start.1
  33.4 2.3 %fusion.14 = f32[2048,256]{1,0:T(8,128)} fusion(f32[2048,256]{1,0:T(8,128)S(1)} %copy-done, f32[256,256]{1,0:T(8,128)S(1)} %copy-done.2), kind=kOutput, calls=%fused_computation.25 | convolution fusion | flops 805306368 | bytes 4456448 | tf_op jit(solution)/shard_map/dot_general | solution.py:86
  35.7 6.8 %all-to-all-done.1 = f32[32,8,128]{2,1,0:T(8,128)S(1)} async-done(((f32[32,8,128]{2,1,0:T(8,128)}), f32[32,8,128]{2,1,0:T(8,128)S(1)}, u32[]{:S(2)}, u32[]{:S(2)}) %all-to-all-start.1) | async-done | bytes 131104 | tf_op jit(solution)/shard_map/all_to_all | solution.py:85
  42.5 3.6 %convolution_subtract_fusion.rot_ref = f32[2048,128]{1,0:T(8,128)} fusion(f32[2048,128]{1,0:T(8,128)S(1)} %copy-done.1, f32[2048,256]{1,0:T(8,128)} %fusion.14, f32[32,8,128]{2,1,0:T(8,128)S(1)} %all-to-all-done.1), kind=kOutput, calls=%fused_computation | convolution fusion | flops 402915328 | bytes 4325376 | tf_op jit(solution)/shard_map/dot_general | solution.py:88
  46.1 4.4 %shard_map.104 = f32[32,24,128]{2,1,0:T(8,128)} custom-call(s32[2080]{0:T(1024)} %min.12.idx_ref, f32[2080]{0:T(1024)} %select_n.9.w_ref, f32[2048,128]{1,0:T(8,128)} %convolution_subtract_fusion.rot_ref), custom_call_target="tpu_custom_call" | custom-call | tf_op jit(solution)/shard_map/pallas_call | solution.py:44
  50.5 14.1 %all_to_all.20 = f32[32,24,128]{2,1,0:T(8,128)S(1)} all-to-all(f32[32,24,128]{2,1,0:T(8,128)} %shard_map.104), channel_id=1, replica_groups=mesh['row'=32,'col'=16] {'row'}, dimensions={0} | all-to-all | bytes 786432 | tf_op jit(solution)/shard_map/all_to_all | solution.py:100
  64.7 0.7 broadcast_in_dim.28
  65.4 12.9 %all-to-all-start.3 = ((f32[16,26,128]{2,1,0:T(8,128)}), f32[16,26,128]{2,1,0:T(8,128)S(1)}, u32[]{:S(2)}, u32[]{:S(2)}) async-start(f32[16,26,128]{2,1,0:T(8,128)} %broadcast_in_dim.28), calls=%async_computation.3 | async-start | bytes 524288 | tf_op jit(solution)/shard_map/all_to_all | solution.py:102
  78.3 11.7 %all-to-all-done.3 = f32[16,26,128]{2,1,0:T(8,128)S(1)} async-done(((f32[16,26,128]{2,1,0:T(8,128)}), f32[16,26,128]{2,1,0:T(8,128)S(1)}, u32[]{:S(2)}, u32[]{:S(2)}) %all-to-all-start.3) | async-done | bytes 213024 | tf_op jit(solution)/shard_map/all_to_all | solution.py:102
  90.1 3.0 %convolution_multiply_fusion = f32[8,16,64]{2,1,0:T(8,128)} fusion(f32[16,2048]{1,0:T(8,128)S(1)} %copy_bitcast_fusion, f32[8,2048]{1,0:T(8,128)S(1)} %slice_bitcast_fusion.1, f32[2048]{0:T(1024)S(1)} %bitcast.28, f32[64]{0:T(128)S(1)} %add_convert_fusion, f32[2048]{0:T(1024)S(1)} %bitcast.27), kind=kOutput, calls=%fused_computation.2 | convolution fusion | flops 101326848 | bytes 246016 | tf_op jit(solution)/shard_map/dot_general | solution.py:112
  (21 shorter events, 0.2 us)
Async XLA Ops:
  0.6 1.6 %copy-start = (f32[2048,256]{1,0:T(8,128)S(1)}, f32[2048,256]{1,0:T(8,128)}, u32[]{:S(2)}) copy-start(f32[2048,256]{1,0:T(8,128)} %param.10) | copy-start | bytes 6291460
  0.6 19.0 %copy-start.3 = (s32[512,4]{0,1:T(4,128)S(1)}, s32[512,4]{0,1:T(4,128)}, u32[]{:S(2)}) copy-start(s32[512,4]{0,1:T(4,128)} %param.12) | copy-start | bytes 24580
  0.7 19.0 %copy-start.5 = (s32[8,4]{0,1:T(4,128)S(1)}, s32[8,4]{0,1:T(4,128)}, u32[]{:S(2)}) copy-start(s32[8,4]{0,1:T(4,128)} %param.14) | copy-start | bytes 388
  0.7 19.9 %copy-start.4 = (f32[512,4]{0,1:T(4,128)S(1)}, f32[512,4]{0,1:T(4,128)}, u32[]{:S(2)}) copy-start(f32[512,4]{0,1:T(4,128)} %param.13) | copy-start | bytes 24580
  0.7 19.9 %copy-start.6 = (f32[8,4]{0,1:T(4,128)S(1)}, f32[8,4]{0,1:T(4,128)}, u32[]{:S(2)}) copy-start(f32[8,4]{0,1:T(4,128)} %param.15) | copy-start | bytes 388
  0.7 32.7 %copy-start.2 = (f32[256,256]{1,0:T(8,128)S(1)}, f32[256,256]{1,0:T(8,128)}, u32[]{:S(2)}) copy-start(f32[256,256]{1,0:T(8,128)} %param.11) | copy-start | bytes 786436
  5.9 22.9 %all-to-all-start = ((f32[32,8,128]{2,1,0:T(8,128)}), f32[32,8,128]{2,1,0:T(8,128)S(1)}, u32[]{:S(2)}, u32[]{:S(2)}) async-start(f32[32,8,128]{2,1,0:T(8,128)} %convolution_bitcast_fusion), calls=%async_computation | async-start | bytes 262144 | tf_op jit(solution)/shard_map/all_to_all | solution.py:83
  29.5 13.0 %all-to-all-start.1 = ((f32[32,8,128]{2,1,0:T(8,128)}), f32[32,8,128]{2,1,0:T(8,128)S(1)}, u32[]{:S(2)}, u32[]{:S(2)}) async-start(f32[32,8,128]{2,1,0:T(8,128)} %broadcast_in_dim.12), calls=%async_computation.1 | async-start | bytes 262144 | tf_op jit(solution)/shard_map/all_to_all | solution.py:85
  33.4 9.1 %copy-start.1 = (f32[2048,128]{1,0:T(8,128)S(1)}, f32[2048,128]{1,0:T(8,128)}, u32[]{:S(2)}) copy-start(f32[2048,128]{1,0:T(8,128)} %param.9) | copy-start | bytes 3145732
  46.1 18.6 %copy-start.7 = (f32[128]{0:T(128)S(1)}, f32[128]{0:T(128)}, u32[]{:S(2)}) copy-start(f32[128]{0:T(128)} %param.17) | copy-start | bytes 1540
  46.1 18.6 %copy-start.8 = (f32[128]{0:T(128)S(1)}, f32[128]{0:T(128)}, u32[]{:S(2)}) copy-start(f32[128]{0:T(128)} %param.16) | copy-start | bytes 1540
  65.4 24.6 %all-to-all-start.3 = ((f32[16,26,128]{2,1,0:T(8,128)}), f32[16,26,128]{2,1,0:T(8,128)S(1)}, u32[]{:S(2)}, u32[]{:S(2)}) async-start(f32[16,26,128]{2,1,0:T(8,128)} %broadcast_in_dim.28), calls=%async_computation.3 | async-start | bytes 524288 | tf_op jit(solution)/shard_map/all_to_all | solution.py:102

commit v13 on v8

--- a/solution.py
+++ b/solution.py
@@ -49,6 +49,34 @@
     )(idx, w, rotated)
 
 
+def panel_kernel(nrow, v_ref, r_ref, out_ref):
+    v = v_ref[...]
+    r = r_ref[...]
+    v_hi = v.astype(jnp.bfloat16)
+    v_lo = (v - v_hi.astype(jnp.float32)).astype(jnp.bfloat16)
+    r_hi = r.astype(jnp.bfloat16)
+    r_lo = (r - r_hi.astype(jnp.float32)).astype(jnp.bfloat16)
+    dims = (((0,), (0,)), ((), ()))
+
+    def prod(a, b):
+        return lax.dot_general(a, b, dims, preferred_element_type=jnp.float32)
+
+    p = prod(r_hi, v_hi) + (prod(r_hi, v_lo) + prod(r_lo, v_hi))
+    out_ref[...] = p.reshape(out_ref.shape)
+
+
+def build_panel(nrow, vectors, reflectors):
+    width = vectors.shape[1]
+    pw = reflectors.shape[1]
+    vmem = pl.BlockSpec(memory_space=pltpu.VMEM)
+    return pl.pallas_call(
+        functools.partial(panel_kernel, nrow),
+        out_shape=jax.ShapeDtypeStruct((nrow, pw // nrow, width), jnp.float32),
+        in_specs=[vmem, vmem],
+        out_specs=vmem,
+    )(vectors, reflectors)
+
+
 def mode_basis(freq, damp, times):
     return jnp.exp(-damp[:, None] * times[None, :]) * jnp.cos(freq[:, None] * times[None, :])
 
@@ -76,11 +104,8 @@
     samples = NT // ncol
     col = lax.axis_index("col")
 
-    partial_panel = jnp.dot(
-        reflectors.T, vectors, precision=high, preferred_element_type=jnp.float32
-    )
     prow = pw // nrow
-    mine = lax.all_to_all(partial_panel.reshape(nrow, prow, width), "row", 0, 0).sum(0)
+    mine = lax.all_to_all(build_panel(nrow, vectors, reflectors), "row", 0, 0).sum(0)
     whole = lax.all_to_all(jnp.broadcast_to(mine[None], (nrow,) + mine.shape), "row", 0, 0)
     panel = whole.reshape(pw, width)
     folded = jnp.dot(panel_factor, panel, precision=high, preferred_element_type=jnp.float32)

time: 92.5 us -> 93.2 us (level)
  waiting for transfers between devices: 18.2 us -> 14.2 us
  matrix products: 9.24 us -> 5.27 us
  Pallas kernels: 4.39 us -> 8.15 us
  blocking collectives: 36.8 us -> 39.8 us
  local copies, waits for them, and re-layouts: 4.86 us -> 6.58 us
    all_to_all x1, waiting for transfers between devices: 6.49 us -> 2.52 us  [shards(): lax.all_to_all(jnp.broadcast_to(mine[None], (nrow,) + mine.shape), 'row',...]
    pallas_call x0 -> x1, Pallas kernels: none -> 3.76 us  [build_panel(): pl.pallas_call(functools.partial(panel_kernel, nrow), out_shape=jax.Shape...]
    dot_general x1 -> x0, matrix products: 3.02 us -> none  [shards(): jnp.dot(reflectors.T, vectors, precision=high, preferred_element_type=jnp...]
    all_to_all x1, blocking collectives: 14.1 us -> 16.9 us  [shards(): got = lax.all_to_all(send, 'row', 0, 0).sum(0)]
    min x2, local copies, waits for them, and re-layouts: 0.92 us -> 2.58 us  [build_taps(): idx = jnp.clip(local, 0, rows_here - 1).reshape(-1)]
    select_n x2, local copies, waits for them, and re-layouts: 0.91 us -> 2.57 us  [build_taps(): w = jnp.where(inside, weights, 0.0).reshape(-1)]
    unnamed x12, local copies, waits for them, and re-layouts: 1.61 us -> 0.03 us
    dot_general x1, matrix products: 1.24 us -> 0.3 us  [shards(): jnp.dot(panel_factor, panel, precision=high, preferred_element_type=jnp.f...]
  transfers between devices with their start and end apart: 2 -> 2, of which waited for: 2 -> 2; matrix products, arithmetic and copies ran while one was open for 3% -> 7% of each run, Pallas kernels for 0% -> 0%
where the time goes in v13:
time: 93.2 us; the launch traced here: 92.6 us
  blocking collectives  39.8 us (43%)
  starting transfers between devices  16.2 us (17%)
  waiting for transfers between devices  14.2 us (15%)
  Pallas kernels  8.15 us (9%)
  local copies, waits for them, and re-layouts  6.58 us (7%)
  matrix products  5.27 us (6%)
  other arithmetic  1.55 us (2%)
    all_to_all x1, blocking collectives, shards(): lax.all_to_all(build_panel(nrow, vectors, reflectors), 'row', 0, 0).sum(0)  22.9 us
    all_to_all x1, blocking collectives, shards(): got = lax.all_to_all(send, 'row', 0, 0).sum(0)  16.9 us
    all_to_all x1, starting transfers between devices, shards(): lax.all_to_all(jnp.broadcast_to(block[None], (ncol,) + block.shape), 'col...  12.4 us
    all_to_all x1, waiting for transfers between devices, shards(): lax.all_to_all(jnp.broadcast_to(block[None], (ncol,) + block.shape), 'col...  11.7 us
    pallas_call x1, Pallas kernels, build_taps(): pl.pallas_call(functools.partial(tap_kernel, taps, nrow, comp_here, event...  4.39 us
    all_to_all x1, starting transfers between devices, shards(): lax.all_to_all(jnp.broadcast_to(mine[None], (nrow,) + mine.shape), 'row',...  3.86 us
    pallas_call x1, Pallas kernels, build_panel(): pl.pallas_call(functools.partial(panel_kernel, nrow), out_shape=jax.Shape...  3.76 us
    dot_general x1, matrix products, shards(): jnp.dot(amplitude, basis, precision=high, preferred_element_type=jnp.floa...  3.01 us
  transfers between devices with their start and end apart: 2, of which 2 were waited for; matrix products, arithmetic and copies ran while one was open for 7% of the time, Pallas kernels for 0%

profile of v13, /device:TPU:1, one launch (start us, length us, event | category | flops | bytes accessed | tf_op | source)
XLA Modules:
  0.0 92.6 jit_solution(18361816746252733805)
XLA Ops:
  0.6 0.0 copy-start
  0.6 0.0 copy-start.1
  0.7 0.0 copy-start.2
  0.7 0.0 copy-start.3
  0.7 3.8 %shard_map.104 = f32[32,8,128]{2,1,0:T(8,128)} custom-call(f32[2048,128]{1,0:T(8,128)} %v_ref.1, f32[2048,256]{1,0:T(8,128)} %r_ref.1), custom_call_target="tpu_custom_call" | custom-call | tf_op jit(solution)/shard_map/pallas_call | solution.py:72
  4.4 22.9 %all_to_all.20 = f32[32,8,128]{2,1,0:T(8,128)S(1)} all-to-all(f32[32,8,128]{2,1,0:T(8,128)} %shard_map.104), channel_id=1, replica_groups=mesh['row'=32,'col'=16] {'row'}, dimensions={0} | all-to-all | bytes 262144 | tf_op jit(solution)/shard_map/all_to_all | solution.py:108
  27.3 0.7 broadcast_in_dim.12
  28.0 3.9 %all-to-all-start.1 = ((f32[32,8,128]{2,1,0:T(8,128)}), f32[32,8,128]{2,1,0:T(8,128)S(1)}, u32[]{:S(2)}, u32[]{:S(2)}) async-start(f32[32,8,128]{2,1,0:T(8,128)} %broadcast_in_dim.12), calls=%async_computation.1 | async-start | bytes 262144 | tf_op jit(solution)/shard_map/all_to_all | solution.py:109
  31.9 0.0 copy-done.3
  31.9 0.7 fusion.15
  32.6 0.9 copy.19
  33.4 1.7 %min.12.idx_ref = s32[2080]{0:T(1024)} reshape(s32[520,4]{1,0:T(8,128)} %copy.19) | data formatting | bytes 16640 | tf_op jit(solution)/shard_map/jit(clip)/min | solution.py:40
  35.2 0.7 maximum_select_fusion
  35.9 0.9 copy.20
  36.8 1.7 %select_n.9.w_ref = f32[2080]{0:T(1024)} reshape(f32[520,4]{1,0:T(8,128)} %copy.20) | data formatting | bytes 16640 | tf_op jit(solution)/shard_map/jit(_where)/select_n | solution.py:41
  38.5 2.5 %all-to-all-done.1 = f32[32,8,128]{2,1,0:T(8,128)S(1)} async-done(((f32[32,8,128]{2,1,0:T(8,128)}), f32[32,8,128]{2,1,0:T(8,128)S(1)}, u32[]{:S(2)}, u32[]{:S(2)}) %all-to-all-start.1) | async-done | bytes 131104 | tf_op jit(solution)/shard_map/all_to_all | solution.py:109
  41.0 0.3 fusion.13
  41.3 2.0 %fusion.rot_ref = f32[2048,128]{1,0:T(8,128)} fusion(f32[2048,128]{1,0:T(8,128)S(1)} %copy-done.2, f32[128,256]{1,0:T(8,128)S(1)} %fusion.13, f32[2048,256]{1,0:T(8,128)S(1)} %copy-done.1), kind=kOutput, calls=%fused_computation.1 | convolution fusion | flops 402915328 | bytes 4325376 | tf_op jit(solution)/shard_map/dot_general | solution.py:112
  43.3 4.4 %shard_map.105 = f32[32,24,128]{2,1,0:T(8,128)} custom-call(s32[2080]{0:T(1024)} %min.12.idx_ref, f32[2080]{0:T(1024)} %select_n.9.w_ref, f32[2048,128]{1,0:T(8,128)} %fusion.rot_ref), custom_call_target="tpu_custom_call" | custom-call | tf_op jit(solution)/shard_map/pallas_call | solution.py:44
  47.7 16.9 %all_to_all.21 = f32[32,24,128]{2,1,0:T(8,128)S(1)} all-to-all(f32[32,24,128]{2,1,0:T(8,128)} %shard_map.105), channel_id=1, replica_groups=mesh['row'=32,'col'=16] {'row'}, dimensions={0} | all-to-all | bytes 786432 | tf_op jit(solution)/shard_map/all_to_all | solution.py:124
  64.7 0.7 broadcast_in_dim.28
  65.4 12.4 %all-to-all-start.3 = ((f32[16,26,128]{2,1,0:T(8,128)}), f32[16,26,128]{2,1,0:T(8,128)S(1)}, u32[]{:S(2)}, u32[]{:S(2)}) async-start(f32[16,26,128]{2,1,0:T(8,128)} %broadcast_in_dim.28), calls=%async_computation.3 | async-start | bytes 524288 | tf_op jit(solution)/shard_map/all_to_all | solution.py:126
  77.8 11.7 %all-to-all-done.3 = f32[16,26,128]{2,1,0:T(8,128)S(1)} async-done(((f32[16,26,128]{2,1,0:T(8,128)}), f32[16,26,128]{2,1,0:T(8,128)S(1)}, u32[]{:S(2)}, u32[]{:S(2)}) %all-to-all-start.3) | async-done | bytes 213024 | tf_op jit(solution)/shard_map/all_to_all | solution.py:126
  89.6 3.0 %convolution_multiply_fusion = f32[8,16,64]{2,1,0:T(8,128)} fusion(f32[16,2048]{1,0:T(8,128)S(1)} %copy_bitcast_fusion, f32[8,2048]{1,0:T(8,128)S(1)} %slice_bitcast_fusion.1, f32[2048]{0:T(1024)S(1)} %bitcast.28, f32[64]{0:T(128)S(1)} %add_convert_fusion, f32[2048]{0:T(1024)S(1)} %bitcast.27), kind=kOutput, calls=%fused_computation.2 | convolution fusion | flops 101326848 | bytes 246016 | tf_op jit(solution)/shard_map/dot_general | solution.py:136
  (14 shorter events, 0.1 us)
Async XLA Ops:
  0.6 40.4 %copy-start = (f32[256,256]{1,0:T(8,128)S(1)}, f32[256,256]{1,0:T(8,128)}, u32[]{:S(2)}) copy-start(f32[256,256]{1,0:T(8,128)} %param.11) | copy-start | bytes 786436
  0.6 40.7 %copy-start.1 = (f32[2048,256]{1,0:T(8,128)S(1)}, f32[2048,256]{1,0:T(8,128)}, u32[]{:S(2)}) copy-start(f32[2048,256]{1,0:T(8,128)} %r_ref.1) | copy-start | bytes 6291460
  0.7 40.7 %copy-start.2 = (f32[2048,128]{1,0:T(8,128)S(1)}, f32[2048,128]{1,0:T(8,128)}, u32[]{:S(2)}) copy-start(f32[2048,128]{1,0:T(8,128)} %v_ref.1) | copy-start | bytes 3145732
  0.7 31.2 %copy-start.3 = (s32[8,4]{0,1:T(4,128)S(1)}, s32[8,4]{0,1:T(4,128)}, u32[]{:S(2)}) copy-start(s32[8,4]{0,1:T(4,128)} %param.14) | copy-start | bytes 388
  28.0 13.0 %all-to-all-start.1 = ((f32[32,8,128]{2,1,0:T(8,128)}), f32[32,8,128]{2,1,0:T(8,128)S(1)}, u32[]{:S(2)}, u32[]{:S(2)}) async-start(f32[32,8,128]{2,1,0:T(8,128)} %broadcast_in_dim.12), calls=%async_computation.1 | async-start | bytes 262144 | tf_op jit(solution)/shard_map/all_to_all | solution.py:109
  43.3 21.4 %copy-start.4 = (f32[128]{0:T(128)S(1)}, f32[128]{0:T(128)}, u32[]{:S(2)}) copy-start(f32[128]{0:T(128)} %param.17) | copy-start | bytes 1540
  43.3 21.4 %copy-start.5 = (f32[128]{0:T(128)S(1)}, f32[128]{0:T(128)}, u32[]{:S(2)}) copy-start(f32[128]{0:T(128)} %param.16) | copy-start | bytes 1540
  65.4 24.1 %all-to-all-start.3 = ((f32[16,26,128]{2,1,0:T(8,128)}), f32[16,26,128]{2,1,0:T(8,128)S(1)}, u32[]{:S(2)}, u32[]{:S(2)}) async-start(f32[16,26,128]{2,1,0:T(8,128)} %broadcast_in_dim.28), calls=%async_computation.3 | async-start | bytes 524288 | tf_op jit(solution)/shard_map/all_to_all | solution.py:126

commit v14 on v8

--- a/solution.py
+++ b/solution.py
@@ -87,6 +87,8 @@
     rotated = vectors - jnp.dot(
         reflectors, folded, precision=high, preferred_element_type=jnp.float32
     )
+    times = (col * samples + jnp.arange(samples)).astype(jnp.float32)
+    times, rotated = lax.optimization_barrier((times, rotated))
     send = build_taps(
         jnp.concatenate([station_rows, event_rows], 0),
         jnp.concatenate([station_weights, event_weights], 0),
@@ -103,7 +105,6 @@
     sources = parts[:, comp_here:comp_here + events].transpose(1, 0, 2).reshape(events, -1)
     freq = parts[:, comp_here + events].reshape(-1)
     damp = parts[:, comp_here + events + 1].reshape(-1)
-    times = (col * samples + jnp.arange(samples)).astype(jnp.float32)
     basis = mode_basis(freq, damp, times)
 
     factor = 1.0 / float(freq.shape[0]) ** 0.5

time: 92.5 us -> 92.4 us (level)
  waiting for transfers between devices: 18.2 us -> 15.6 us
  blocking collectives: 36.8 us -> 38.6 us
    all_to_all x1, waiting for transfers between devices: 11.7 us -> 9.15 us  [shards(): lax.all_to_all(partial_panel.reshape(nrow, prow, width), 'row', 0, 0).sum(0)]
    all_to_all x1, blocking collectives: 22.7 us -> 24.4 us  [shards(): lax.all_to_all(jnp.broadcast_to(block[None], (ncol,) + block.shape), 'col...]
where the time goes in v14:
time: 92.4 us; the launch traced here: 91.9 us
  blocking collectives  38.6 us (42%)
  starting transfers between devices  17.6 us (19%)
  waiting for transfers between devices  15.6 us (17%)
  matrix products  9.89 us (11%)
  Pallas kernels  4.39 us (5%)
  local copies, waits for them, and re-layouts  4.15 us (4%)
    all_to_all x1, blocking collectives, shards(): lax.all_to_all(jnp.broadcast_to(block[None], (ncol,) + block.shape), 'col...  24.4 us
    all_to_all x1, blocking collectives, shards(): got = lax.all_to_all(send, 'row', 0, 0).sum(0)  14.1 us
    all_to_all x1, starting transfers between devices, shards(): lax.all_to_all(partial_panel.reshape(nrow, prow, width), 'row', 0, 0).sum(0)  13.7 us
    all_to_all x1, waiting for transfers between devices, shards(): lax.all_to_all(partial_panel.reshape(nrow, prow, width), 'row', 0, 0).sum(0)  9.15 us
    all_to_all x1, waiting for transfers between devices, shards(): lax.all_to_all(jnp.broadcast_to(mine[None], (nrow,) + mine.shape), 'row',...  6.49 us
    pallas_call x1, Pallas kernels, build_taps(): pl.pallas_call(functools.partial(tap_kernel, taps, nrow, comp_here, event...  4.39 us
    all_to_all x1, starting transfers between devices, shards(): lax.all_to_all(jnp.broadcast_to(mine[None], (nrow,) + mine.shape), 'row',...  3.86 us
    dot_general x1, matrix products, shards(): jnp.dot(reflectors.T, vectors, precision=high, preferred_element_type=jnp...  3.68 us
  transfers between devices with their start and end apart: 2, of which 2 were waited for; matrix products, arithmetic and copies ran while one was open for 3% of the time, Pallas kernels for 0%

profile of v14, /device:TPU:1, one launch (start us, length us, event | category | flops | bytes accessed | tf_op | source)
XLA Modules:
  0.0 91.9 jit_solution(15430809868461243561)
XLA Ops:
  0.6 0.0 copy-start
  0.7 0.0 copy-start.3
  0.7 0.0 copy-start.2
  0.7 1.6 %copy-done = f32[2048,256]{1,0:T(8,128)S(1)} copy-done((f32[2048,256]{1,0:T(8,128)S(1)}, f32[2048,256]{1,0:T(8,128)}, u32[]{:S(2)}) %copy-start) | copy-done | bytes 2097176
  2.3 3.7 %convolution_bitcast_fusion.1 = f32[32,8,128]{2,1,0:T(8,128)} fusion(f32[2048,256]{1,0:T(8,128)S(1)} %copy-done, f32[2048,128]{1,0:T(8,128)} %param.9), kind=kOutput, calls=%fused_computation.2 | convolution fusion | flops 402653184 | bytes 3276800 | tf_op jit(solution)/shard_map/dot_general | solution.py:79
  5.9 13.7 %all-to-all-start = ((f32[32,8,128]{2,1,0:T(8,128)}), f32[32,8,128]{2,1,0:T(8,128)S(1)}, u32[]{:S(2)}, u32[]{:S(2)}) async-start(f32[32,8,128]{2,1,0:T(8,128)} %convolution_bitcast_fusion.1), calls=%async_computation | async-start | bytes 262144 | tf_op jit(solution)/shard_map/all_to_all | solution.py:83
  19.7 9.1 %all-to-all-done = f32[32,8,128]{2,1,0:T(8,128)S(1)} async-done(((f32[32,8,128]{2,1,0:T(8,128)}), f32[32,8,128]{2,1,0:T(8,128)S(1)}, u32[]{:S(2)}, u32[]{:S(2)}) %all-to-all-start) | async-done | bytes 131104 | tf_op jit(solution)/shard_map/all_to_all | solution.py:83
  28.9 0.7 broadcast_in_dim.12
  29.5 3.9 %all-to-all-start.1 = ((f32[32,8,128]{2,1,0:T(8,128)}), f32[32,8,128]{2,1,0:T(8,128)S(1)}, u32[]{:S(2)}, u32[]{:S(2)}) async-start(f32[32,8,128]{2,1,0:T(8,128)} %broadcast_in_dim.12), calls=%async_computation.1 | async-start | bytes 262144 | tf_op jit(solution)/shard_map/all_to_all | solution.py:84
  33.4 0.0 copy-done.3
  33.4 0.0 copy-done.2
  33.4 0.1 copy.19
  33.6 0.8 min.12.idx_ref
  34.4 0.8 maximum_select_fusion
  35.1 0.1 copy.20
  35.3 0.8 select_n.9.w_ref
  36.0 6.5 %all-to-all-done.1 = f32[32,8,128]{2,1,0:T(8,128)S(1)} async-done(((f32[32,8,128]{2,1,0:T(8,128)}), f32[32,8,128]{2,1,0:T(8,128)S(1)}, u32[]{:S(2)}, u32[]{:S(2)}) %all-to-all-start.1) | async-done | bytes 131104 | tf_op jit(solution)/shard_map/all_to_all | solution.py:84
  42.5 1.2 %fusion.13 = f32[128,256]{1,0:T(8,128)S(1)} fusion(f32[256,256]{1,0:T(8,128)} %param.11, f32[32,8,128]{2,1,0:T(8,128)S(1)} %all-to-all-done.1), kind=kOutput, calls=%fused_computation.18 | convolution fusion | flops 50331648 | bytes 524288 | tf_op jit(solution)/shard_map/dot_general | solution.py:86
  43.8 2.0 %fusion.rot_ref = f32[2048,128]{1,0:T(8,128)} fusion(f32[2048,128]{1,0:T(8,128)S(1)} %copy-done.1, f32[128,256]{1,0:T(8,128)S(1)} %fusion.13, f32[2048,256]{1,0:T(8,128)S(1)} %copy-done), kind=kOutput, calls=%fused_computation.1 | convolution fusion | flops 402915328 | bytes 4325376 | tf_op jit(solution)/shard_map/dot_general | solution.py:87
  45.8 4.4 %shard_map.104 = f32[32,24,128]{2,1,0:T(8,128)} custom-call(s32[2080]{0:T(1024)} %min.12.idx_ref, f32[2080]{0:T(1024)} %select_n.9.w_ref, f32[2048,128]{1,0:T(8,128)} %fusion.rot_ref), custom_call_target="tpu_custom_call" | custom-call | tf_op jit(solution)/shard_map/pallas_call | solution.py:44
  50.1 14.1 %all_to_all.20 = f32[32,24,128]{2,1,0:T(8,128)S(1)} all-to-all(f32[32,24,128]{2,1,0:T(8,128)} %shard_map.104), channel_id=1, replica_groups=mesh['row'=32,'col'=16] {'row'}, dimensions={0} | all-to-all | bytes 786432 | tf_op jit(solution)/shard_map/all_to_all | solution.py:101
  64.3 0.0 copy-done.4
  64.4 24.4 %all_to_all.21 = f32[16,26,128]{2,1,0:T(8,128)S(1)} all-to-all(f32[16,26,128]{2,1,0:T(8,128)S(1)} %broadcast_in_dim.28), channel_id=1, replica_groups=mesh['row'=32,'col'=16] {'col'}, dimensions={0} | all-to-all | bytes 425984 | tf_op jit(solution)/shard_map/all_to_all | solution.py:103
  88.9 3.0 %convolution_multiply_fusion = f32[8,16,64]{2,1,0:T(8,128)} fusion(f32[16,2048]{1,0:T(8,128)S(1)} %copy_bitcast_fusion, f32[8,2048]{1,0:T(8,128)S(1)} %slice_bitcast_fusion.1, f32[2048]{0:T(1024)S(1)} %bitcast.32, f32[64]{0:T(128)S(1)} %add_convert_fusion, f32[2048]{0:T(1024)S(1)} %bitcast.31), kind=kOutput, calls=%fused_computation.3 | convolution fusion | flops 101326848 | bytes 246016 | tf_op jit(solution)/shard_map/dot_general | solution.py:112
  (14 shorter events, 0.2 us)
Async XLA Ops:
  0.6 1.6 %copy-start = (f32[2048,256]{1,0:T(8,128)S(1)}, f32[2048,256]{1,0:T(8,128)}, u32[]{:S(2)}) copy-start(f32[2048,256]{1,0:T(8,128)} %param.10) | copy-start | bytes 6291460
  0.6 43.1 %copy-start.1 = (f32[2048,128]{1,0:T(8,128)S(1)}, f32[2048,128]{1,0:T(8,128)}, u32[]{:S(2)}) copy-start(f32[2048,128]{1,0:T(8,128)} %param.9) | copy-start | bytes 3145732
  0.7 32.7 %copy-start.3 = (s32[8,4]{0,1:T(4,128)S(1)}, s32[8,4]{0,1:T(4,128)}, u32[]{:S(2)}) copy-start(s32[8,4]{0,1:T(4,128)} %param.14) | copy-start | bytes 388
  0.7 32.7 %copy-start.2 = (s32[512,4]{0,1:T(4,128)S(1)}, s32[512,4]{0,1:T(4,128)}, u32[]{:S(2)}) copy-start(s32[512,4]{0,1:T(4,128)} %param.12) | copy-start | bytes 24580
  5.9 22.9 %all-to-all-start = ((f32[32,8,128]{2,1,0:T(8,128)}), f32[32,8,128]{2,1,0:T(8,128)S(1)}, u32[]{:S(2)}, u32[]{:S(2)}) async-start(f32[32,8,128]{2,1,0:T(8,128)} %convolution_bitcast_fusion.1), calls=%async_computation | async-start | bytes 262144 | tf_op jit(solution)/shard_map/all_to_all | solution.py:83
  29.5 13.0 %all-to-all-start.1 = ((f32[32,8,128]{2,1,0:T(8,128)}), f32[32,8,128]{2,1,0:T(8,128)S(1)}, u32[]{:S(2)}, u32[]{:S(2)}) async-start(f32[32,8,128]{2,1,0:T(8,128)} %broadcast_in_dim.12), calls=%async_computation.1 | async-start | bytes 262144 | tf_op jit(solution)/shard_map/all_to_all | solution.py:84
  45.8 18.6 %copy-start.4 = (f32[128]{0:T(128)S(1)}, f32[128]{0:T(128)}, u32[]{:S(2)}) copy-start(f32[128]{0:T(128)} %param.17) | copy-start | bytes 1540
  45.8 18.6 %copy-start.5 = (f32[128]{0:T(128)S(1)}, f32[128]{0:T(128)}, u32[]{:S(2)}) copy-start(f32[128]{0:T(128)} %param.16) | copy-start | bytes 1540

commit v15 on v8

--- a/solution.py
+++ b/solution.py
@@ -98,7 +98,8 @@
     )
     got = lax.all_to_all(send, "row", 0, 0).sum(0)
     block = jnp.concatenate([got, mode_freq[None], mode_damp[None]], 0)
-    parts = lax.all_to_all(jnp.broadcast_to(block[None], (ncol,) + block.shape), "col", 0, 0)
+    flat = jnp.broadcast_to(block.reshape(1, -1), (ncol, block.size))
+    parts = lax.all_to_all(flat, "col", 0, 0, tiled=True).reshape((ncol,) + block.shape)
     receivers = parts[:, :comp_here].transpose(1, 0, 2).reshape(comp_here, -1)
     sources = parts[:, comp_here:comp_here + events].transpose(1, 0, 2).reshape(events, -1)
     freq = parts[:, comp_here + events].reshape(-1)

time: 92.5 us -> 92.1 us (level)
  waiting for transfers between devices: 18.2 us -> 17.2 us
    all_to_all x1, waiting for transfers between devices: 11.7 us -> 10.7 us  [shards(): lax.all_to_all(flat, 'col', 0, 0, tiled=True).reshape((ncol,) + block.shape)]
where the time goes in v15:
time: 92.1 us; the launch traced here: 91.5 us
  blocking collectives  36.8 us (40%)
  waiting for transfers between devices  17.2 us (19%)
  starting transfers between devices  16.8 us (18%)
  matrix products  9.24 us (10%)
  local copies, waits for them, and re-layouts  4.96 us (5%)
  Pallas kernels  4.4 us (5%)
  other arithmetic  1.37 us (1%)
    all_to_all x1, blocking collectives, shards(): lax.all_to_all(partial_panel.reshape(nrow, prow, width), 'row', 0, 0).sum(0)  22.7 us
    all_to_all x1, blocking collectives, shards(): got = lax.all_to_all(send, 'row', 0, 0).sum(0)  14.1 us
    all_to_all x1, starting transfers between devices, shards(): lax.all_to_all(flat, 'col', 0, 0, tiled=True).reshape((ncol,) + block.shape)  12.9 us
    all_to_all x1, waiting for transfers between devices, shards(): lax.all_to_all(flat, 'col', 0, 0, tiled=True).reshape((ncol,) + block.shape)  10.7 us
    all_to_all x1, waiting for transfers between devices, shards(): lax.all_to_all(jnp.broadcast_to(mine[None], (nrow,) + mine.shape), 'row',...  6.48 us
    pallas_call x1, Pallas kernels, build_taps(): pl.pallas_call(functools.partial(tap_kernel, taps, nrow, comp_here, event...  4.4 us
    all_to_all x1, starting transfers between devices, shards(): lax.all_to_all(jnp.broadcast_to(mine[None], (nrow,) + mine.shape), 'row',...  3.86 us
    dot_general x1, matrix products, shards(): jnp.dot(reflectors.T, vectors, precision=high, preferred_element_type=jnp...  3.02 us
  transfers between devices with their start and end apart: 2, of which 2 were waited for; matrix products, arithmetic and copies ran while one was open for 3% of the time, Pallas kernels for 0%

profile of v15, /device:TPU:1, one launch (start us, length us, event | category | flops | bytes accessed | tf_op | source)
XLA Modules:
  0.0 91.5 jit_solution(203425794674339106)
XLA Ops:
  0.6 0.0 copy-start
  0.7 0.0 copy-start.3
  0.7 0.0 copy-start.2
  0.7 1.6 %copy-done = f32[2048,256]{1,0:T(8,128)S(1)} copy-done((f32[2048,256]{1,0:T(8,128)S(1)}, f32[2048,256]{1,0:T(8,128)}, u32[]{:S(2)}) %copy-start) | copy-done | bytes 2097176
  2.3 3.0 %convolution_bitcast_fusion.1 = f32[32,8,128]{2,1,0:T(8,128)S(1)} fusion(f32[2048,256]{1,0:T(8,128)S(1)} %copy-done, f32[2048,128]{1,0:T(8,128)} %param.9), kind=kOutput, calls=%fused_computation.2 | convolution fusion | flops 402653184 | bytes 3276800 | tf_op jit(solution)/shard_map/dot_general | solution.py:79
  5.3 22.7 %all_to_all.21 = f32[32,8,128]{2,1,0:T(8,128)S(1)} all-to-all(f32[32,8,128]{2,1,0:T(8,128)S(1)} %convolution_bitcast_fusion.1), channel_id=1, replica_groups=mesh['row'=32,'col'=16] {'row'}, dimensions={0} | all-to-all | bytes 262144 | tf_op jit(solution)/shard_map/all_to_all | solution.py:83
  28.0 0.7 broadcast_in_dim.25
  28.7 3.9 %all-to-all-start.1 = ((f32[32,8,128]{2,1,0:T(8,128)}), f32[32,8,128]{2,1,0:T(8,128)S(1)}, u32[]{:S(2)}, u32[]{:S(2)}) async-start(f32[32,8,128]{2,1,0:T(8,128)} %broadcast_in_dim.25), calls=%async_computation.1 | async-start | bytes 262144 | tf_op jit(solution)/shard_map/all_to_all | solution.py:84
  32.5 0.0 copy-done.3
  32.6 0.1 copy.20
  32.7 0.8 min.12.idx_ref
  33.5 0.8 maximum_select_fusion
  34.3 0.1 copy.21
  34.4 0.8 select_n.9.w_ref
  35.2 6.5 %all-to-all-done.1 = f32[32,8,128]{2,1,0:T(8,128)S(1)} async-done(((f32[32,8,128]{2,1,0:T(8,128)}), f32[32,8,128]{2,1,0:T(8,128)S(1)}, u32[]{:S(2)}, u32[]{:S(2)}) %all-to-all-start.1) | async-done | bytes 131104 | tf_op jit(solution)/shard_map/all_to_all | solution.py:84
  41.7 1.2 %fusion.13 = f32[128,256]{1,0:T(8,128)S(1)} fusion(f32[256,256]{1,0:T(8,128)} %param.11, f32[32,8,128]{2,1,0:T(8,128)S(1)} %all-to-all-done.1), kind=kOutput, calls=%fused_computation.18 | convolution fusion | flops 50331648 | bytes 524288 | tf_op jit(solution)/shard_map/dot_general | solution.py:86
  42.9 2.0 %fusion.rot_ref = f32[2048,128]{1,0:T(8,128)} fusion(f32[2048,128]{1,0:T(8,128)S(1)} %copy-done.1, f32[128,256]{1,0:T(8,128)S(1)} %fusion.13, f32[2048,256]{1,0:T(8,128)S(1)} %copy-done), kind=kOutput, calls=%fused_computation.1 | convolution fusion | flops 402915328 | bytes 4325376 | tf_op jit(solution)/shard_map/dot_general | solution.py:87
  44.9 4.4 %shard_map.104 = f32[32,24,128]{2,1,0:T(8,128)} custom-call(s32[2080]{0:T(1024)} %min.12.idx_ref, f32[2080]{0:T(1024)} %select_n.9.w_ref, f32[2048,128]{1,0:T(8,128)} %fusion.rot_ref), custom_call_target="tpu_custom_call" | custom-call | tf_op jit(solution)/shard_map/pallas_call | solution.py:44
  49.3 14.1 %all_to_all.22 = f32[32,24,128]{2,1,0:T(8,128)S(1)} all-to-all(f32[32,24,128]{2,1,0:T(8,128)} %shard_map.104), channel_id=1, replica_groups=mesh['row'=32,'col'=16] {'row'}, dimensions={0} | all-to-all | bytes 786432 | tf_op jit(solution)/shard_map/all_to_all | solution.py:99
  63.5 0.8 broadcast_in_dim.30
  64.3 12.9 %all-to-all-start.3 = ((f32[16,1,3328]{2,1,0:T(1,128)}), f32[16,1,3328]{2,1,0:T(1,128)S(1)}, u32[]{:S(2)}, u32[]{:S(2)}) async-start(f32[16,1,3328]{2,1,0:T(1,128)} %broadcast_in_dim.30), calls=%async_computation.3 | async-start | bytes 425984 | tf_op jit(solution)/shard_map/all_to_all | solution.py:102
  77.2 10.7 %all-to-all-done.3 = f32[16,1,3328]{2,1,0:T(1,128)S(1)} async-done(((f32[16,1,3328]{2,1,0:T(1,128)}), f32[16,1,3328]{2,1,0:T(1,128)S(1)}, u32[]{:S(2)}, u32[]{:S(2)}) %all-to-all-start.3) | async-done | bytes 213024 | tf_op jit(solution)/shard_map/all_to_all | solution.py:102
  87.9 0.5 reduce
  88.5 3.0 %convolution_multiply_fusion = f32[8,16,64]{2,1,0:T(8,128)} fusion(f32[16,2048]{1,0:T(8,128)S(1)} %copy_bitcast_fusion, f32[8,2048]{1,0:T(8,128)S(1)} %slice_bitcast_fusion.1, f32[2048]{0:T(1024)S(1)} %bitcast.34, f32[64]{0:T(128)S(1)} %add_convert_fusion, f32[2048]{0:T(1024)S(1)} %bitcast.33), kind=kOutput, calls=%fused_computation.3 | convolution fusion | flops 101326848 | bytes 246016 | tf_op jit(solution)/shard_map/dot_general | solution.py:112
  (16 shorter events, 0.2 us)
Async XLA Ops:
  0.6 1.6 %copy-start = (f32[2048,256]{1,0:T(8,128)S(1)}, f32[2048,256]{1,0:T(8,128)}, u32[]{:S(2)}) copy-start(f32[2048,256]{1,0:T(8,128)} %param.10) | copy-start | bytes 6291460
  0.6 42.3 %copy-start.1 = (f32[2048,128]{1,0:T(8,128)S(1)}, f32[2048,128]{1,0:T(8,128)}, u32[]{:S(2)}) copy-start(f32[2048,128]{1,0:T(8,128)} %param.9) | copy-start | bytes 3145732
  0.7 31.9 %copy-start.3 = (s32[8,4]{0,1:T(4,128)S(1)}, s32[8,4]{0,1:T(4,128)}, u32[]{:S(2)}) copy-start(s32[8,4]{0,1:T(4,128)} %param.14) | copy-start | bytes 388
  0.7 31.9 %copy-start.2 = (s32[512,4]{0,1:T(4,128)S(1)}, s32[512,4]{0,1:T(4,128)}, u32[]{:S(2)}) copy-start(s32[512,4]{0,1:T(4,128)} %param.12) | copy-start | bytes 24580
  28.7 13.0 %all-to-all-start.1 = ((f32[32,8,128]{2,1,0:T(8,128)}), f32[32,8,128]{2,1,0:T(8,128)S(1)}, u32[]{:S(2)}, u32[]{:S(2)}) async-start(f32[32,8,128]{2,1,0:T(8,128)} %broadcast_in_dim.25), calls=%async_computation.1 | async-start | bytes 262144 | tf_op jit(solution)/shard_map/all_to_all | solution.py:84
  44.9 18.6 %copy-start.4 = (f32[128]{0:T(128)S(1)}, f32[128]{0:T(128)}, u32[]{:S(2)}) copy-start(f32[128]{0:T(128)} %param.17) | copy-start | bytes 1540
  44.9 18.6 %copy-start.5 = (f32[128]{0:T(128)S(1)}, f32[128]{0:T(128)}, u32[]{:S(2)}) copy-start(f32[128]{0:T(128)} %param.16) | copy-start | bytes 1540
  64.3 23.6 %all-to-all-start.3 = ((f32[16,1,3328]{2,1,0:T(1,128)}), f32[16,1,3328]{2,1,0:T(1,128)S(1)}, u32[]{:S(2)}, u32[]{:S(2)}) async-start(f32[16,1,3328]{2,1,0:T(1,128)} %broadcast_in_dim.30), calls=%async_computation.3 | async-start | bytes 425984 | tf_op jit(solution)/shard_map/all_to_all | solution.py:102

commit v16 on v15

--- a/solution.py
+++ b/solution.py
@@ -10,7 +10,7 @@
 NT = 1024
 
 
-def tap_kernel(taps, nrow, comp_here, events, idx_ref, w_ref, rot_ref, send_ref):
+def tap_kernel(taps, nrow, comp_here, events, idx_ref, w_ref, rot_ref, send_ref, ev_ref):
     def tap_row(c):
         acc = None
         for t in range(taps):
@@ -20,13 +20,14 @@
             acc = v if acc is None else acc + v
         return acc
 
-    ev = [tap_row(nrow * comp_here + e) for e in range(events)]
+    for e in range(events):
+        ev_ref[pl.ds(e, 1), :] = tap_row(nrow * comp_here + e)
+    ev = ev_ref[...]
 
     def dest(j, carry):
         for cc in range(comp_here):
             send_ref[j, pl.ds(cc, 1), :] = tap_row(j * comp_here + cc)
-        for e in range(events):
-            send_ref[j, pl.ds(comp_here + e, 1), :] = ev[e]
+        send_ref[j, pl.ds(comp_here, events), :] = ev
         return carry
 
     lax.fori_loop(0, nrow, dest, 0)
@@ -46,6 +47,7 @@
         out_shape=jax.ShapeDtypeStruct((nrow, comp_here + events, width), jnp.float32),
         in_specs=[smem, smem, vmem],
         out_specs=vmem,
+        scratch_shapes=[pltpu.VMEM((events, width), jnp.float32)],
     )(idx, w, rotated)
 
 

time: 92.1 us -> 92.1 us (level)
  no operation moved by 1% of the time
where the time goes in v16:
time: 92.1 us; the launch traced here: 91.5 us
  blocking collectives  36.8 us (40%)
  waiting for transfers between devices  17.2 us (19%)
  starting transfers between devices  16.8 us (18%)
  matrix products  9.24 us (10%)
  local copies, waits for them, and re-layouts  4.96 us (5%)
  Pallas kernels  4.4 us (5%)
  other arithmetic  1.37 us (1%)
    all_to_all x1, blocking collectives, shards(): lax.all_to_all(partial_panel.reshape(nrow, prow, width), 'row', 0, 0).sum(0)  22.7 us
    all_to_all x1, blocking collectives, shards(): got = lax.all_to_all(send, 'row', 0, 0).sum(0)  14.1 us
    all_to_all x1, starting transfers between devices, shards(): lax.all_to_all(flat, 'col', 0, 0, tiled=True).reshape((ncol,) + block.shape)  12.9 us
    all_to_all x1, waiting for transfers between devices, shards(): lax.all_to_all(flat, 'col', 0, 0, tiled=True).reshape((ncol,) + block.shape)  10.7 us
    all_to_all x1, waiting for transfers between devices, shards(): lax.all_to_all(jnp.broadcast_to(mine[None], (nrow,) + mine.shape), 'row',...  6.48 us
    pallas_call x1, Pallas kernels, build_taps(): pl.pallas_call(functools.partial(tap_kernel, taps, nrow, comp_here, event...  4.4 us
    all_to_all x1, starting transfers between devices, shards(): lax.all_to_all(jnp.broadcast_to(mine[None], (nrow,) + mine.shape), 'row',...  3.86 us
    dot_general x1, matrix products, shards(): jnp.dot(reflectors.T, vectors, precision=high, preferred_element_type=jnp...  3.02 us
  transfers between devices with their start and end apart: 2, of which 2 were waited for; matrix products, arithmetic and copies ran while one was open for 3% of the time, Pallas kernels for 0%

profile of v16, /device:TPU:1, one launch (start us, length us, event | category | flops | bytes accessed | tf_op | source)
XLA Modules:
  0.0 91.5 jit_solution(10099265745033473881)
XLA Ops:
  0.6 0.0 copy-start
  0.7 0.0 copy-start.3
  0.7 0.0 copy-start.2
  0.7 1.6 %copy-done = f32[2048,256]{1,0:T(8,128)S(1)} copy-done((f32[2048,256]{1,0:T(8,128)S(1)}, f32[2048,256]{1,0:T(8,128)}, u32[]{:S(2)}) %copy-start) | copy-done | bytes 2097176
  2.3 3.0 %convolution_bitcast_fusion.1 = f32[32,8,128]{2,1,0:T(8,128)S(1)} fusion(f32[2048,256]{1,0:T(8,128)S(1)} %copy-done, f32[2048,128]{1,0:T(8,128)} %param.9), kind=kOutput, calls=%fused_computation.2 | convolution fusion | flops 402653184 | bytes 3276800 | tf_op jit(solution)/shard_map/dot_general | solution.py:81
  5.3 22.7 %all_to_all.21 = f32[32,8,128]{2,1,0:T(8,128)S(1)} all-to-all(f32[32,8,128]{2,1,0:T(8,128)S(1)} %convolution_bitcast_fusion.1), channel_id=1, replica_groups=mesh['row'=32,'col'=16] {'row'}, dimensions={0} | all-to-all | bytes 262144 | tf_op jit(solution)/shard_map/all_to_all | solution.py:85
  28.0 0.7 broadcast_in_dim.25
  28.7 3.9 %all-to-all-start.1 = ((f32[32,8,128]{2,1,0:T(8,128)}), f32[32,8,128]{2,1,0:T(8,128)S(1)}, u32[]{:S(2)}, u32[]{:S(2)}) async-start(f32[32,8,128]{2,1,0:T(8,128)} %broadcast_in_dim.25), calls=%async_computation.1 | async-start | bytes 262144 | tf_op jit(solution)/shard_map/all_to_all | solution.py:86
  32.5 0.0 copy-done.3
  32.6 0.1 copy.20
  32.7 0.8 min.12.idx_ref
  33.5 0.8 maximum_select_fusion
  34.3 0.1 copy.21
  34.4 0.8 select_n.9.w_ref
  35.2 6.5 %all-to-all-done.1 = f32[32,8,128]{2,1,0:T(8,128)S(1)} async-done(((f32[32,8,128]{2,1,0:T(8,128)}), f32[32,8,128]{2,1,0:T(8,128)S(1)}, u32[]{:S(2)}, u32[]{:S(2)}) %all-to-all-start.1) | async-done | bytes 131104 | tf_op jit(solution)/shard_map/all_to_all | solution.py:86
  41.7 1.2 %fusion.13 = f32[128,256]{1,0:T(8,128)S(1)} fusion(f32[256,256]{1,0:T(8,128)} %param.11, f32[32,8,128]{2,1,0:T(8,128)S(1)} %all-to-all-done.1), kind=kOutput, calls=%fused_computation.18 | convolution fusion | flops 50331648 | bytes 524288 | tf_op jit(solution)/shard_map/dot_general | solution.py:88
  42.9 2.0 %fusion.rot_ref = f32[2048,128]{1,0:T(8,128)} fusion(f32[2048,128]{1,0:T(8,128)S(1)} %copy-done.1, f32[128,256]{1,0:T(8,128)S(1)} %fusion.13, f32[2048,256]{1,0:T(8,128)S(1)} %copy-done), kind=kOutput, calls=%fused_computation.1 | convolution fusion | flops 402915328 | bytes 4325376 | tf_op jit(solution)/shard_map/dot_general | solution.py:89
  44.9 4.4 %shard_map.104 = f32[32,24,128]{2,1,0:T(8,128)} custom-call(s32[2080]{0:T(1024)} %min.12.idx_ref, f32[2080]{0:T(1024)} %select_n.9.w_ref, f32[2048,128]{1,0:T(8,128)} %fusion.rot_ref), custom_call_target="tpu_custom_call" | custom-call | tf_op jit(solution)/shard_map/pallas_call | solution.py:45
  49.3 14.1 %all_to_all.22 = f32[32,24,128]{2,1,0:T(8,128)S(1)} all-to-all(f32[32,24,128]{2,1,0:T(8,128)} %shard_map.104), channel_id=1, replica_groups=mesh['row'=32,'col'=16] {'row'}, dimensions={0} | all-to-all | bytes 786432 | tf_op jit(solution)/shard_map/all_to_all | solution.py:101
  63.5 0.8 broadcast_in_dim.30
  64.3 12.9 %all-to-all-start.3 = ((f32[16,1,3328]{2,1,0:T(1,128)}), f32[16,1,3328]{2,1,0:T(1,128)S(1)}, u32[]{:S(2)}, u32[]{:S(2)}) async-start(f32[16,1,3328]{2,1,0:T(1,128)} %broadcast_in_dim.30), calls=%async_computation.3 | async-start | bytes 425984 | tf_op jit(solution)/shard_map/all_to_all | solution.py:104
  77.2 10.7 %all-to-all-done.3 = f32[16,1,3328]{2,1,0:T(1,128)S(1)} async-done(((f32[16,1,3328]{2,1,0:T(1,128)}), f32[16,1,3328]{2,1,0:T(1,128)S(1)}, u32[]{:S(2)}, u32[]{:S(2)}) %all-to-all-start.3) | async-done | bytes 213024 | tf_op jit(solution)/shard_map/all_to_all | solution.py:104
  87.9 0.5 reduce
  88.5 3.0 %convolution_multiply_fusion = f32[8,16,64]{2,1,0:T(8,128)} fusion(f32[16,2048]{1,0:T(8,128)S(1)} %copy_bitcast_fusion, f32[8,2048]{1,0:T(8,128)S(1)} %slice_bitcast_fusion.1, f32[2048]{0:T(1024)S(1)} %bitcast.34, f32[64]{0:T(128)S(1)} %add_convert_fusion, f32[2048]{0:T(1024)S(1)} %bitcast.33), kind=kOutput, calls=%fused_computation.3 | convolution fusion | flops 101326848 | bytes 246016 | tf_op jit(solution)/shard_map/dot_general | solution.py:114
  (16 shorter events, 0.2 us)
Async XLA Ops:
  0.6 1.6 %copy-start = (f32[2048,256]{1,0:T(8,128)S(1)}, f32[2048,256]{1,0:T(8,128)}, u32[]{:S(2)}) copy-start(f32[2048,256]{1,0:T(8,128)} %param.10) | copy-start | bytes 6291460
  0.6 42.3 %copy-start.1 = (f32[2048,128]{1,0:T(8,128)S(1)}, f32[2048,128]{1,0:T(8,128)}, u32[]{:S(2)}) copy-start(f32[2048,128]{1,0:T(8,128)} %param.9) | copy-start | bytes 3145732
  0.7 31.9 %copy-start.3 = (s32[8,4]{0,1:T(4,128)S(1)}, s32[8,4]{0,1:T(4,128)}, u32[]{:S(2)}) copy-start(s32[8,4]{0,1:T(4,128)} %param.14) | copy-start | bytes 388
  0.7 31.9 %copy-start.2 = (s32[512,4]{0,1:T(4,128)S(1)}, s32[512,4]{0,1:T(4,128)}, u32[]{:S(2)}) copy-start(s32[512,4]{0,1:T(4,128)} %param.12) | copy-start | bytes 24580
  28.7 13.0 %all-to-all-start.1 = ((f32[32,8,128]{2,1,0:T(8,128)}), f32[32,8,128]{2,1,0:T(8,128)S(1)}, u32[]{:S(2)}, u32[]{:S(2)}) async-start(f32[32,8,128]{2,1,0:T(8,128)} %broadcast_in_dim.25), calls=%async_computation.1 | async-start | bytes 262144 | tf_op jit(solution)/shard_map/all_to_all | solution.py:86
  44.9 18.6 %copy-start.4 = (f32[128]{0:T(128)S(1)}, f32[128]{0:T(128)}, u32[]{:S(2)}) copy-start(f32[128]{0:T(128)} %param.17) | copy-start | bytes 1540
  44.9 18.6 %copy-start.5 = (f32[128]{0:T(128)S(1)}, f32[128]{0:T(128)}, u32[]{:S(2)}) copy-start(f32[128]{0:T(128)} %param.16) | copy-start | bytes 1540
  64.3 23.6 %all-to-all-start.3 = ((f32[16,1,3328]{2,1,0:T(1,128)}), f32[16,1,3328]{2,1,0:T(1,128)S(1)}, u32[]{:S(2)}, u32[]{:S(2)}) async-start(f32[16,1,3328]{2,1,0:T(1,128)} %broadcast_in_dim.30), calls=%async_computation.3 | async-start | bytes 425984 | tf_op jit(solution)/shard_map/all_to_all | solution.py:104

commit v17 on v16

--- a/solution.py
+++ b/solution.py
@@ -25,8 +25,9 @@
     ev = ev_ref[...]
 
     def dest(j, carry):
-        for cc in range(comp_here):
-            send_ref[j, pl.ds(cc, 1), :] = tap_row(j * comp_here + cc)
+        send_ref[j, pl.ds(0, comp_here), :] = jnp.concatenate(
+            [tap_row(j * comp_here + cc) for cc in range(comp_here)], 0
+        )
         send_ref[j, pl.ds(comp_here, events), :] = ev
         return carry
 

time: 92.1 us -> 92.6 us (level)
  no operation moved by 1% of the time
where the time goes in v17:
time: 92.6 us; the launch traced here: 92 us
  blocking collectives  36.8 us (40%)
  waiting for transfers between devices  17.2 us (19%)
  starting transfers between devices  16.8 us (18%)
  matrix products  9.24 us (10%)
  local copies, waits for them, and re-layouts  4.96 us (5%)
  Pallas kernels  4.87 us (5%)
  other arithmetic  1.37 us (1%)
    all_to_all x1, blocking collectives, shards(): lax.all_to_all(partial_panel.reshape(nrow, prow, width), 'row', 0, 0).sum(0)  22.7 us
    all_to_all x1, blocking collectives, shards(): got = lax.all_to_all(send, 'row', 0, 0).sum(0)  14.1 us
    all_to_all x1, starting transfers between devices, shards(): lax.all_to_all(flat, 'col', 0, 0, tiled=True).reshape((ncol,) + block.shape)  12.9 us
    all_to_all x1, waiting for transfers between devices, shards(): lax.all_to_all(flat, 'col', 0, 0, tiled=True).reshape((ncol,) + block.shape)  10.7 us
    all_to_all x1, waiting for transfers between devices, shards(): lax.all_to_all(jnp.broadcast_to(mine[None], (nrow,) + mine.shape), 'row',...  6.48 us
    pallas_call x1, Pallas kernels, build_taps(): pl.pallas_call(functools.partial(tap_kernel, taps, nrow, comp_here, event...  4.87 us
    all_to_all x1, starting transfers between devices, shards(): lax.all_to_all(jnp.broadcast_to(mine[None], (nrow,) + mine.shape), 'row',...  3.86 us
    dot_general x1, matrix products, shards(): jnp.dot(reflectors.T, vectors, precision=high, preferred_element_type=jnp...  3.02 us
  transfers between devices with their start and end apart: 2, of which 2 were waited for; matrix products, arithmetic and copies ran while one was open for 3% of the time, Pallas kernels for 0%

profile of v17, /device:TPU:1, one launch (start us, length us, event | category | flops | bytes accessed | tf_op | source)
XLA Modules:
  0.0 92.0 jit_solution(8940868215508450728)
XLA Ops:
  0.6 0.0 copy-start
  0.7 0.0 copy-start.3
  0.7 0.0 copy-start.2
  0.7 1.6 %copy-done = f32[2048,256]{1,0:T(8,128)S(1)} copy-done((f32[2048,256]{1,0:T(8,128)S(1)}, f32[2048,256]{1,0:T(8,128)}, u32[]{:S(2)}) %copy-start) | copy-done | bytes 2097176
  2.3 3.0 %convolution_bitcast_fusion.1 = f32[32,8,128]{2,1,0:T(8,128)S(1)} fusion(f32[2048,256]{1,0:T(8,128)S(1)} %copy-done, f32[2048,128]{1,0:T(8,128)} %param.9), kind=kOutput, calls=%fused_computation.2 | convolution fusion | flops 402653184 | bytes 3276800 | tf_op jit(solution)/shard_map/dot_general | solution.py:82
  5.3 22.7 %all_to_all.21 = f32[32,8,128]{2,1,0:T(8,128)S(1)} all-to-all(f32[32,8,128]{2,1,0:T(8,128)S(1)} %convolution_bitcast_fusion.1), channel_id=1, replica_groups=mesh['row'=32,'col'=16] {'row'}, dimensions={0} | all-to-all | bytes 262144 | tf_op jit(solution)/shard_map/all_to_all | solution.py:86
  28.0 0.7 broadcast_in_dim.25
  28.7 3.9 %all-to-all-start.1 = ((f32[32,8,128]{2,1,0:T(8,128)}), f32[32,8,128]{2,1,0:T(8,128)S(1)}, u32[]{:S(2)}, u32[]{:S(2)}) async-start(f32[32,8,128]{2,1,0:T(8,128)} %broadcast_in_dim.25), calls=%async_computation.1 | async-start | bytes 262144 | tf_op jit(solution)/shard_map/all_to_all | solution.py:87
  32.5 0.0 copy-done.3
  32.6 0.1 copy.20
  32.7 0.8 min.12.idx_ref
  33.5 0.8 maximum_select_fusion
  34.3 0.1 copy.21
  34.4 0.8 select_n.9.w_ref
  35.2 6.5 %all-to-all-done.1 = f32[32,8,128]{2,1,0:T(8,128)S(1)} async-done(((f32[32,8,128]{2,1,0:T(8,128)}), f32[32,8,128]{2,1,0:T(8,128)S(1)}, u32[]{:S(2)}, u32[]{:S(2)}) %all-to-all-start.1) | async-done | bytes 131104 | tf_op jit(solution)/shard_map/all_to_all | solution.py:87
  41.7 1.2 %fusion.13 = f32[128,256]{1,0:T(8,128)S(1)} fusion(f32[256,256]{1,0:T(8,128)} %param.11, f32[32,8,128]{2,1,0:T(8,128)S(1)} %all-to-all-done.1), kind=kOutput, calls=%fused_computation.18 | convolution fusion | flops 50331648 | bytes 524288 | tf_op jit(solution)/shard_map/dot_general | solution.py:89
  42.9 2.0 %fusion.rot_ref = f32[2048,128]{1,0:T(8,128)} fusion(f32[2048,128]{1,0:T(8,128)S(1)} %copy-done.1, f32[128,256]{1,0:T(8,128)S(1)} %fusion.13, f32[2048,256]{1,0:T(8,128)S(1)} %copy-done), kind=kOutput, calls=%fused_computation.1 | convolution fusion | flops 402915328 | bytes 4325376 | tf_op jit(solution)/shard_map/dot_general | solution.py:90
  44.9 4.9 %shard_map.104 = f32[32,24,128]{2,1,0:T(8,128)} custom-call(s32[2080]{0:T(1024)} %min.12.idx_ref, f32[2080]{0:T(1024)} %select_n.9.w_ref, f32[2048,128]{1,0:T(8,128)} %fusion.rot_ref), custom_call_target="tpu_custom_call" | custom-call | tf_op jit(solution)/shard_map/pallas_call | solution.py:46
  49.8 14.1 %all_to_all.22 = f32[32,24,128]{2,1,0:T(8,128)S(1)} all-to-all(f32[32,24,128]{2,1,0:T(8,128)} %shard_map.104), channel_id=1, replica_groups=mesh['row'=32,'col'=16] {'row'}, dimensions={0} | all-to-all | bytes 786432 | tf_op jit(solution)/shard_map/all_to_all | solution.py:102
  64.0 0.8 broadcast_in_dim.30
  64.8 12.9 %all-to-all-start.3 = ((f32[16,1,3328]{2,1,0:T(1,128)}), f32[16,1,3328]{2,1,0:T(1,128)S(1)}, u32[]{:S(2)}, u32[]{:S(2)}) async-start(f32[16,1,3328]{2,1,0:T(1,128)} %broadcast_in_dim.30), calls=%async_computation.3 | async-start | bytes 425984 | tf_op jit(solution)/shard_map/all_to_all | solution.py:105
  77.7 10.7 %all-to-all-done.3 = f32[16,1,3328]{2,1,0:T(1,128)S(1)} async-done(((f32[16,1,3328]{2,1,0:T(1,128)}), f32[16,1,3328]{2,1,0:T(1,128)S(1)}, u32[]{:S(2)}, u32[]{:S(2)}) %all-to-all-start.3) | async-done | bytes 213024 | tf_op jit(solution)/shard_map/all_to_all | solution.py:105
  88.4 0.5 reduce
  89.0 3.0 %convolution_multiply_fusion = f32[8,16,64]{2,1,0:T(8,128)} fusion(f32[16,2048]{1,0:T(8,128)S(1)} %copy_bitcast_fusion, f32[8,2048]{1,0:T(8,128)S(1)} %slice_bitcast_fusion.1, f32[2048]{0:T(1024)S(1)} %bitcast.34, f32[64]{0:T(128)S(1)} %add_convert_fusion, f32[2048]{0:T(1024)S(1)} %bitcast.33), kind=kOutput, calls=%fused_computation.3 | convolution fusion | flops 101326848 | bytes 246016 | tf_op jit(solution)/shard_map/dot_general | solution.py:115
  (16 shorter events, 0.2 us)
Async XLA Ops:
  0.6 1.6 %copy-start = (f32[2048,256]{1,0:T(8,128)S(1)}, f32[2048,256]{1,0:T(8,128)}, u32[]{:S(2)}) copy-start(f32[2048,256]{1,0:T(8,128)} %param.10) | copy-start | bytes 6291460
  0.6 42.3 %copy-start.1 = (f32[2048,128]{1,0:T(8,128)S(1)}, f32[2048,128]{1,0:T(8,128)}, u32[]{:S(2)}) copy-start(f32[2048,128]{1,0:T(8,128)} %param.9) | copy-start | bytes 3145732
  0.7 31.9 %copy-start.3 = (s32[8,4]{0,1:T(4,128)S(1)}, s32[8,4]{0,1:T(4,128)}, u32[]{:S(2)}) copy-start(s32[8,4]{0,1:T(4,128)} %param.14) | copy-start | bytes 388
  0.7 31.9 %copy-start.2 = (s32[512,4]{0,1:T(4,128)S(1)}, s32[512,4]{0,1:T(4,128)}, u32[]{:S(2)}) copy-start(s32[512,4]{0,1:T(4,128)} %param.12) | copy-start | bytes 24580
  28.7 13.0 %all-to-all-start.1 = ((f32[32,8,128]{2,1,0:T(8,128)}), f32[32,8,128]{2,1,0:T(8,128)S(1)}, u32[]{:S(2)}, u32[]{:S(2)}) async-start(f32[32,8,128]{2,1,0:T(8,128)} %broadcast_in_dim.25), calls=%async_computation.1 | async-start | bytes 262144 | tf_op jit(solution)/shard_map/all_to_all | solution.py:87
  44.9 19.0 %copy-start.4 = (f32[128]{0:T(128)S(1)}, f32[128]{0:T(128)}, u32[]{:S(2)}) copy-start(f32[128]{0:T(128)} %param.17) | copy-start | bytes 1540
  44.9 19.0 %copy-start.5 = (f32[128]{0:T(128)S(1)}, f32[128]{0:T(128)}, u32[]{:S(2)}) copy-start(f32[128]{0:T(128)} %param.16) | copy-start | bytes 1540
  64.8 23.6 %all-to-all-start.3 = ((f32[16,1,3328]{2,1,0:T(1,128)}), f32[16,1,3328]{2,1,0:T(1,128)S(1)}, u32[]{:S(2)}, u32[]{:S(2)}) async-start(f32[16,1,3328]{2,1,0:T(1,128)} %broadcast_in_dim.30), calls=%async_computation.3 | async-start | bytes 425984 | tf_op jit(solution)/shard_map/all_to_all | solution.py:105

commit v18 on v16

--- a/solution.py
+++ b/solution.py
@@ -12,13 +12,10 @@
 
 def tap_kernel(taps, nrow, comp_here, events, idx_ref, w_ref, rot_ref, send_ref, ev_ref):
     def tap_row(c):
-        acc = None
-        for t in range(taps):
-            i = idx_ref[c * taps + t]
-            w = w_ref[c * taps + t]
-            v = w * rot_ref[pl.ds(i, 1), :]
-            acc = v if acc is None else acc + v
-        return acc
+        terms = [w_ref[c * taps + t] * rot_ref[pl.ds(idx_ref[c * taps + t], 1), :] for t in range(taps)]
+        while len(terms) > 1:
+            terms = [terms[k] + terms[k + 1] for k in range(0, len(terms) - 1, 2)] + terms[len(terms) - len(terms) % 2:]
+        return terms[0]
 
     for e in range(events):
         ev_ref[pl.ds(e, 1), :] = tap_row(nrow * comp_here + e)
@@ -30,7 +27,7 @@
         send_ref[j, pl.ds(comp_here, events), :] = ev
         return carry
 
-    lax.fori_loop(0, nrow, dest, 0)
+    lax.fori_loop(0, nrow, dest, 0, unroll=2)
 
 
 def build_taps(rows, weights, first, nrow, comp_here, events, rotated):

time: 92.1 us -> 92 us (level)
  no operation moved by 1% of the time
where the time goes in v18:
time: 92 us; the launch traced here: 91.4 us
  blocking collectives  36.8 us (40%)
  waiting for transfers between devices  17.2 us (19%)
  starting transfers between devices  16.8 us (18%)
  matrix products  9.24 us (10%)
  local copies, waits for them, and re-layouts  4.96 us (5%)
  Pallas kernels  4.33 us (5%)
  other arithmetic  1.37 us (1%)
    all_to_all x1, blocking collectives, shards(): lax.all_to_all(partial_panel.reshape(nrow, prow, width), 'row', 0, 0).sum(0)  22.7 us
    all_to_all x1, blocking collectives, shards(): got = lax.all_to_all(send, 'row', 0, 0).sum(0)  14.1 us
    all_to_all x1, starting transfers between devices, shards(): lax.all_to_all(flat, 'col', 0, 0, tiled=True).reshape((ncol,) + block.shape)  12.9 us
    all_to_all x1, waiting for transfers between devices, shards(): lax.all_to_all(flat, 'col', 0, 0, tiled=True).reshape((ncol,) + block.shape)  10.7 us
    all_to_all x1, waiting for transfers between devices, shards(): lax.all_to_all(jnp.broadcast_to(mine[None], (nrow,) + mine.shape), 'row',...  6.48 us
    pallas_call x1, Pallas kernels, build_taps(): pl.pallas_call(functools.partial(tap_kernel, taps, nrow, comp_here, event...  4.33 us
    all_to_all x1, starting transfers between devices, shards(): lax.all_to_all(jnp.broadcast_to(mine[None], (nrow,) + mine.shape), 'row',...  3.86 us
    dot_general x1, matrix products, shards(): jnp.dot(reflectors.T, vectors, precision=high, preferred_element_type=jnp...  3.02 us
  transfers between devices with their start and end apart: 2, of which 2 were waited for; matrix products, arithmetic and copies ran while one was open for 3% of the time, Pallas kernels for 0%

profile of v18, /device:TPU:1, one launch (start us, length us, event | category | flops | bytes accessed | tf_op | source)
XLA Modules:
  0.0 91.4 jit_solution(12989897072167550869)
XLA Ops:
  0.6 0.0 copy-start
  0.7 0.0 copy-start.3
  0.7 0.0 copy-start.2
  0.7 1.6 %copy-done = f32[2048,256]{1,0:T(8,128)S(1)} copy-done((f32[2048,256]{1,0:T(8,128)S(1)}, f32[2048,256]{1,0:T(8,128)}, u32[]{:S(2)}) %copy-start) | copy-done | bytes 2097176
  2.3 3.0 %convolution_bitcast_fusion.1 = f32[32,8,128]{2,1,0:T(8,128)S(1)} fusion(f32[2048,256]{1,0:T(8,128)S(1)} %copy-done, f32[2048,128]{1,0:T(8,128)} %param.9), kind=kOutput, calls=%fused_computation.2 | convolution fusion | flops 402653184 | bytes 3276800 | tf_op jit(solution)/shard_map/dot_general | solution.py:78
  5.3 22.7 %all_to_all.21 = f32[32,8,128]{2,1,0:T(8,128)S(1)} all-to-all(f32[32,8,128]{2,1,0:T(8,128)S(1)} %convolution_bitcast_fusion.1), channel_id=1, replica_groups=mesh['row'=32,'col'=16] {'row'}, dimensions={0} | all-to-all | bytes 262144 | tf_op jit(solution)/shard_map/all_to_all | solution.py:82
  28.0 0.7 broadcast_in_dim.25
  28.7 3.9 %all-to-all-start.1 = ((f32[32,8,128]{2,1,0:T(8,128)}), f32[32,8,128]{2,1,0:T(8,128)S(1)}, u32[]{:S(2)}, u32[]{:S(2)}) async-start(f32[32,8,128]{2,1,0:T(8,128)} %broadcast_in_dim.25), calls=%async_computation.1 | async-start | bytes 262144 | tf_op jit(solution)/shard_map/all_to_all | solution.py:83
  32.5 0.0 copy-done.3
  32.6 0.1 copy.20
  32.7 0.8 min.12.idx_ref
  33.5 0.8 maximum_select_fusion
  34.3 0.1 copy.21
  34.4 0.8 select_n.9.w_ref
  35.2 6.5 %all-to-all-done.1 = f32[32,8,128]{2,1,0:T(8,128)S(1)} async-done(((f32[32,8,128]{2,1,0:T(8,128)}), f32[32,8,128]{2,1,0:T(8,128)S(1)}, u32[]{:S(2)}, u32[]{:S(2)}) %all-to-all-start.1) | async-done | bytes 131104 | tf_op jit(solution)/shard_map/all_to_all | solution.py:83
  41.7 1.2 %fusion.13 = f32[128,256]{1,0:T(8,128)S(1)} fusion(f32[256,256]{1,0:T(8,128)} %param.11, f32[32,8,128]{2,1,0:T(8,128)S(1)} %all-to-all-done.1), kind=kOutput, calls=%fused_computation.18 | convolution fusion | flops 50331648 | bytes 524288 | tf_op jit(solution)/shard_map/dot_general | solution.py:85
  42.9 2.0 %fusion.rot_ref = f32[2048,128]{1,0:T(8,128)} fusion(f32[2048,128]{1,0:T(8,128)S(1)} %copy-done.1, f32[128,256]{1,0:T(8,128)S(1)} %fusion.13, f32[2048,256]{1,0:T(8,128)S(1)} %copy-done), kind=kOutput, calls=%fused_computation.1 | convolution fusion | flops 402915328 | bytes 4325376 | tf_op jit(solution)/shard_map/dot_general | solution.py:86
  44.9 4.3 %shard_map.104 = f32[32,24,128]{2,1,0:T(8,128)} custom-call(s32[2080]{0:T(1024)} %min.12.idx_ref, f32[2080]{0:T(1024)} %select_n.9.w_ref, f32[2048,128]{1,0:T(8,128)} %fusion.rot_ref), custom_call_target="tpu_custom_call" | custom-call | tf_op jit(solution)/shard_map/pallas_call | solution.py:42
  49.2 14.1 %all_to_all.22 = f32[32,24,128]{2,1,0:T(8,128)S(1)} all-to-all(f32[32,24,128]{2,1,0:T(8,128)} %shard_map.104), channel_id=1, replica_groups=mesh['row'=32,'col'=16] {'row'}, dimensions={0} | all-to-all | bytes 786432 | tf_op jit(solution)/shard_map/all_to_all | solution.py:98
  63.4 0.8 broadcast_in_dim.30
  64.2 12.9 %all-to-all-start.3 = ((f32[16,1,3328]{2,1,0:T(1,128)}), f32[16,1,3328]{2,1,0:T(1,128)S(1)}, u32[]{:S(2)}, u32[]{:S(2)}) async-start(f32[16,1,3328]{2,1,0:T(1,128)} %broadcast_in_dim.30), calls=%async_computation.3 | async-start | bytes 425984 | tf_op jit(solution)/shard_map/all_to_all | solution.py:101
  77.1 10.7 %all-to-all-done.3 = f32[16,1,3328]{2,1,0:T(1,128)S(1)} async-done(((f32[16,1,3328]{2,1,0:T(1,128)}), f32[16,1,3328]{2,1,0:T(1,128)S(1)}, u32[]{:S(2)}, u32[]{:S(2)}) %all-to-all-start.3) | async-done | bytes 213024 | tf_op jit(solution)/shard_map/all_to_all | solution.py:101
  87.8 0.5 reduce
  88.4 3.0 %convolution_multiply_fusion = f32[8,16,64]{2,1,0:T(8,128)} fusion(f32[16,2048]{1,0:T(8,128)S(1)} %copy_bitcast_fusion, f32[8,2048]{1,0:T(8,128)S(1)} %slice_bitcast_fusion.1, f32[2048]{0:T(1024)S(1)} %bitcast.34, f32[64]{0:T(128)S(1)} %add_convert_fusion, f32[2048]{0:T(1024)S(1)} %bitcast.33), kind=kOutput, calls=%fused_computation.3 | convolution fusion | flops 101326848 | bytes 246016 | tf_op jit(solution)/shard_map/dot_general | solution.py:111
  (16 shorter events, 0.2 us)
Async XLA Ops:
  0.6 1.6 %copy-start = (f32[2048,256]{1,0:T(8,128)S(1)}, f32[2048,256]{1,0:T(8,128)}, u32[]{:S(2)}) copy-start(f32[2048,256]{1,0:T(8,128)} %param.10) | copy-start | bytes 6291460
  0.6 42.3 %copy-start.1 = (f32[2048,128]{1,0:T(8,128)S(1)}, f32[2048,128]{1,0:T(8,128)}, u32[]{:S(2)}) copy-start(f32[2048,128]{1,0:T(8,128)} %param.9) | copy-start | bytes 3145732
  0.7 31.9 %copy-start.3 = (s32[8,4]{0,1:T(4,128)S(1)}, s32[8,4]{0,1:T(4,128)}, u32[]{:S(2)}) copy-start(s32[8,4]{0,1:T(4,128)} %param.14) | copy-start | bytes 388
  0.7 31.9 %copy-start.2 = (s32[512,4]{0,1:T(4,128)S(1)}, s32[512,4]{0,1:T(4,128)}, u32[]{:S(2)}) copy-start(s32[512,4]{0,1:T(4,128)} %param.12) | copy-start | bytes 24580
  28.7 13.0 %all-to-all-start.1 = ((f32[32,8,128]{2,1,0:T(8,128)}), f32[32,8,128]{2,1,0:T(8,128)S(1)}, u32[]{:S(2)}, u32[]{:S(2)}) async-start(f32[32,8,128]{2,1,0:T(8,128)} %broadcast_in_dim.25), calls=%async_computation.1 | async-start | bytes 262144 | tf_op jit(solution)/shard_map/all_to_all | solution.py:83
  44.9 18.5 %copy-start.4 = (f32[128]{0:T(128)S(1)}, f32[128]{0:T(128)}, u32[]{:S(2)}) copy-start(f32[128]{0:T(128)} %param.17) | copy-start | bytes 1540
  44.9 18.5 %copy-start.5 = (f32[128]{0:T(128)S(1)}, f32[128]{0:T(128)}, u32[]{:S(2)}) copy-start(f32[128]{0:T(128)} %param.16) | copy-start | bytes 1540
  64.2 23.6 %all-to-all-start.3 = ((f32[16,1,3328]{2,1,0:T(1,128)}), f32[16,1,3328]{2,1,0:T(1,128)S(1)}, u32[]{:S(2)}, u32[]{:S(2)}) async-start(f32[16,1,3328]{2,1,0:T(1,128)} %broadcast_in_dim.30), calls=%async_computation.3 | async-start | bytes 425984 | tf_op jit(solution)/shard_map/all_to_all | solution.py:101

commit v19 on v18

--- a/solution.py
+++ b/solution.py
@@ -27,7 +27,7 @@
         send_ref[j, pl.ds(comp_here, events), :] = ev
         return carry
 
-    lax.fori_loop(0, nrow, dest, 0, unroll=2)
+    lax.fori_loop(0, nrow, dest, 0, unroll=4)
 
 
 def build_taps(rows, weights, first, nrow, comp_here, events, rotated):

time: 92 us -> 91.9 us (level)
  no operation moved by 1% of the time
where the time goes in v19:
time: 91.9 us; the launch traced here: 91.4 us
  blocking collectives  36.8 us (40%)
  waiting for transfers between devices  17.2 us (19%)
  starting transfers between devices  16.8 us (18%)
  matrix products  9.24 us (10%)
  local copies, waits for them, and re-layouts  4.96 us (5%)
  Pallas kernels  4.26 us (5%)
  other arithmetic  1.37 us (1%)
    all_to_all x1, blocking collectives, shards(): lax.all_to_all(partial_panel.reshape(nrow, prow, width), 'row', 0, 0).sum(0)  22.7 us
    all_to_all x1, blocking collectives, shards(): got = lax.all_to_all(send, 'row', 0, 0).sum(0)  14.1 us
    all_to_all x1, starting transfers between devices, shards(): lax.all_to_all(flat, 'col', 0, 0, tiled=True).reshape((ncol,) + block.shape)  12.9 us
    all_to_all x1, waiting for transfers between devices, shards(): lax.all_to_all(flat, 'col', 0, 0, tiled=True).reshape((ncol,) + block.shape)  10.7 us
    all_to_all x1, waiting for transfers between devices, shards(): lax.all_to_all(jnp.broadcast_to(mine[None], (nrow,) + mine.shape), 'row',...  6.48 us
    pallas_call x1, Pallas kernels, build_taps(): pl.pallas_call(functools.partial(tap_kernel, taps, nrow, comp_here, event...  4.26 us
    all_to_all x1, starting transfers between devices, shards(): lax.all_to_all(jnp.broadcast_to(mine[None], (nrow,) + mine.shape), 'row',...  3.86 us
    dot_general x1, matrix products, shards(): jnp.dot(reflectors.T, vectors, precision=high, preferred_element_type=jnp...  3.02 us
  transfers between devices with their start and end apart: 2, of which 2 were waited for; matrix products, arithmetic and copies ran while one was open for 3% of the time, Pallas kernels for 0%

profile of v19, /device:TPU:1, one launch (start us, length us, event | category | flops | bytes accessed | tf_op | source)
XLA Modules:
  0.0 91.4 jit_solution(5199061050545392775)
XLA Ops:
  0.6 0.0 copy-start
  0.6 0.0 copy-start.1
  0.7 0.0 copy-start.3
  0.7 0.0 copy-start.2
  0.7 1.6 %copy-done = f32[2048,256]{1,0:T(8,128)S(1)} copy-done((f32[2048,256]{1,0:T(8,128)S(1)}, f32[2048,256]{1,0:T(8,128)}, u32[]{:S(2)}) %copy-start) | copy-done | bytes 2097176
  2.3 3.0 %convolution_bitcast_fusion.1 = f32[32,8,128]{2,1,0:T(8,128)S(1)} fusion(f32[2048,256]{1,0:T(8,128)S(1)} %copy-done, f32[2048,128]{1,0:T(8,128)} %param.9), kind=kOutput, calls=%fused_computation.2 | convolution fusion | flops 402653184 | bytes 3276800 | tf_op jit(solution)/shard_map/dot_general | solution.py:78
  5.3 22.7 %all_to_all.21 = f32[32,8,128]{2,1,0:T(8,128)S(1)} all-to-all(f32[32,8,128]{2,1,0:T(8,128)S(1)} %convolution_bitcast_fusion.1), channel_id=1, replica_groups=mesh['row'=32,'col'=16] {'row'}, dimensions={0} | all-to-all | bytes 262144 | tf_op jit(solution)/shard_map/all_to_all | solution.py:82
  28.0 0.7 broadcast_in_dim.25
  28.7 3.9 %all-to-all-start.1 = ((f32[32,8,128]{2,1,0:T(8,128)}), f32[32,8,128]{2,1,0:T(8,128)S(1)}, u32[]{:S(2)}, u32[]{:S(2)}) async-start(f32[32,8,128]{2,1,0:T(8,128)} %broadcast_in_dim.25), calls=%async_computation.1 | async-start | bytes 262144 | tf_op jit(solution)/shard_map/all_to_all | solution.py:83
  32.6 0.1 copy.20
  32.7 0.8 min.12.idx_ref
  33.5 0.8 maximum_select_fusion
  34.3 0.1 copy.21
  34.4 0.8 select_n.9.w_ref
  35.2 6.5 %all-to-all-done.1 = f32[32,8,128]{2,1,0:T(8,128)S(1)} async-done(((f32[32,8,128]{2,1,0:T(8,128)}), f32[32,8,128]{2,1,0:T(8,128)S(1)}, u32[]{:S(2)}, u32[]{:S(2)}) %all-to-all-start.1) | async-done | bytes 131104 | tf_op jit(solution)/shard_map/all_to_all | solution.py:83
  41.7 1.2 %fusion.13 = f32[128,256]{1,0:T(8,128)S(1)} fusion(f32[256,256]{1,0:T(8,128)} %param.11, f32[32,8,128]{2,1,0:T(8,128)S(1)} %all-to-all-done.1), kind=kOutput, calls=%fused_computation.18 | convolution fusion | flops 50331648 | bytes 524288 | tf_op jit(solution)/shard_map/dot_general | solution.py:85
  42.9 2.0 %fusion.rot_ref = f32[2048,128]{1,0:T(8,128)} fusion(f32[2048,128]{1,0:T(8,128)S(1)} %copy-done.1, f32[128,256]{1,0:T(8,128)S(1)} %fusion.13, f32[2048,256]{1,0:T(8,128)S(1)} %copy-done), kind=kOutput, calls=%fused_computation.1 | convolution fusion | flops 402915328 | bytes 4325376 | tf_op jit(solution)/shard_map/dot_general | solution.py:86
  44.9 4.3 %shard_map.104 = f32[32,24,128]{2,1,0:T(8,128)} custom-call(s32[2080]{0:T(1024)} %min.12.idx_ref, f32[2080]{0:T(1024)} %select_n.9.w_ref, f32[2048,128]{1,0:T(8,128)} %fusion.rot_ref), custom_call_target="tpu_custom_call" | custom-call | tf_op jit(solution)/shard_map/pallas_call | solution.py:42
  49.2 14.1 %all_to_all.22 = f32[32,24,128]{2,1,0:T(8,128)S(1)} all-to-all(f32[32,24,128]{2,1,0:T(8,128)} %shard_map.104), channel_id=1, replica_groups=mesh['row'=32,'col'=16] {'row'}, dimensions={0} | all-to-all | bytes 786432 | tf_op jit(solution)/shard_map/all_to_all | solution.py:98
  63.4 0.8 broadcast_in_dim.30
  64.2 12.9 %all-to-all-start.3 = ((f32[16,1,3328]{2,1,0:T(1,128)}), f32[16,1,3328]{2,1,0:T(1,128)S(1)}, u32[]{:S(2)}, u32[]{:S(2)}) async-start(f32[16,1,3328]{2,1,0:T(1,128)} %broadcast_in_dim.30), calls=%async_computation.3 | async-start | bytes 425984 | tf_op jit(solution)/shard_map/all_to_all | solution.py:101
  77.1 10.7 %all-to-all-done.3 = f32[16,1,3328]{2,1,0:T(1,128)S(1)} async-done(((f32[16,1,3328]{2,1,0:T(1,128)}), f32[16,1,3328]{2,1,0:T(1,128)S(1)}, u32[]{:S(2)}, u32[]{:S(2)}) %all-to-all-start.3) | async-done | bytes 213024 | tf_op jit(solution)/shard_map/all_to_all | solution.py:101
  87.8 0.5 reduce
  88.4 3.0 %convolution_multiply_fusion = f32[8,16,64]{2,1,0:T(8,128)} fusion(f32[16,2048]{1,0:T(8,128)S(1)} %copy_bitcast_fusion, f32[8,2048]{1,0:T(8,128)S(1)} %slice_bitcast_fusion.1, f32[2048]{0:T(1024)S(1)} %bitcast.34, f32[64]{0:T(128)S(1)} %add_convert_fusion, f32[2048]{0:T(1024)S(1)} %bitcast.33), kind=kOutput, calls=%fused_computation.3 | convolution fusion | flops 101326848 | bytes 246016 | tf_op jit(solution)/shard_map/dot_general | solution.py:111
  (16 shorter events, 0.2 us)
Async XLA Ops:
  0.6 1.6 %copy-start = (f32[2048,256]{1,0:T(8,128)S(1)}, f32[2048,256]{1,0:T(8,128)}, u32[]{:S(2)}) copy-start(f32[2048,256]{1,0:T(8,128)} %param.10) | copy-start | bytes 6291460
  0.6 42.3 %copy-start.1 = (f32[2048,128]{1,0:T(8,128)S(1)}, f32[2048,128]{1,0:T(8,128)}, u32[]{:S(2)}) copy-start(f32[2048,128]{1,0:T(8,128)} %param.9) | copy-start | bytes 3145732
  0.7 31.9 %copy-start.3 = (s32[8,4]{0,1:T(4,128)S(1)}, s32[8,4]{0,1:T(4,128)}, u32[]{:S(2)}) copy-start(s32[8,4]{0,1:T(4,128)} %param.14) | copy-start | bytes 388
  0.7 31.9 %copy-start.2 = (s32[512,4]{0,1:T(4,128)S(1)}, s32[512,4]{0,1:T(4,128)}, u32[]{:S(2)}) copy-start(s32[512,4]{0,1:T(4,128)} %param.12) | copy-start | bytes 24580
  28.7 13.0 %all-to-all-start.1 = ((f32[32,8,128]{2,1,0:T(8,128)}), f32[32,8,128]{2,1,0:T(8,128)S(1)}, u32[]{:S(2)}, u32[]{:S(2)}) async-start(f32[32,8,128]{2,1,0:T(8,128)} %broadcast_in_dim.25), calls=%async_computation.1 | async-start | bytes 262144 | tf_op jit(solution)/shard_map/all_to_all | solution.py:83
  44.9 18.4 %copy-start.4 = (f32[128]{0:T(128)S(1)}, f32[128]{0:T(128)}, u32[]{:S(2)}) copy-start(f32[128]{0:T(128)} %param.17) | copy-start | bytes 1540
  44.9 18.4 %copy-start.5 = (f32[128]{0:T(128)S(1)}, f32[128]{0:T(128)}, u32[]{:S(2)}) copy-start(f32[128]{0:T(128)} %param.16) | copy-start | bytes 1540
  64.2 23.6 %all-to-all-start.3 = ((f32[16,1,3328]{2,1,0:T(1,128)}), f32[16,1,3328]{2,1,0:T(1,128)S(1)}, u32[]{:S(2)}, u32[]{:S(2)}) async-start(f32[16,1,3328]{2,1,0:T(1,128)} %broadcast_in_dim.30), calls=%async_computation.3 | async-start | bytes 425984 | tf_op jit(solution)/shard_map/all_to_all | solution.py:101
